TPU v7x, 32 devices: a whole 2x2x4 slice. The times are simulated.
32 devices in a mesh: dp: 2 (over x), seq: 16 (over z, y, core).
Axes of the slice: x: 2, y: 2, z: 4, core: 2. Of those that a mesh axis runs over, the one named last changes fastest.
Arguments:
- x_input: bfloat16 [2, 8192, 768], P('dp', 'seq'), may hold values from -6 to 6
- gain_one: bfloat16 [768], replicated, may hold values from 0.3984375 to 1.59375
- shift_one: bfloat16 [768], replicated, may hold values from -1.5 to 1.5
- w_query: bfloat16 [768, 768], replicated, may hold values from -0.21875 to 0.21875
- b_query: bfloat16 [768], replicated, may hold values from -1.5 to 1.5
- w_key: bfloat16 [768, 768], replicated, may hold values from -0.21875 to 0.21875
- w_value: bfloat16 [768, 768], replicated, may hold values from -0.21875 to 0.21875
- b_value: bfloat16 [768], replicated, may hold values from -1.5 to 1.5
- w_attn_out: bfloat16 [768, 768], replicated, may hold values from -1.25 to 1.25
- b_attn_out: bfloat16 [768], replicated, may hold values from -1.5 to 1.5
- pool_key: bfloat16 [5, 768], replicated, may hold values from -2.5 to 2.5
- pool_value: bfloat16 [5, 768], replicated, may hold values from -2.5 to 2.5
- gain_two: bfloat16 [768], replicated, may hold values from 0.3984375 to 1.59375
- shift_two: bfloat16 [768], replicated, may hold values from -1.5 to 1.5
- w_in: bfloat16 [768, 3072], replicated, may hold values from -0.21875 to 0.21875
- b_in: bfloat16 [3072], replicated, may hold values from -1.5 to 1.5
- w_out: bfloat16 [3072, 768], replicated, may hold values from -0.109375 to 0.109375
- b_out: bfloat16 [768], replicated, may hold values from -1.5 to 1.5
- mask_slots: int32 [2, 16, 128], P('dp', 'seq'), may hold values from -1 to 511, as said below
- cot_rows: bfloat16 [2, 16, 128, 768], P('dp', 'seq'), may hold values from -6 to 6
Outputs:
- output: bfloat16 [2, 8192, 768], P('dp', 'seq')
- grad_input: float32 [2, 8192, 768], P('dp', 'seq')
- grad_gain_one: float32 [768], P('seq')
- grad_shift_one: float32 [768], P('seq')
- grad_w_query: float32 [768, 768], P('seq')
- grad_b_query: float32 [768], P('seq')
- grad_w_key: float32 [768, 768], P('seq')
- grad_w_value: float32 [768, 768], P('seq')
- grad_b_value: float32 [768], P('seq')
- grad_w_attn_out: float32 [768, 768], P('seq')
- grad_b_attn_out: float32 [768], P('seq')
- grad_pool_key: float32 [5, 768], P(None, 'seq')
- grad_pool_value: float32 [5, 768], P(None, 'seq')
- grad_gain_two: float32 [768], P('seq')
- grad_shift_two: float32 [768], P('seq')
- grad_w_in: float32 [768, 3072], P('seq')
- grad_b_in: float32 [3072], P('seq')
- grad_w_out: float32 [3072, 768], P('seq')
- grad_b_out: float32 [768], P('seq')
Inputs may be any that keep to these rules, and one draw needn't show every extreme that they name: `mask_slots`: for each sequence and each device's block of 512 tokens, the used slots come first and hold distinct positions within the block; the rest are -1. In every sequence one block uses all 128 slots and another block fewer than a third of them.
All inputs are finite; a program needn't handle non-finite values.
Results may differ from a plain program's by a relative error of at most 0.02.
Values may be sent and summed in bfloat16 or wider, within the bound.
A program may use at most 192 MiB of HBM per device.

v0:
```python
import jax
import jax.numpy as jnp
from jax import lax
from jax.sharding import PartitionSpec as P

D = 768
HEADS = 12
HD = 64
KERNEL = 5
STRIDE = 4
WIN = 128
POOL_SPAN = 512


EPSILON = 1e-05
MASKED_OUT = -1000000000.0


def with_halo(shard, sides, width):
    for axis, dim in sides:
        size, length = (lax.axis_size(axis), shard.shape[dim])
        up = [(i, (i + 1) % size) for i in range(size - 1)]
        down = [(j, i) for i, j in up]
        last = lax.slice_in_dim(shard, length - width, length, axis=dim)
        initial = lax.slice_in_dim(shard, 0, width, axis=dim)
        before = lax.ppermute(last, axis, up)
        after = lax.ppermute(initial, axis, down)
        shard = jnp.concatenate([before, shard, after], axis=dim)
    return shard


def from_behind(shard, axis, by):
    length = lax.axis_size(axis)
    pairs = [(i, i + by) for i in range(length) if 0 <= i + by < length]
    return lax.ppermute(shard, axis, pairs)


def norm_apply(values, gain_vec, shift_vec):
    centre = jnp.mean(values, axis=-1, keepdims=True)
    shifted = values - centre
    inv_std = lax.rsqrt(jnp.mean(shifted * shifted, axis=-1, keepdims=True) + EPSILON)
    return shifted * inv_std * gain_vec + shift_vec


def gelu_exact(values):
    return jax.nn.gelu(values, approximate=False)


def product(left_side, right_side):
    return jnp.dot(left_side, right_side, preferred_element_type=jnp.float32)


def product_t(left_side, right_side):
    return lax.dot_general(
        left_side, right_side, (((1,), (1,)), ((), ())), preferred_element_type=jnp.float32
    )


def inner_rows(left_side, right_side):
    return lax.dot_general(
        left_side, right_side, (((0,), (0,)), ((), ())), preferred_element_type=jnp.float32
    )


def split_heads(matrix):
    return matrix.reshape(matrix.shape[0], HEADS, HD)


def masked_scores(queries_b, key_rows, allowed):
    scores = jnp.einsum(
        "qhd,khd->hqk",
        split_heads(queries_b),
        split_heads(key_rows),
        preferred_element_type=jnp.float32,
    ) * HD ** (-0.5)
    return jnp.where(allowed[None], scores, MASKED_OUT)


def level_forward(queries_b, key_rows, value_rows, allowed):
    scores = masked_scores(queries_b, key_rows, allowed)
    largest = jnp.max(scores, axis=-1, keepdims=True)
    exp_scores = jnp.exp(scores - largest)
    summed = jnp.sum(exp_scores, axis=-1, keepdims=True)
    weights = exp_scores / summed
    log_total = largest + jnp.log(summed)
    mixture = jnp.einsum(
        "hqk,khd->qhd",
        weights.astype(jnp.bfloat16),
        split_heads(value_rows),
        preferred_element_type=jnp.float32,
    )
    return (mixture.reshape(queries_b.shape[0], D), log_total)


def level_backward(queries_b, key_rows, value_rows, allowed, log_total, grad_mixed_b):
    scale = HD ** (-0.5)
    scores = masked_scores(queries_b, key_rows, allowed)
    weights = jnp.exp(scores - log_total)
    grad_heads = split_heads(grad_mixed_b)
    grad_values = jnp.einsum(
        "hqk,qhd->khd", weights.astype(jnp.bfloat16), grad_heads, preferred_element_type=jnp.float32
    )
    grad_weights = jnp.einsum(
        "qhd,khd->hqk", grad_heads, split_heads(value_rows), preferred_element_type=jnp.float32
    )
    grad_scores = weights * (grad_weights - jnp.sum(weights * grad_weights, axis=-1, keepdims=True))
    grad_scores_b = grad_scores.astype(jnp.bfloat16)
    grad_queries = (
        jnp.einsum(
            "hqk,khd->qhd", grad_scores_b, split_heads(key_rows), preferred_element_type=jnp.float32
        )
        * scale
    )
    grad_keys = (
        jnp.einsum(
            "hqk,qhd->khd",
            grad_scores_b,
            split_heads(queries_b),
            preferred_element_type=jnp.float32,
        )
        * scale
    )
    key_count = key_rows.shape[0]
    return (
        grad_queries.reshape(queries_b.shape[0], D),
        grad_keys.reshape(key_count, D),
        grad_values.reshape(key_count, D),
    )


def ffn_backward(
    hidden_rows, normed_rows_b, pre_rows, act_rows_b, cot_b, gain_two_f, shift_two_f, w_in, w_out
):
    unused_act, gelu_pull = jax.vjp(gelu_exact, pre_rows)
    grad_act = product_t(cot_b, w_out)
    grad_pre_b = gelu_pull(grad_act)[0].astype(jnp.bfloat16)
    grad_w_out = inner_rows(act_rows_b, cot_b)
    grad_b_out = jnp.sum(cot_b.astype(jnp.float32), axis=0)
    grad_w_in = inner_rows(normed_rows_b, grad_pre_b)
    grad_b_in = jnp.sum(grad_pre_b.astype(jnp.float32), axis=0)
    grad_normed_two = product_t(grad_pre_b, w_in)
    unused_norm, norm_pull = jax.vjp(norm_apply, hidden_rows, gain_two_f, shift_two_f)
    grad_h_ffn, grad_gain_two, grad_shift_two = norm_pull(grad_normed_two)
    return (
        grad_h_ffn,
        (grad_gain_two, grad_shift_two, grad_w_in, grad_b_in, grad_w_out, grad_b_out),
    )


def on_device(
    x_input,
    gain_one,
    shift_one,
    w_query,
    b_query,
    w_key,
    w_value,
    b_value,
    w_attn_out,
    b_attn_out,
    pool_key,
    pool_value,
    gain_two,
    shift_two,
    w_in,
    b_in,
    w_out,
    b_out,
    mask_slots,
    cot_rows,
):
    tok_rows = x_input.shape[1]
    seq_count = lax.axis_size("seq")
    seq_index = lax.axis_index("seq")
    seq_len = tok_rows * seq_count
    half_win = WIN // 2
    half_pool = POOL_SPAN // 2
    pooled_rows = tok_rows // STRIDE
    reach = half_pool // STRIDE
    half_taps = KERNEL // 2
    gain_one_f = gain_one.astype(jnp.float32)
    shift_one_f = shift_one.astype(jnp.float32)
    gain_two_f = gain_two.astype(jnp.float32)
    shift_two_f = shift_two.astype(jnp.float32)
    residual_in = x_input[0].astype(jnp.float32)
    normed_b = norm_apply(residual_in, gain_one_f, shift_one_f).astype(jnp.bfloat16)
    queries_b = (product(normed_b, w_query) + b_query.astype(jnp.float32)).astype(jnp.bfloat16)
    keys_b = product(normed_b, w_key).astype(jnp.bfloat16)
    values_b = (product(normed_b, w_value) + b_value.astype(jnp.float32)).astype(jnp.bfloat16)
    paired = jnp.stack([keys_b, values_b])
    paired_ext = with_halo(paired, (("seq", 1),), half_win)
    ext_f = paired_ext.astype(jnp.float32)
    taps = jnp.stack([pool_key, pool_value]).astype(jnp.float32)
    pooled = jnp.zeros((2, pooled_rows, D), jnp.float32)
    for tap_id in range(KERNEL):
        begin = half_win - half_taps + tap_id
        pooled = (
            pooled
            + ext_f[:, begin : begin + STRIDE * pooled_rows : STRIDE] * taps[:, tap_id][:, None, :]
        )
    pooled_b = pooled.astype(jnp.bfloat16)
    pooled_ext = with_halo(pooled_b, (("seq", 1),), reach)
    query_pos = seq_index * tok_rows + jnp.arange(tok_rows, dtype=jnp.int32)
    near_pos = (
        seq_index * tok_rows - half_win + jnp.arange(tok_rows + 2 * half_win, dtype=jnp.int32)
    )
    far_pos = seq_index * pooled_rows - reach + jnp.arange(pooled_rows + 2 * reach, dtype=jnp.int32)
    near_ok = (near_pos[None, :] >= query_pos[:, None] - half_win) & (
        near_pos[None, :] < query_pos[:, None] + half_win
    )
    near_ok = near_ok & (near_pos[None, :] >= 0) & (near_pos[None, :] < seq_len)
    far_ok = (STRIDE * far_pos[None, :] >= query_pos[:, None] - half_pool) & (
        STRIDE * far_pos[None, :] < query_pos[:, None] + half_pool
    )
    far_ok = far_ok & (far_pos[None, :] >= 0) & (far_pos[None, :] < seq_len // STRIDE)
    near_mix, near_lse = level_forward(queries_b, paired_ext[0], paired_ext[1], near_ok)
    far_mix, far_lse = level_forward(queries_b, pooled_ext[0], pooled_ext[1], far_ok)
    attn_b = (near_mix + far_mix).astype(jnp.bfloat16)
    hidden_res = residual_in + product(attn_b, w_attn_out) + b_attn_out.astype(jnp.float32)
    normed_two_b = norm_apply(hidden_res, gain_two_f, shift_two_f).astype(jnp.bfloat16)
    pre_act = product(normed_two_b, w_in) + b_in.astype(jnp.float32)
    act_b = gelu_exact(pre_act).astype(jnp.bfloat16)
    output = hidden_res + product(act_b, w_out) + b_out.astype(jnp.float32)
    slot_ids = mask_slots[0, 0]
    slot_rows = cot_rows[0, 0]
    live = slot_ids >= 0
    target = jnp.where(live, slot_ids, tok_rows)
    cot_dense = jnp.zeros((tok_rows + 1, D), jnp.bfloat16).at[target].set(slot_rows)[:tok_rows]
    grad_h_ffn, ffn_grads = ffn_backward(
        hidden_res, normed_two_b, pre_act, act_b, cot_dense, gain_two_f, shift_two_f, w_in, w_out
    )
    grad_gain_two, grad_shift_two, grad_w_in, grad_b_in, grad_w_out, grad_b_out = ffn_grads
    grad_hidden = cot_dense.astype(jnp.float32) + grad_h_ffn
    grad_branch_b = grad_hidden.astype(jnp.bfloat16)
    grad_w_attn_out = inner_rows(attn_b, grad_branch_b)
    grad_b_attn_out = jnp.sum(grad_branch_b.astype(jnp.float32), axis=0)
    grad_attn_b = product_t(grad_branch_b, w_attn_out).astype(jnp.bfloat16)
    grad_q_near, grad_k_near, grad_v_near = level_backward(
        queries_b, paired_ext[0], paired_ext[1], near_ok, near_lse, grad_attn_b
    )
    grad_q_far, grad_k_far, grad_v_far = level_backward(
        queries_b, pooled_ext[0], pooled_ext[1], far_ok, far_lse, grad_attn_b
    )
    pooled_grad_ext = jnp.stack([grad_k_far, grad_v_far])
    from_above = from_behind(pooled_grad_ext[:, :reach].astype(jnp.bfloat16), "seq", -1).astype(
        jnp.float32
    )
    from_below = from_behind(
        pooled_grad_ext[:, pooled_rows + reach :].astype(jnp.bfloat16), "seq", 1
    ).astype(jnp.float32)
    pooled_grad = pooled_grad_ext[:, reach : reach + pooled_rows]
    pooled_grad = pooled_grad.at[:, :reach].add(from_below)
    pooled_grad = pooled_grad.at[:, pooled_rows - reach :].add(from_above)
    pooled_grad_f = pooled_grad.astype(jnp.bfloat16).astype(jnp.float32)
    grad_ext = jnp.stack([grad_k_near, grad_v_near])
    tap_grads = []
    for tap_id in range(KERNEL):
        begin = half_win - half_taps + tap_id
        grad_ext = grad_ext.at[:, begin : begin + STRIDE * pooled_rows : STRIDE].add(
            pooled_grad_f * taps[:, tap_id][:, None, :]
        )
        tap_grads.append(
            jnp.sum(ext_f[:, begin : begin + STRIDE * pooled_rows : STRIDE] * pooled_grad_f, axis=1)
        )
    grad_taps = jnp.stack(tap_grads, axis=1)
    rim_above = from_behind(grad_ext[:, :half_win].astype(jnp.bfloat16), "seq", -1).astype(
        jnp.float32
    )
    rim_below = from_behind(
        grad_ext[:, half_win + tok_rows :].astype(jnp.bfloat16), "seq", 1
    ).astype(jnp.float32)
    grad_kv = grad_ext[:, half_win : half_win + tok_rows]
    grad_kv = grad_kv.at[:, :half_win].add(rim_below)
    grad_kv = grad_kv.at[:, tok_rows - half_win :].add(rim_above)
    grad_kv_b = grad_kv.astype(jnp.bfloat16)
    grad_q_b = (grad_q_near + grad_q_far).astype(jnp.bfloat16)
    grad_w_query = inner_rows(normed_b, grad_q_b)
    grad_b_query = jnp.sum(grad_q_b.astype(jnp.float32), axis=0)
    grad_w_key = inner_rows(normed_b, grad_kv_b[0])
    grad_w_value = inner_rows(normed_b, grad_kv_b[1])
    grad_b_value = jnp.sum(grad_kv_b[1].astype(jnp.float32), axis=0)
    grad_normed = (
        product_t(grad_q_b, w_query)
        + product_t(grad_kv_b[0], w_key)
        + product_t(grad_kv_b[1], w_value)
    )
    unused_norm, norm_pull = jax.vjp(norm_apply, residual_in, gain_one_f, shift_one_f)
    grad_in_norm, grad_gain_one, grad_shift_one = norm_pull(grad_normed)
    grad_input = grad_hidden + grad_in_norm
    reduced = (
        lax.psum_scatter(
            grad_gain_one.astype(jnp.bfloat16), "seq", scatter_dimension=0, tiled=True
        ).astype(jnp.float32),
        lax.psum_scatter(
            grad_shift_one.astype(jnp.bfloat16), "seq", scatter_dimension=0, tiled=True
        ).astype(jnp.float32),
        lax.psum_scatter(
            grad_w_query.astype(jnp.bfloat16), "seq", scatter_dimension=0, tiled=True
        ).astype(jnp.float32),
        lax.psum_scatter(
            grad_b_query.astype(jnp.bfloat16), "seq", scatter_dimension=0, tiled=True
        ).astype(jnp.float32),
        lax.psum_scatter(
            grad_w_key.astype(jnp.bfloat16), "seq", scatter_dimension=0, tiled=True
        ).astype(jnp.float32),
        lax.psum_scatter(
            grad_w_value.astype(jnp.bfloat16), "seq", scatter_dimension=0, tiled=True
        ).astype(jnp.float32),
        lax.psum_scatter(
            grad_b_value.astype(jnp.bfloat16), "seq", scatter_dimension=0, tiled=True
        ).astype(jnp.float32),
        lax.psum_scatter(
            grad_w_attn_out.astype(jnp.bfloat16), "seq", scatter_dimension=0, tiled=True
        ).astype(jnp.float32),
        lax.psum_scatter(
            grad_b_attn_out.astype(jnp.bfloat16), "seq", scatter_dimension=0, tiled=True
        ).astype(jnp.float32),
        lax.psum_scatter(
            grad_taps[0].astype(jnp.bfloat16), "seq", scatter_dimension=1, tiled=True
        ).astype(jnp.float32),
        lax.psum_scatter(
            grad_taps[1].astype(jnp.bfloat16), "seq", scatter_dimension=1, tiled=True
        ).astype(jnp.float32),
        lax.psum_scatter(
            grad_gain_two.astype(jnp.bfloat16), "seq", scatter_dimension=0, tiled=True
        ).astype(jnp.float32),
        lax.psum_scatter(
            grad_shift_two.astype(jnp.bfloat16), "seq", scatter_dimension=0, tiled=True
        ).astype(jnp.float32),
        lax.psum_scatter(
            grad_w_in.astype(jnp.bfloat16), "seq", scatter_dimension=0, tiled=True
        ).astype(jnp.float32),
        lax.psum_scatter(
            grad_b_in.astype(jnp.bfloat16), "seq", scatter_dimension=0, tiled=True
        ).astype(jnp.float32),
        lax.psum_scatter(
            grad_w_out.astype(jnp.bfloat16), "seq", scatter_dimension=0, tiled=True
        ).astype(jnp.float32),
        lax.psum_scatter(
            grad_b_out.astype(jnp.bfloat16), "seq", scatter_dimension=0, tiled=True
        ).astype(jnp.float32),
    )
    reduced = (
        lax.psum(reduced[0].astype(jnp.bfloat16), "dp").astype(jnp.float32),
        lax.psum(reduced[1].astype(jnp.bfloat16), "dp").astype(jnp.float32),
        lax.psum(reduced[2].astype(jnp.bfloat16), "dp").astype(jnp.float32),
        lax.psum(reduced[3].astype(jnp.bfloat16), "dp").astype(jnp.float32),
        lax.psum(reduced[4].astype(jnp.bfloat16), "dp").astype(jnp.float32),
        lax.psum(reduced[5].astype(jnp.bfloat16), "dp").astype(jnp.float32),
        lax.psum(reduced[6].astype(jnp.bfloat16), "dp").astype(jnp.float32),
        lax.psum(reduced[7].astype(jnp.bfloat16), "dp").astype(jnp.float32),
        lax.psum(reduced[8].astype(jnp.bfloat16), "dp").astype(jnp.float32),
        lax.psum(reduced[9].astype(jnp.bfloat16), "dp").astype(jnp.float32),
        lax.psum(reduced[10].astype(jnp.bfloat16), "dp").astype(jnp.float32),
        lax.psum(reduced[11].astype(jnp.bfloat16), "dp").astype(jnp.float32),
        lax.psum(reduced[12].astype(jnp.bfloat16), "dp").astype(jnp.float32),
        lax.psum(reduced[13].astype(jnp.bfloat16), "dp").astype(jnp.float32),
        lax.psum(reduced[14].astype(jnp.bfloat16), "dp").astype(jnp.float32),
        lax.psum(reduced[15].astype(jnp.bfloat16), "dp").astype(jnp.float32),
        lax.psum(reduced[16].astype(jnp.bfloat16), "dp").astype(jnp.float32),
    )
    return (output.astype(jnp.bfloat16)[None], grad_input[None]) + tuple(reduced)


def solution(mesh):
    return jax.shard_map(
        on_device,
        mesh=mesh,
        in_specs=(
            P("dp", "seq", None),
            P(),
            P(),
            P(),
            P(),
            P(),
            P(),
            P(),
            P(),
            P(),
            P(),
            P(),
            P(),
            P(),
            P(),
            P(),
            P(),
            P(),
            P("dp", "seq", None),
            P("dp", "seq", None, None),
        ),
        out_specs=(
            P("dp", "seq", None),
            P("dp", "seq", None),
            P("seq"),
            P("seq"),
            P("seq", None),
            P("seq"),
            P("seq", None),
            P("seq", None),
            P("seq"),
            P("seq", None),
            P("seq"),
            P(None, "seq"),
            P(None, "seq"),
            P("seq"),
            P("seq"),
            P("seq", None),
            P("seq"),
            P("seq", None),
            P("seq"),
        ),
        check_vma=False,
    )
```

profile of v0, /device:TPU:0, one launch (start us, length us, event | category | flops | bytes accessed | tf_op | source)
XLA Modules:
  0.0 838.3 jit_solution(2833418597596058446)
XLA Ops:
  31.5 3.1 add_convert_fusion.4
  44.6 4.2 pad_maximum_fusion.2
  48.8 4.5 slice.220
  53.4 6.0 slice.218
  59.4 5.7 slice.216
  65.1 5.7 slice.214
  70.8 5.8 slice.212
  84.6 4.5 collective-permute-start.2
  93.2 4.6 fusion.109
  97.9 3.6 fusion
  117.7 5.4 add_convert_fusion.3
  124.6 20.8 %multiply_convert_fusion.2 = (bf16[512,3072]{1,0:T(8,128)(2,1)}, f32[512,3072]{1,0:T(8,128)}, f32[512,3072]{1,0:T(8,128)}) fusion(f32[3072]{0:T(1024)S(1)} %copy-done.70, bf16[768,3072]{1,0:T(8,128)(2,1)} %param.42, f32[512,768]{1,0:T(8,128)S(1)} %get-tuple-element.147, f32[768]{0:T(1024)S(1)} %copy-done.75, f32[768]{0:T(1024)S(1)} %copy-done.67, ...), kind=kOutput, calls=%fused_computation.23 | convolution fusion | flops 2521694208 | bytes 22042624 | tf_op jit(solution)/shard_map/dot_general | solution.py:50
  145.4 8.2 fusion.111
  153.6 3.5 multiply_reduce_fusion.2
  164.0 5.2 fusion.14
  169.2 4.5 multiply_reduce_fusion.1
  175.2 6.5 multiply_convert_fusion.1
  190.4 5.0 collective-permute-start.4
  195.5 14.7 %multiply_reduce_fusion = (f32[12,512]{1,0:T(8,128)}, f32[12,512,640]{2,1,0:T(8,128)}) fusion(f32[12,512,640]{2,1,0:T(8,128)} %copy-done.1, f32[12,512]{1,0:T(8,128)S(1)} %copy-done.41, bf16[512,12,64]{0,2,1:T(8,128)(2,1)S(1)} %bitcast.191, bf16[640,12,64]{0,2,1:T(8,128)(2,1)S(1)} %bitcast.198), kind=kOutput, calls=%fused_computation.7 | convolution fusion | flops 515106816 | bytes 33275904 | tf_op jit(solution)/shard_map/qhd,khd->hqk/dot_general | solution.py:103
  214.4 8.6 %fusion.2 = f32[12,64,640]{2,1,0:T(8,128)} fusion(bf16[512,12,64]{0,2,1:T(8,128)(2,1)S(1)} %bitcast.192, f32[12,512,640]{2,1,0:T(8,128)} %copy-done.1, f32[12,512]{1,0:T(8,128)} %log_add_fusion.1), kind=kOutput, calls=%fused_computation.15 | convolution fusion | flops 511180800 | bytes 18505728 | tf_op jit(solution)/shard_map/hqk,qhd->khd/dot_general | solution.py:100
  227.0 11.3 %multiply_convert_fusion = bf16[12,512,640]{2,1,0:T(8,128)(2,1)S(1)} fusion(f32[12,512,640]{2,1,0:T(8,128)} %get-tuple-element.153, f32[12,512,640]{2,1,0:T(8,128)} %copy-done.1, f32[12,512]{1,0:T(8,128)S(1)} %copy-done.47, f32[12,512]{1,0:T(8,128)S(1)} %copy-done.42), kind=kLoop, calls=%fused_computation.6 | loop fusion | flops 15728640 | bytes 39370752 | tf_op jit(solution)/shard_map/convert_element_type | solution.py:107
  238.4 3.3 convolution_multiply_fusion
  242.1 5.5 copy.96
  247.5 3.1 copy.95
  253.4 6.5 bitcast_reduce_fusion
  262.9 7.6 pad_maximum_fusion
  277.0 18.4 %scatter_fusion = f32[2,640,768]{2,0,1:T(2,128)} fusion(f32[2,640,768]{2,0,1:T(2,128)} %pad_maximum_fusion, s32[128]{0:T(128)} %add_bitcast_fusion.5, f32[128,2,768]{2,1,0:T(2,128)} %copy.101), kind=kCustom, calls=%fused_computation.1 | custom fusion | flops 196608 | bytes 2359808 | tf_op jit(solution)/shard_map/scatter-add | solution.py:259
  295.3 18.3 %scatter_fusion.1 = f32[2,640,768]{2,0,1:T(2,128)} fusion(f32[2,640,768]{2,0,1:T(2,128)} %scatter_fusion, s32[128]{0:T(128)} %add_bitcast_fusion.4, f32[128,2,768]{2,1,0:T(2,128)} %copy.102), kind=kCustom, calls=%fused_computation.2 | custom fusion | flops 196608 | bytes 2359808 | tf_op jit(solution)/shard_map/scatter-add | solution.py:259
  313.6 18.3 %scatter_fusion.2 = f32[2,640,768]{2,0,1:T(2,128)} fusion(f32[2,640,768]{2,0,1:T(2,128)} %scatter_fusion.1, s32[128]{0:T(128)} %add_bitcast_fusion.3, f32[128,2,768]{2,1,0:T(2,128)} %copy.103), kind=kCustom, calls=%fused_computation.3 | custom fusion | flops 196608 | bytes 2359808 | tf_op jit(solution)/shard_map/scatter-add | solution.py:259
  332.0 16.7 %scatter_fusion.3 = f32[2,640,768]{2,0,1:T(2,128)} fusion(f32[2,640,768]{2,0,1:T(2,128)} %scatter_fusion.2, s32[128]{0:T(128)} %add_bitcast_fusion.2, f32[128,2,768]{2,1,0:T(2,128)S(1)} %copy.104), kind=kCustom, calls=%fused_computation.4 | custom fusion | flops 196608 | bytes 2359808 | tf_op jit(solution)/shard_map/scatter-add | solution.py:259
  348.7 16.7 %scatter_fusion.4 = f32[2,640,768]{2,0,1:T(2,128)} fusion(f32[2,640,768]{2,0,1:T(2,128)} %scatter_fusion.3, s32[128]{0:T(128)} %add_bitcast_fusion.1, f32[128,2,768]{2,1,0:T(2,128)S(1)} %copy.105), kind=kCustom, calls=%fused_computation.5 | custom fusion | flops 196608 | bytes 2359808 | tf_op jit(solution)/shard_map/scatter-add | solution.py:259
  365.4 3.7 convert.18
  369.3 3.5 collective-permute-start.6
  379.0 4.5 slice_reduce_fusion.1
  386.7 3.5 convolution_convert_fusion.4
  390.3 6.7 convolution_convert_fusion
  398.4 6.6 convolution_convert_fusion.1
  409.8 3.6 fusion.113
  413.5 5.8 fusion.38
  424.6 3.6 fusion.98
  428.3 21.2 %reduce-scatter.13.cloned.1.call-done = bf16[48,768]{1,0:T(8,128)(2,1)} async-done(((bf16[768,768]{1,0:T(8,128)(2,1)}), bf16[48,768]{1,0:T(8,128)(2,1)}) %reduce-scatter.13.cloned.1.call-update) | async-done | bytes 73744 | tf_op jit(solution)/shard_map/reduce_scatter | solution.py:297
  449.6 60.6 %reduce-scatter.17.cloned.1.call-done = bf16[48,768]{1,0:T(8,128)(2,1)} async-done(((bf16[768,768]{1,0:T(8,128)(2,1)}), bf16[48,768]{1,0:T(8,128)(2,1)}) %reduce-scatter.17.cloned.1.call-update) | async-done | bytes 73744 | tf_op jit(solution)/shard_map/reduce_scatter | solution.py:306
  510.2 60.6 %reduce-scatter.15.cloned.1.call-done = bf16[48,768]{1,0:T(8,128)(2,1)} async-done(((bf16[768,768]{1,0:T(8,128)(2,1)}), bf16[48,768]{1,0:T(8,128)(2,1)}) %reduce-scatter.15.cloned.1.call-update) | async-done | bytes 73744 | tf_op jit(solution)/shard_map/reduce_scatter | solution.py:303
  570.8 78.4 %reduce-scatter.23.cloned.1.call-done = bf16[192,768]{1,0:T(8,128)(2,1)} async-done(((bf16[3072,768]{1,0:T(8,128)(2,1)}), bf16[192,768]{1,0:T(8,128)(2,1)}) %reduce-scatter.23.cloned.1.call-update) | async-done | bytes 294928 | tf_op jit(solution)/shard_map/reduce_scatter | solution.py:336
  649.3 78.6 %reduce-scatter.21.cloned.1.call-done = bf16[48,3072]{1,0:T(8,128)(2,1)} async-done(((bf16[768,3072]{1,0:T(8,128)(2,1)}), bf16[48,3072]{1,0:T(8,128)(2,1)}) %reduce-scatter.21.cloned.1.call-update) | async-done | bytes 294928 | tf_op jit(solution)/shard_map/reduce_scatter | solution.py:330
  729.3 58.1 %all-reduce.9 = (bf16[768]{0:T(1024)(128)(2,1)}, bf16[768]{0:T(1024)(128)(2,1)}, bf16[768]{0:T(1024)(128)(2,1)}, bf16[768]{0:T(1024)(128)(2,1)}, bf16[768]{0:T(1...) all-reduce(bf16[768]{0:T(1024)(128)(2,1)} %get-tuple-element.69, ...), channel_id=2, replica_groups=mesh['dp'=2,'seq'=16] {'seq'}, use_global_device_ids=true, to_apply=%region_21.22.clone | all-reduce | flops 9216 | bytes 36864
  798.7 5.7 all-reduce.10
  818.2 3.4 add_bitcast_fusion
  (360 shorter events, 157.2 us)
Async XLA Ops:
  7.2 412.1 %reduce-scatter.27.cloned.1.call-start = ((), (), s32[]{:S(2)}) async-start(), calls=%async_computation.15 | async-start | bytes 208896
  8.7 22.7 %copy-start.57 = (f32[512]{0:T(512)}, f32[512]{0:T(512)S(1)}, u32[]{:S(2)}) copy-start(f32[512]{0:T(512)S(1)} %broadcast_multiply_fusion.1) | copy-start | bytes 6148
  10.3 21.2 %copy-start.59 = (f32[512]{0:T(512)}, f32[512]{0:T(512)S(1)}, u32[]{:S(2)}) copy-start(f32[512]{0:T(512)S(1)} %fusion.83) | copy-start | bytes 6148
  11.0 20.5 %copy-start.48 = (f32[768]{0:T(1024)}, f32[768]{0:T(1024)S(1)}, u32[]{:S(2)}) copy-start(f32[768]{0:T(1024)S(1)} %convert_element_type.284) | copy-start | bytes 9220
  11.6 19.8 %copy-start.73 = (f32[768]{0:T(1024)}, f32[768]{0:T(1024)S(1)}, u32[]{:S(2)}) copy-start(f32[768]{0:T(1024)S(1)} %convert_element_type.285) | copy-start | bytes 9220
  14.8 13.0 %copy-start.83 = (s32[1,1,128]{2,1,0:T(1,128)S(1)}, s32[1,1,128]{2,1,0:T(1,128)}, u32[]{:S(2)}) copy-start(s32[1,1,128]{2,1,0:T(1,128)} %param.46) | copy-start | bytes 1540
  14.8 13.5 %copy-start.78 = (bf16[768]{0:T(1024)(128)(2,1)S(1)}, bf16[768]{0:T(1024)(128)(2,1)}, u32[]{:S(2)}) copy-start(bf16[768]{0:T(1024)(128)(2,1)} %param.40) | copy-start | bytes 4612
  14.8 14.1 %copy-start.79 = (bf16[768]{0:T(1024)(128)(2,1)S(1)}, bf16[768]{0:T(1024)(128)(2,1)}, u32[]{:S(2)}) copy-start(bf16[768]{0:T(1024)(128)(2,1)} %param.41) | copy-start | bytes 4612
  14.8 14.7 %copy-start.80 = (bf16[768]{0:T(1024)(128)(2,1)S(1)}, bf16[768]{0:T(1024)(128)(2,1)}, u32[]{:S(2)}) copy-start(bf16[768]{0:T(1024)(128)(2,1)} %param.32) | copy-start | bytes 4612
  14.8 14.7 %copy-start.81 = (bf16[768]{0:T(1024)(128)(2,1)S(1)}, bf16[768]{0:T(1024)(128)(2,1)}, u32[]{:S(2)}) copy-start(bf16[768]{0:T(1024)(128)(2,1)} %param.37) | copy-start | bytes 4612
  14.9 15.3 %copy-start.72 = (bf16[3072]{0:T(1024)(128)(2,1)S(1)}, bf16[3072]{0:T(1024)(128)(2,1)}, u32[]{:S(2)}) copy-start(bf16[3072]{0:T(1024)(128)(2,1)} %param.43) | copy-start | bytes 18436
  14.9 15.9 %copy-start.68 = (bf16[5,768]{1,0:T(8,128)(2,1)S(1)}, bf16[5,768]{1,0:T(8,128)(2,1)}, u32[]{:S(2)}) copy-start(bf16[5,768]{1,0:T(8,128)(2,1)} %param.39) | copy-start | bytes 23044
  14.9 15.9 %copy-start.69 = (bf16[5,768]{1,0:T(8,128)(2,1)S(1)}, bf16[5,768]{1,0:T(8,128)(2,1)}, u32[]{:S(2)}) copy-start(bf16[5,768]{1,0:T(8,128)(2,1)} %param.38) | copy-start | bytes 23044
  17.5 27.1 %collective-permute-start = (bf16[2,64,768]{2,1,0:T(8,128)(2,1)}, bf16[2,64,768]{2,1,0:T(8,128)(2,1)}, u32[]{:S(2)}, u32[]{:S(2)}) collective-permute-start(bf16[2,64,768]{2,1,0:T(8,128)(2,1)} %get-tuple-element.121), channel_id=1, source_target_pairs={{0,1},{1,2},{2,3},{3,4},{4,5},{5,6},{6,7},{7,8},{8,9},{9,10},{10,1... | collective-permute-start | bytes 589832 | tf_op jit(solution)/shard_map/ppermute | solution.py:26
  20.5 24.0 %collective-permute-start.1 = (bf16[2,64,768]{2,1,0:T(8,128)(2,1)}, bf16[2,64,768]{2,1,0:T(8,128)(2,1)}, u32[]{:S(2)}, u32[]{:S(2)}) collective-permute-start(bf16[2,64,768]{2,1,0:T(8,128)(2,1)} %get-tuple-element.122), channel_id=1, source_target_pairs={{1,0},{2,1},{3,2},{4,3},{5,4},{6,5},{7,6},{8,7},{9,8},{10,9},{11,1... | collective-permute-start | bytes 589832 | tf_op jit(solution)/shard_map/ppermute | solution.py:27
  31.4 50.3 %copy-start.50 = (f32[2,1,768]{2,0,1:T(2,128)}, f32[2,1,768]{2,0,1:T(2,128)S(1)}, u32[]{:S(2)}) copy-start(f32[2,1,768]{2,0,1:T(2,128)S(1)} %copy.144) | copy-start | bytes 18436
  35.9 71.3 %copy-start.6 = (bf16[512,768]{0,1:T(8,128)(2,1)}, bf16[512,768]{0,1:T(8,128)(2,1)S(1)}, u32[]{:S(2)}) copy-start(bf16[512,768]{0,1:T(8,128)(2,1)S(1)} %copy.88) | copy-start | bytes 2359300
  37.3 44.4 %copy-start.52 = (f32[2,768]{1,0:T(2,128)}, f32[2,768]{1,0:T(2,128)S(1)}, u32[]{:S(2)}) copy-start(f32[2,768]{1,0:T(2,128)S(1)} %get-tuple-element.159) | copy-start | bytes 18436
  53.4 28.4 %copy-start.16 = (f32[2,128,768]{2,1,0:T(8,128)}, f32[2,128,768]{2,1,0:T(8,128)S(1)}, u32[]{:S(2)}) copy-start(f32[2,128,768]{2,1,0:T(8,128)S(1)} %slice.220) | copy-start | bytes 2359300
  84.6 19.6 %collective-permute-start.2 = (bf16[2,64,768]{2,1,0:T(8,128)(2,1)S(1)}, bf16[2,64,768]{2,1,0:T(8,128)(2,1)S(1)}, u32[]{:S(2)}, u32[]{:S(2)}) collective-permute-start(bf16[2,64,768]{2,1,0:T(8,128)(2,1)S(1)} %get-tuple-element.133), channel_id=1, source_target_pairs={{0,1},{1,2},{2,3},{3,4},{4,5},{5,6},{6,7},{7,8},{8,9},{9,10},{10,1... | collective-permute-start | bytes 589832 | tf_op jit(solution)/shard_map/ppermute | solution.py:26
  89.2 15.1 %collective-permute-start.3 = (bf16[2,64,768]{2,1,0:T(8,128)(2,1)S(1)}, bf16[2,64,768]{2,1,0:T(8,128)(2,1)S(1)}, u32[]{:S(2)}, u32[]{:S(2)}) collective-permute-start(bf16[2,64,768]{2,1,0:T(8,128)(2,1)S(1)} %get-tuple-element.134), channel_id=1, source_target_pairs={{1,0},{2,1},{3,2},{4,3},{5,4},{6,5},{7,6},{8,7},{9,8},{10,9},{11,1... | collective-permute-start | bytes 589832 | tf_op jit(solution)/shard_map/ppermute | solution.py:27
  110.3 58.9 %copy-start.40 = (f32[12,512]{1,0:T(8,128)}, f32[12,512]{1,0:T(8,128)S(1)}, u32[]{:S(2)}) copy-start(f32[12,512]{1,0:T(8,128)S(1)} %log_add_fusion) | copy-start | bytes 73732
  123.2 22.2 %slice-start.8 = ((s8[4718592]{0:T(1024)(128)(4,1)}), s8[4194304]{0:T(1024)(128)(4,1)S(1)}, s32[]{:S(2)}) async-start(s8[4718592]{0:T(1024)(128)(4,1)} %bitcast.217), calls=%async_computation.25 | async-start | bytes 8388608
  123.2 30.4 %slice-start.6 = ((s8[4718592]{0:T(1024)(128)(4,1)}), s8[4194304]{0:T(1024)(128)(4,1)S(1)}, s32[]{:S(2)}) async-start(s8[4718592]{0:T(1024)(128)(4,1)} %bitcast.215), calls=%async_computation.23 | async-start | bytes 8388608
  124.2 33.0 %copy-start.24 = (f32[512,768]{1,0:T(8,128)}, f32[512,768]{1,0:T(8,128)S(1)}, u32[]{:S(2)}) copy-start(f32[512,768]{1,0:T(8,128)S(1)} %get-tuple-element.147) | copy-start | bytes 4718596
  124.2 33.0 %copy-start.62 = (f32[512]{0:T(512)}, f32[512]{0:T(512)S(1)}, u32[]{:S(2)}) copy-start(f32[512]{0:T(512)S(1)} %broadcast_multiply_fusion) | copy-start | bytes 6148
  124.5 32.6 %copy-start.71 = (f32[512]{0:T(512)}, f32[512]{0:T(512)S(1)}, u32[]{:S(2)}) copy-start(f32[512]{0:T(512)S(1)} %fusion.84) | copy-start | bytes 6148
  124.6 20.8 %copy-start.22 = (bf16[513,768]{1,0:T(8,128)(2,1)S(1)}, bf16[513,768]{1,0:T(8,128)(2,1)}, u32[]{:S(2)}) copy-start(bf16[513,768]{1,0:T(8,128)(2,1)} %scatter_custom_fusion) | copy-start | bytes 2363908
  124.6 20.8 %slice-start.9 = ((s8[4718592]{0:T(1024)(128)(4,1)}), s8[524288]{0:T(1024)(128)(4,1)S(1)}, s32[]{:S(2)}) async-start(s8[4718592]{0:T(1024)(128)(4,1)} %bitcast.217), calls=%async_computation.26 | async-start | bytes 1048576
  124.6 29.1 %slice-start.7 = ((s8[4718592]{0:T(1024)(128)(4,1)}), s8[524288]{0:T(1024)(128)(4,1)S(1)}, s32[]{:S(2)}) async-start(s8[4718592]{0:T(1024)(128)(4,1)} %bitcast.215), calls=%async_computation.24 | async-start | bytes 1048576
  159.9 9.3 %slice-start.4 = ((s8[6291456]{0:T(1024)(128)(4,1)}), s8[2097152]{0:T(1024)(128)(4,1)S(1)}, s32[]{:S(2)}) async-start(s8[6291456]{0:T(1024)(128)(4,1)} %bitcast.183), calls=%async_computation.21 | async-start | bytes 4194304
  175.2 8.1 copy-start.7
  185.4 10.1 %copy-start.11 = (bf16[512,768]{0,1:T(8,128)(2,1)S(1)}, bf16[512,768]{0,1:T(8,128)(2,1)}, u32[]{:S(2)}) copy-start(bf16[512,768]{0,1:T(8,128)(2,1)} %copy.93) | copy-start | bytes 2359300
  189.1 21.3 %collective-permute-start.5 = (bf16[2,64,768]{2,1,0:T(8,128)(2,1)S(1)}, bf16[2,64,768]{2,1,0:T(8,128)(2,1)S(1)}, u32[]{:S(2)}, u32[]{:S(2)}) collective-permute-start(bf16[2,64,768]{2,1,0:T(8,128)(2,1)S(1)} %get-tuple-element.124), channel_id=1, source_target_pairs={{1,0},{2,1},{3,2},{4,3},{5,4},{6,5},{7,6},{8,7},{9,8},{10,9},{11,1... | collective-permute-start | bytes 589832 | tf_op jit(solution)/shard_map/ppermute | solution.py:35
  190.4 19.8 %copy-start.13 = (f32[1,256,768]{2,1,0:T(8,128)S(1)}, f32[1,256,768]{2,1,0:T(8,128)}, u32[]{:S(2)}) copy-start(f32[1,256,768]{2,1,0:T(8,128)} %copy.99) | copy-start | bytes 2359300
  190.4 19.9 %collective-permute-start.4 = (bf16[2,64,768]{2,1,0:T(8,128)(2,1)S(1)}, bf16[2,64,768]{2,1,0:T(8,128)(2,1)S(1)}, u32[]{:S(2)}, u32[]{:S(2)}) collective-permute-start(bf16[2,64,768]{2,1,0:T(8,128)(2,1)S(1)} %get-tuple-element.125), channel_id=1, source_target_pairs={{0,1},{1,2},{2,3},{3,4},{4,5},{5,6},{6,7},{7,8},{8,9},{9,10},{10,1... | collective-permute-start | bytes 589832 | tf_op jit(solution)/shard_map/ppermute | solution.py:35
  214.4 9.6 %copy-start.39 = (bf16[512,768]{1,0:T(8,128)(2,1)S(1)}, bf16[512,768]{1,0:T(8,128)(2,1)}, u32[]{:S(2)}) copy-start(bf16[512,768]{1,0:T(8,128)(2,1)} %copy-done.38) | copy-start | bytes 2359300
  214.4 206.3 %reduce-scatter.25.cloned.1.call-start = ((), (), s32[]{:S(2)}) async-start(), calls=%async_computation.14 | async-start | bytes 208896
  223.9 204.4 %reduce-scatter.19.cloned.1.call-start = ((), (), s32[]{:S(2)}) async-start(), calls=%async_computation.11 | async-start | bytes 1253376 | tf_op jit(solution)/shard_map/reduce_scatter | solution.py:312
  226.9 222.6 %reduce-scatter.13.cloned.1.call-start = ((), (), s32[]{:S(2)}) async-start(), calls=%async_computation.8 | async-start | bytes 1253376 | tf_op jit(solution)/shard_map/reduce_scatter | solution.py:297
  242.1 8.6 %copy-start.32 = (bf16[1,256,768]{1,2,0:T(8,128)(2,1)S(1)}, bf16[1,256,768]{1,2,0:T(8,128)(2,1)}, u32[]{:S(2)}) copy-start(bf16[1,256,768]{1,2,0:T(8,128)(2,1)} %copy-done.31) | copy-start | bytes 1179652
  270.6 239.6 %reduce-scatter.17.cloned.1.call-start = ((), (), s32[]{:S(2)}) async-start(), calls=%async_computation.10 | async-start | bytes 1253376 | tf_op jit(solution)/shard_map/reduce_scatter | solution.py:306
  369.3 6.2 collective-permute-start.6
  373.9 3.7 collective-permute-start.7
  386.7 184.2 %reduce-scatter.15.cloned.1.call-start = ((), (), s32[]{:S(2)}) async-start(), calls=%async_computation.9 | async-start | bytes 1253376 | tf_op jit(solution)/shard_map/reduce_scatter | solution.py:303
  390.3 259.0 %reduce-scatter.23.cloned.1.call-start = ((), (), s32[]{:S(2)}) async-start(), calls=%async_computation.13 | async-start | bytes 5013504 | tf_op jit(solution)/shard_map/reduce_scatter | solution.py:336
  397.0 330.8 %reduce-scatter.21.cloned.1.call-start = ((), (), s32[]{:S(2)}) async-start(), calls=%async_computation.12 | async-start | bytes 5013504 | tf_op jit(solution)/shard_map/reduce_scatter | solution.py:330
  405.0 416.6 %all-reduce.14.cloned.1.call-start = ((), (), s32[]{:S(2)}) async-start(), calls=%async_computation.16 | async-start | bytes 1769472 | tf_op jit(solution)/shard_map/psum | solution.py:346
  (66 other events, 280.4 us)
Sparse Core Ops, SparseCore 0:
  214.5 56.7 reduce-scatter.26
  274.8 52.2 reduce-scatter.24
  330.7 58.1 reduce-scatter.18
  392.4 57.0 reduce-scatter.12
  453.0 57.1 reduce-scatter.16
  513.7 57.1 reduce-scatter.14
  574.7 74.5 reduce-scatter.22
  653.1 74.7 reduce-scatter.20
  730.6 35.9 all-reduce.13
where the time goes:
time: 849 us; the launch traced here: 838 us
  waiting for transfers between devices  302 us (36%)
  other arithmetic  189 us (22%)
  matrix products  142 us (17%)
  local copies, waits for them, and re-layouts  102 us (12%)
  blocking collectives  63.8 us (8%)
  starting transfers between devices  22.8 us (3%)
  between operations  16.7 us (2%)
    scatter-add x5, other arithmetic, on_device(): grad_ext.at[:, begin:begin + STRIDE * pooled_rows:STRIDE]  88.4 us
    reduce_scatter x1, waiting for transfers between devices, on_device(): lax.psum_scatter(grad_w_in.astype(jnp.bfloat16), 'seq', scatter_dimension...  78.6 us
    reduce_scatter x1, waiting for transfers between devices, on_device(): lax.psum_scatter(grad_w_out.astype(jnp.bfloat16), 'seq', scatter_dimensio...  78.4 us
    reduce_scatter x1, waiting for transfers between devices, on_device(): lax.psum_scatter(grad_w_value.astype(jnp.bfloat16), 'seq', scatter_dimens...  60.6 us
    reduce_scatter x1, waiting for transfers between devices, on_device(): lax.psum_scatter(grad_w_key.astype(jnp.bfloat16), 'seq', scatter_dimensio...  60.6 us
    unnamed x1, blocking collectives  58.1 us
    unnamed x211, local copies, waits for them, and re-layouts  38 us
    dot_general x6, matrix products, product(): return jnp.dot(left_side, right_side, preferred_element_type=jnp.float32)  34 us
  transfers between devices with their start and end apart: 17, of which 6 were waited for; matrix products, arithmetic and copies ran while one was open for 33% of the time, Pallas kernels for 0%

commit v1 on v0

v1 whole, which is shorter than its diff:
```python
import functools

import jax
import jax.numpy as jnp
from jax import lax
from jax.experimental import pallas as pl
from jax.experimental.pallas import tpu as pltpu
from jax.sharding import PartitionSpec as P

D = 768
HEADS = 12
HD = 64
FF = 3072
KERNEL = 5
STRIDE = 4
WIN = 128
POOL_SPAN = 512
HALF = WIN // 2
REACH = POOL_SPAN // (2 * STRIDE)
PAIRS = HEADS // 2
EPSILON = 1e-05
MASKED_OUT = -1000000000.0
SQRT_HALF = 0.7071067811865476
INV_SQRT_2PI = 0.3989422804014327

F32 = jnp.float32
BF16 = jnp.bfloat16
MESH = pl.DeviceIdType.MESH
VMEM = pl.BlockSpec(memory_space=pltpu.VMEM)
ANY = pl.BlockSpec(memory_space=pl.ANY)
VMEM_LIMIT = 64000 * 1024


def struct(shape, dtype):
    return jax.ShapeDtypeStruct(shape, dtype)


def row_of(ref):
    return ref[...].astype(F32)[None, :]


def dot_nn(a, b):
    return lax.dot_general(a, b, (((1,), (0,)), ((), ())), preferred_element_type=F32)


def dot_nt(a, b):
    return lax.dot_general(a, b, (((1,), (1,)), ((), ())), preferred_element_type=F32)


def dot_tn(a, b):
    return lax.dot_general(a, b, (((0,), (0,)), ((), ())), preferred_element_type=F32)


def cols(block, width=128):
    return pl.ds(pl.multiple_of(block * width, 128), width)


def rows_at(start, size, align):
    return pl.ds(pl.multiple_of(start, align), size)


def norm_stats(values):
    shifted = values - jnp.mean(values, axis=-1, keepdims=True)
    inv_std = lax.rsqrt(jnp.mean(shifted * shifted, axis=-1, keepdims=True) + EPSILON)
    return shifted * inv_std, inv_std


def norm_back(n, inv_std, gain, grad):
    u = grad * gain
    mean_u = jnp.mean(u, axis=-1, keepdims=True)
    mean_un = jnp.mean(u * n, axis=-1, keepdims=True)
    return inv_std * (u - mean_u - n * mean_un)


def col_sum(values):
    return jnp.sum(values, axis=0, keepdims=True)


def head_masks():
    lane = lax.broadcasted_iota(jnp.int32, (1, 128), 1)
    low = jnp.where(lane < HD, 1.0, 0.0)
    return low.astype(BF16), (1.0 - low).astype(BF16)


def stack_pair(pair, low, high):
    return jnp.concatenate([pair * low, pair * high], axis=0)


def merge_pair(stacked):
    half = stacked.shape[0] // 2
    lane = lax.broadcasted_iota(jnp.int32, (1, 128), 1)
    return jnp.where(lane < HD, stacked[:half], stacked[half:])


def softmax_rows(scores):
    exp_scores = jnp.exp(scores - jnp.max(scores, axis=-1, keepdims=True))
    return exp_scores * (1.0 / jnp.sum(exp_scores, axis=-1, keepdims=True))


def project_kernel(
    x_ref, g_ref, s_ref, wq_ref, bq_ref, wk_ref, wv_ref, bv_ref, pk_ref, pv_ref,
    nrm_ref, q_ref, kv_ref, pkv_ref, lanes,
):
    tok = x_ref.shape[0]
    pooled = tok // STRIDE
    n, _ = norm_stats(x_ref[...].astype(F32))
    nrm_ref[...] = (n * row_of(g_ref) + row_of(s_ref)).astype(BF16)
    width = 256

    def tile(j, carry):
        c = cols(j, width)
        nrm = nrm_ref[...]
        kv_ref[:, c] = dot_nn(nrm, wk_ref[:, c]).astype(BF16)
        vals = dot_nn(nrm, wv_ref[:, c]) + row_of(bv_ref.at[c])
        kv_ref[:, cols(j + D // width, width)] = vals.astype(BF16)
        qs = dot_nn(nrm, wq_ref[:, c]) + row_of(bq_ref.at[c])
        q_ref[:, c] = qs.astype(BF16)
        return carry

    lax.fori_loop(0, D // width, tile, 0)
    lanes[0:8, :] = jnp.zeros((8, 128), F32)
    for base, taps_ref in ((0, pk_ref), (D // 128, pv_ref)):

        def pool(j, carry):
            taps = taps_ref[:, cols(j)].astype(F32)
            lanes[8 : 8 + tok, :] = kv_ref[:, cols(base + j)].astype(F32)
            total = jnp.zeros((pooled, 128), F32)
            for t in range(KERNEL):
                total = total + lanes[pl.ds(6 + t, pooled, stride=STRIDE), :] * taps[t : t + 1]
            pkv_ref[:, cols(base + j)] = total.astype(BF16)
            return carry

        lax.fori_loop(0, D // 128, pool, 0)


def project(x, g, s, wq, bq, wk, wv, bv, pk, pv):
    tok = x.shape[0]
    return pl.pallas_call(
        project_kernel,
        out_shape=(
            struct((tok, D), BF16),
            struct((tok, D), BF16),
            struct((tok, 2 * D), BF16),
            struct((tok // STRIDE, 2 * D), BF16),
        ),
        in_specs=[VMEM] * 10,
        out_specs=(VMEM,) * 4,
        scratch_shapes=[pltpu.VMEM((tok + 16, 128), F32)],
        compiler_params=pltpu.CompilerParams(vmem_limit_bytes=VMEM_LIMIT),
        name="project",
    )(x, g, s, wq, bq, wk, wv, bv, pk, pv)


def greet(before, after, has_before, has_after):
    barrier = pltpu.get_barrier_semaphore()

    @pl.when(has_before)
    def _():
        pl.semaphore_signal(barrier, inc=1, device_id=before, device_id_type=MESH)

    @pl.when(has_after)
    def _():
        pl.semaphore_signal(barrier, inc=1, device_id=after, device_id_type=MESH)

    inner = jnp.logical_and(has_before, has_after)

    @pl.when(inner)
    def _():
        pl.semaphore_wait(barrier, 2)

    @pl.when(jnp.logical_not(inner))
    def _():
        pl.semaphore_wait(barrier, 1)


def remote(src, dst, send, recv, device):
    return pltpu.make_async_remote_copy(
        src_ref=src, dst_ref=dst, send_sem=send, recv_sem=recv, device_id=device, device_id_type=MESH
    )


def halo_kernel(count, kv_ref, pkv_ref, pk_ref, pv_ref, kvx_ref, pkvx_ref, send, recv):
    tok = kv_ref.shape[0]
    pooled = pkv_ref.shape[0]
    d, s = lax.axis_index("dp"), lax.axis_index("seq")
    before, after = (d, s - 1), (d, s + 1)
    has_before, has_after = s > 0, s < count - 1
    greet(before, after, has_before, has_after)
    to_before = (
        remote(kv_ref.at[pl.ds(0, HALF)], kvx_ref.at[pl.ds(HALF + tok, HALF)], send.at[0], recv.at[0], before),
        remote(pkv_ref.at[pl.ds(0, REACH)], pkvx_ref.at[pl.ds(REACH + pooled, REACH)], send.at[1], recv.at[1], before),
    )
    to_after = (
        remote(kv_ref.at[pl.ds(tok - HALF, HALF)], kvx_ref.at[pl.ds(0, HALF)], send.at[2], recv.at[2], after),
        remote(pkv_ref.at[pl.ds(pooled - REACH, REACH)], pkvx_ref.at[pl.ds(0, REACH)], send.at[3], recv.at[3], after),
    )

    @pl.when(has_before)
    def _():
        for copy in to_before:
            copy.start()

    @pl.when(has_after)
    def _():
        for copy in to_after:
            copy.start()

    kvx_ref[HALF : HALF + tok, :] = kv_ref[...]
    pkvx_ref[REACH : REACH + pooled, :] = pkv_ref[...]

    @pl.when(has_before)
    def _():
        for copy in to_before:
            copy.wait_send()
        for copy in to_after:
            copy.wait_recv()

    @pl.when(jnp.logical_not(has_before))
    def _():
        kvx_ref[0:HALF, :] = jnp.zeros((HALF, 2 * D), BF16)
        pkvx_ref[0:REACH, :] = jnp.zeros((REACH, 2 * D), BF16)

    @pl.when(has_after)
    def _():
        for copy in to_after:
            copy.wait_send()
        for copy in to_before:
            copy.wait_recv()

    @pl.when(jnp.logical_not(has_after))
    def _():
        kvx_ref[HALF + tok :, :] = jnp.zeros((HALF, 2 * D), BF16)
        pkvx_ref[REACH + pooled :, :] = jnp.zeros((REACH, 2 * D), BF16)

    taps = jnp.concatenate([pk_ref[...].astype(F32), pv_ref[...].astype(F32)], axis=1)

    def fix(key_row, pooled_row):
        near = kvx_ref[key_row - 16 : key_row + 16, :].astype(F32)[14 : 14 + KERNEL]
        value = jnp.sum(near * taps, axis=0, keepdims=True)
        old = pkvx_ref[pooled_row : pooled_row + 16, :].astype(F32)
        row = lax.broadcasted_iota(jnp.int32, (16, 1), 0)
        pkvx_ref[pooled_row : pooled_row + 16, :] = jnp.where(row == 0, value, old).astype(BF16)

    fix(HALF, REACH)

    @pl.when(has_after)
    def _():
        fix(HALF + tok, REACH + pooled)


def halo(count, kv, pkv, pk, pv):
    tok, pooled = kv.shape[0], pkv.shape[0]
    return pl.pallas_call(
        functools.partial(halo_kernel, count),
        out_shape=(struct((tok + WIN, 2 * D), BF16), struct((pooled + 2 * REACH, 2 * D), BF16)),
        in_specs=[VMEM] * 4,
        out_specs=(VMEM,) * 2,
        scratch_shapes=[pltpu.SemaphoreType.DMA((4,)), pltpu.SemaphoreType.DMA((4,))],
        compiler_params=pltpu.CompilerParams(
            collective_id=0, has_side_effects=True, vmem_limit_bytes=VMEM_LIMIT
        ),
        name="halo",
    )(kv, pkv, pk, pv)


def halo_back_kernel(count, near_ref, far_ref, nb_ref, na_ref, fb_ref, fa_ref, p0_ref, send, recv):
    tok = near_ref.shape[0] - WIN
    pooled = far_ref.shape[0] - 2 * REACH
    d, s = lax.axis_index("dp"), lax.axis_index("seq")
    before, after = (d, s - 1), (d, s + 1)
    has_before, has_after = s > 0, s < count - 1
    greet(before, after, has_before, has_after)
    to_before = (
        remote(near_ref.at[pl.ds(0, HALF)], na_ref, send.at[0], recv.at[0], before),
        remote(far_ref.at[pl.ds(0, REACH)], fa_ref, send.at[1], recv.at[1], before),
        remote(far_ref.at[pl.ds(REACH, 16)], p0_ref, send.at[2], recv.at[2], before),
    )
    to_after = (
        remote(near_ref.at[pl.ds(HALF + tok, HALF)], nb_ref, send.at[3], recv.at[3], after),
        remote(far_ref.at[pl.ds(REACH + pooled, REACH)], fb_ref, send.at[4], recv.at[4], after),
    )

    @pl.when(has_before)
    def _():
        for copy in to_before:
            copy.start()

    @pl.when(has_after)
    def _():
        for copy in to_after:
            copy.start()

    @pl.when(has_before)
    def _():
        for copy in to_before:
            copy.wait_send()
        for copy in to_after:
            copy.wait_recv()

    @pl.when(jnp.logical_not(has_before))
    def _():
        nb_ref[...] = jnp.zeros_like(nb_ref)
        fb_ref[...] = jnp.zeros_like(fb_ref)

    @pl.when(has_after)
    def _():
        for copy in to_after:
            copy.wait_send()
        for copy in to_before:
            copy.wait_recv()

    @pl.when(jnp.logical_not(has_after))
    def _():
        na_ref[...] = jnp.zeros_like(na_ref)
        fa_ref[...] = jnp.zeros_like(fa_ref)
        p0_ref[...] = jnp.zeros_like(p0_ref)


def halo_back(count, near, far):
    return pl.pallas_call(
        functools.partial(halo_back_kernel, count),
        out_shape=(
            struct((HALF, 2 * D), BF16),
            struct((HALF, 2 * D), BF16),
            struct((REACH, 2 * D), BF16),
            struct((REACH, 2 * D), BF16),
            struct((16, 2 * D), BF16),
        ),
        in_specs=[VMEM] * 2,
        out_specs=(VMEM,) * 5,
        scratch_shapes=[pltpu.SemaphoreType.DMA((5,)), pltpu.SemaphoreType.DMA((5,))],
        compiler_params=pltpu.CompilerParams(
            collective_id=1, has_side_effects=True, vmem_limit_bytes=VMEM_LIMIT
        ),
        name="halo_back",
    )(near, far)


def window_biases(count, s, query_pos, near_keys, near_base, far_keys, far_base, tok):
    near_index = near_base + lax.broadcasted_iota(jnp.int32, (1, near_keys), 1)
    near_ok = (near_index >= query_pos) & (near_index < query_pos + WIN)
    near_ok = near_ok & ((near_index >= HALF) | (s > 0))
    near_ok = near_ok & ((near_index < HALF + tok) | (s < count - 1))
    far_index = far_base + lax.broadcasted_iota(jnp.int32, (1, far_keys), 1)
    far_ok = (STRIDE * far_index >= query_pos) & (STRIDE * far_index < query_pos + POOL_SPAN)
    far_ok = far_ok & ((far_index >= REACH) | (s > 0))
    far_ok = far_ok & ((far_index < REACH + tok // STRIDE) | (s < count - 1))
    return jnp.where(near_ok, 0.0, MASKED_OUT), jnp.where(far_ok, 0.0, MASKED_OUT)


FF_TILE = 384


def masked_kernel(
    count, groups,
    x_ref, nrm_ref, q_ref, kvx_ref, pkvx_ref, slots_ref, cotr_ref, wo_ref, bo_ref, g2_ref, s2_ref,
    win_hbm, bin_ref, wout_hbm,
    actt_ref, gpre_ref, n2t_ref, cot_ref, mixt_ref, gbr_ref, nrmt_ref, gq_ref,
    gnear_ref, gfar_ref, ghid_ref, gqd_ref, veca_ref, binsum_ref,
    win_ref, wout_ref, wn_ref, wf_ref, qm_ref, mix_ref, gm_ref, nbias_ref, fbias_ref, n2_ref, acc_ref, bin_row, sems,
):
    s = lax.axis_index("seq")
    bin_row[...] = row_of(bin_ref)
    tok = x_ref.shape[0]
    cap = cotr_ref.shape[0]
    near_keys, far_keys = kvx_ref.shape[0], pkvx_ref.shape[0]
    load_in = pltpu.make_async_copy(win_hbm, win_ref, sems.at[0])
    load_out = pltpu.make_async_copy(wout_hbm, wout_ref, sems.at[1])
    load_in.start()
    load_out.start()

    slots = slots_ref[0, 0].reshape(1, cap)
    onehot_t = jnp.where(lax.broadcasted_iota(jnp.int32, (tok, cap), 0) == slots, 1.0, 0.0).astype(BF16)
    slot_col = jnp.transpose(jnp.broadcast_to(slots, (cap, cap)))[:, 0:1]
    x_rows = dot_tn(onehot_t, x_ref[...])
    nrm_rows = dot_tn(onehot_t, nrm_ref[...])
    qm_ref[...] = (dot_tn(onehot_t, q_ref[...]) * (HD**-0.5)).astype(BF16)
    nrm_rows_t = jnp.transpose(nrm_rows).astype(BF16)
    store_rows(nrmt_ref, nrm_rows_t, groups)
    live = jnp.where(slot_col >= 0, 1.0, 0.0)
    cot_ref[...] = jnp.where(slot_col >= 0, cotr_ref[...].astype(F32), 0.0).astype(BF16)

    nbias, fbias = window_biases(count, s, slot_col, near_keys, 0, far_keys, 0, tok)
    nbias_ref[...] = nbias
    fbias_ref[...] = fbias
    low, high = head_masks()

    def attend(p, carry):
        c, cv = cols(p), cols(p + PAIRS)
        qs = stack_pair(qm_ref[:, c], low, high)
        near = dot_nt(qs, kvx_ref[:, c])
        nb, fb = nbias_ref[...], fbias_ref[...]
        near_w = softmax_rows(near + jnp.concatenate([nb, nb], axis=0))
        wn_ref[p] = near_w
        far = dot_nt(qs, pkvx_ref[:, c])
        far_w = softmax_rows(far + jnp.concatenate([fb, fb], axis=0))
        wf_ref[p] = far_w
        out = dot_nn(near_w.astype(BF16), kvx_ref[:, cv]) + dot_nn(far_w.astype(BF16), pkvx_ref[:, cv])
        mix_ref[:, c] = merge_pair(out).astype(BF16)
        return carry

    lax.fori_loop(0, PAIRS, attend, 0)
    mixed = mix_ref[...]
    store_rows(mixt_ref, jnp.transpose(mixed.astype(F32)).astype(BF16), groups)
    hidden = x_rows + dot_nn(mixed, wo_ref[...]) + row_of(bo_ref)
    gain_two = row_of(g2_ref)
    n_two, inv_two = norm_stats(hidden)
    normed_two = n_two * gain_two + row_of(s2_ref)
    n2_ref[...] = normed_two.astype(BF16)
    store_rows(n2t_ref, jnp.transpose(normed_two).astype(BF16), groups)
    acc_ref[...] = jnp.zeros_like(acc_ref)
    load_in.wait()
    load_out.wait()

    def feed(t, carry):
        c = cols(t, FF_TILE)
        pre = dot_nn(n2_ref[...], win_ref[:, c]) + bin_row[:, c]
        cdf = 0.5 * (1.0 + lax.erf(pre * SQRT_HALF))
        store_act(actt_ref, t, jnp.transpose(pre * cdf), groups)
        slope = cdf + pre * (INV_SQRT_2PI * jnp.exp(-0.5 * pre * pre))
        grad_act = dot_nt(cot_ref[...], wout_ref[rows_at(t * FF_TILE, FF_TILE, FF_TILE), :])
        gpre = (grad_act * slope).astype(BF16)
        gpre_ref[t] = gpre
        binsum_ref[:, c] = col_sum(gpre.astype(F32))
        acc_ref[...] += dot_nt(gpre, win_ref[:, c])
        return carry

    lax.fori_loop(0, FF // FF_TILE, feed, 0)
    cot = cot_ref[...].astype(F32)
    grad_n2 = acc_ref[...]
    grad_hidden = cot + norm_back(n_two, inv_two, gain_two, grad_n2)
    grad_branch = grad_hidden.astype(BF16)
    gbr_ref[...] = grad_branch
    gm_ref[...] = dot_nt(grad_branch, wo_ref[...]).astype(BF16)
    high_part = grad_branch
    low_part = (grad_hidden - high_part.astype(F32)).astype(BF16)
    ghid_ref[...] = dot_nn(onehot_t, high_part) + dot_nn(onehot_t, low_part)

    def attend_back(p, carry):
        c, cv = cols(p), cols(p + PAIRS)
        qs = stack_pair(qm_ref[:, c], low, high)
        gs = stack_pair(gm_ref[:, c], low, high)
        near_w, far_w = wn_ref[p], wf_ref[p]
        dn = dot_nt(gs, kvx_ref[:, cv])
        ds = (near_w * (dn - jnp.sum(near_w * dn, axis=-1, keepdims=True))).astype(BF16)
        df = dot_nt(gs, pkvx_ref[:, cv])
        dsf = (far_w * (df - jnp.sum(far_w * df, axis=-1, keepdims=True))).astype(BF16)
        gq = dot_nn(ds, kvx_ref[:, c]) + dot_nn(dsf, pkvx_ref[:, c])
        gq_ref[:, c] = (merge_pair(gq) * (HD**-0.5)).astype(BF16)
        gnear_ref[:, c] = dot_tn(ds, qs).astype(BF16)
        gnear_ref[:, cv] = dot_tn(near_w.astype(BF16), gs).astype(BF16)
        gfar_ref[:, c] = dot_tn(dsf, qs).astype(BF16)
        gfar_ref[:, cv] = dot_tn(far_w.astype(BF16), gs).astype(BF16)
        return carry

    lax.fori_loop(0, PAIRS, attend_back, 0)
    gq = gq_ref[...]
    gqd_ref[...] = dot_nn(onehot_t, gq).astype(BF16)
    veca_ref[0:1, :] = col_sum(gq.astype(F32))
    veca_ref[1:2, :] = col_sum(grad_branch.astype(F32))
    veca_ref[2:3, :] = col_sum(grad_n2 * n_two)
    veca_ref[3:4, :] = col_sum(grad_n2)
    veca_ref[4:5, :] = col_sum(cot)
    veca_ref[5:8, :] = jnp.zeros((3, D), F32)


def store_rows(ref, values, groups):
    if groups is None:
        ref[...] = values
        return
    shard = D // groups["seq"]
    for k in range(groups["chips"]):
        at = groups["place"](k) * shard
        for core in range(2):
            start = (2 * k + core) * shard
            ref[core, at : at + shard, :] = values[start : start + shard]


def store_act(ref, t, values, groups):
    if groups is None:
        ref[t] = values.astype(BF16)
        return
    part = FF // groups["seq"] // 2
    values = values.astype(BF16)
    at = groups["place"](t) * part
    for core in range(2):
        for half in range(2):
            start = (2 * core + half) * part
            ref[core, half, rows_at(at, part, part), :] = values[start : start + part]


def masked(count, groups, x, nrm, q, kvx, pkvx, slots, cot_rows, wo, bo, g2, s2, w_in, b_in, w_out):
    tok, cap = x.shape[0], cot_rows.shape[0]
    near_keys, far_keys = kvx.shape[0], pkvx.shape[0]
    tiles = FF // FF_TILE
    if groups is None:
        actt, rows_t = (tiles, FF_TILE, cap), (D, cap)
    else:
        actt, rows_t = (2, 2, FF // 4, cap), (2, D // 2, cap)
    return pl.pallas_call(
        functools.partial(masked_kernel, count, groups),
        out_shape=(
            struct(actt, BF16),
            struct((tiles, cap, FF_TILE), BF16),
            struct(rows_t, BF16),
            struct((cap, D), BF16),
            struct(rows_t, BF16),
            struct((cap, D), BF16),
            struct(rows_t, BF16),
            struct((cap, D), BF16),
            struct((near_keys, 2 * D), BF16),
            struct((far_keys, 2 * D), BF16),
            struct((tok, D), F32),
            struct((tok, D), BF16),
            struct((8, D), F32),
            struct((1, FF), F32),
        ),
        in_specs=[VMEM] * 11 + [ANY, VMEM, ANY],
        out_specs=(VMEM,) * 14,
        scratch_shapes=[
            pltpu.VMEM((D, FF), BF16),
            pltpu.VMEM((FF, D), BF16),
            pltpu.VMEM((PAIRS, 2 * cap, near_keys), F32),
            pltpu.VMEM((PAIRS, 2 * cap, far_keys), F32),
            pltpu.VMEM((cap, D), BF16),
            pltpu.VMEM((cap, D), BF16),
            pltpu.VMEM((cap, D), BF16),
            pltpu.VMEM((cap, near_keys), F32),
            pltpu.VMEM((cap, far_keys), F32),
            pltpu.VMEM((cap, D), BF16),
            pltpu.VMEM((cap, D), F32),
            pltpu.VMEM((1, FF), F32),
            pltpu.SemaphoreType.DMA((2,)),
        ],
        compiler_params=pltpu.CompilerParams(vmem_limit_bytes=VMEM_LIMIT),
        name="masked_rows",
    )(x, nrm, q, kvx, pkvx, slots, cot_rows, wo, bo, g2, s2, w_in, b_in, w_out)


def finish_kernel(
    groups,
    x_ref, nrm_ref, g1_ref, kvx_ref, gnear_ref, gfar_ref, nb_ref, na_ref, fb_ref, fa_ref, p0_ref,
    gqd_ref, ghid_ref, wq_ref, wk_ref, wv_ref, pk_ref, pv_ref,
    gin_ref, gw_ref, vecb_ref,
    gkv_ref, gp_ref, keys, grads, acc_ref,
):
    tok = x_ref.shape[0]
    pooled = tok // STRIDE
    half = pooled - REACH
    own = gfar_ref[REACH : REACH + pooled, :].astype(F32)
    gp_ref[0:pooled, :] = own
    gp_ref[0:REACH, :] += fb_ref[...].astype(F32)
    gp_ref[half:pooled, :] += fa_ref[...].astype(F32)
    gp_ref[0:pooled, :] = gp_ref[0:pooled, :].astype(BF16).astype(F32)
    nxt = gfar_ref[REACH + pooled : REACH + pooled + 16, :].astype(F32) + p0_ref[...].astype(F32)
    gp_ref[pooled : pooled + 16, :] = nxt.astype(BF16).astype(F32)
    vecb_ref[...] = jnp.zeros_like(vecb_ref)
    for base, first, taps_ref in ((0, 3, pk_ref), (D // 128, 8, pv_ref)):

        def pool(j, carry):
            c = cols(base + j)
            taps = taps_ref[:, cols(j)].astype(F32)
            keys[...] = kvx_ref[HALF - 16 : HALF + tok, c].astype(F32)
            grads[8 : 8 + tok, :] = gnear_ref[HALF : HALF + tok, c].astype(F32)
            grads[8 : 8 + HALF, :] += nb_ref[:, c].astype(F32)
            grads[8 + tok - HALF : 8 + tok, :] += na_ref[:, c].astype(F32)
            gp = gp_ref[0:pooled, c]
            for t in range(KERNEL):
                at = pl.ds(6 + t, pooled, stride=STRIDE)
                grads[at, :] += gp * taps[t : t + 1]
                key_rows = keys[pl.ds(14 + t, pooled, stride=STRIDE), :]
                vecb_ref[first + t : first + t + 1, cols(j)] = col_sum(key_rows * gp)
            last = gp_ref[pooled : pooled + 8, c][0:1]
            tail = jnp.concatenate([jnp.zeros((6, 128), F32), last * taps[0:1], last * taps[1:2]], axis=0)
            grads[tok : tok + 8, :] += tail
            gkv_ref[:, c] = grads[8 : 8 + tok, :].astype(BF16)
            return carry

        grads[0:8, :] = jnp.zeros((8, 128), F32)
        lax.fori_loop(0, D // 128, pool, 0)

    width = 256

    def weights(j, carry):
        c = cols(j, width)
        gw_ref[j] = dot_tn(nrm_ref[...], gkv_ref[:, c]).astype(BF16)
        return carry

    lax.fori_loop(0, 2 * D // width, weights, 0)

    def back(j, carry):
        c = cols(j, width)
        r = rows_at(j * width, width, width)
        total = dot_nt(gqd_ref[...], wq_ref[r, :])
        total = total + dot_nt(gkv_ref[:, 0:D], wk_ref[r, :]) + dot_nt(gkv_ref[:, D : 2 * D], wv_ref[r, :])
        acc_ref[:, c] = total
        return carry

    lax.fori_loop(0, D // width, back, 0)
    rows = 128
    gain = row_of(g1_ref)

    def norm(j, sums):
        r = rows_at(j * rows, rows, rows)
        n, inv = norm_stats(x_ref[r, :].astype(F32))
        e = acc_ref[r, :]
        gin_ref[r, :] = ghid_ref[r, :] + norm_back(n, inv, gain, e)
        return (
            sums[0] + col_sum(e * n),
            sums[1] + col_sum(e),
            sums[2] + col_sum(gkv_ref[r, D : 2 * D].astype(F32)),
        )

    zero = jnp.zeros((1, D), F32)
    sums = lax.fori_loop(0, tok // rows, norm, (zero, zero, zero))
    for i in range(3):
        vecb_ref[i : i + 1, :] = sums[i]


def finish(groups, x, nrm, g1, kvx, gnear, gfar, edges, gqd, ghid, wq, wk, wv, pk, pv):
    tok = x.shape[0]
    return pl.pallas_call(
        functools.partial(finish_kernel, groups),
        out_shape=(
            struct((tok, D), F32),
            struct((6, D, 256), BF16),
            struct((16, D), F32),
        ),
        in_specs=[VMEM] * 18,
        out_specs=(VMEM,) * 3,
        scratch_shapes=[
            pltpu.VMEM((tok, 2 * D), BF16),
            pltpu.VMEM((tok // STRIDE + 16, 2 * D), F32),
            pltpu.VMEM((tok + 16, 128), F32),
            pltpu.VMEM((tok + 16, 128), F32),
            pltpu.VMEM((tok, D), F32),
        ],
        compiler_params=pltpu.CompilerParams(vmem_limit_bytes=VMEM_LIMIT),
        name="finish",
    )(x, nrm, g1, kvx, gnear, gfar, *edges, gqd, ghid, wq, wk, wv, pk, pv)


def dense_kernel(
    count,
    x_ref, q_ref, kvx_ref, pkvx_ref, wo_ref, bo_ref, g2_ref, s2_ref, win_hbm, bin_ref, wout_hbm, bout_ref,
    out_ref,
    win_ref, wout_ref, nbias_ref, fbias_ref, mix_ref, n2_ref, acc_ref, bin_row, sems,
):
    s = lax.axis_index("seq")
    bin_row[...] = row_of(bin_ref)
    tok = x_ref.shape[0]
    load_in = pltpu.make_async_copy(win_hbm, win_ref, sems.at[0])
    load_out = pltpu.make_async_copy(wout_hbm, wout_ref, sems.at[1])
    load_in.start()
    load_out.start()
    block = 128
    near_keys, far_keys = block + WIN, (block + POOL_SPAN) // STRIDE
    step = block // STRIDE
    blocks = tok // block
    for b in range(blocks):
        pos = b * block + lax.broadcasted_iota(jnp.int32, (block, 1), 0)
        nb, fb = window_biases(count, s, pos, near_keys, b * block, far_keys, b * step, tok)
        nbias_ref[b] = nb
        fbias_ref[b] = fb
    low, high = head_masks()

    def attend(i, carry):
        b, p = i // PAIRS, i % PAIRS
        c, cv = cols(p), cols(p + PAIRS)
        rows = rows_at(b * block, block, block)
        near = rows_at(b * block, near_keys, block)
        far = rows_at(b * step, far_keys, step)
        qs = stack_pair(q_ref[rows, c] * jnp.asarray(HD**-0.5, BF16), low, high)
        nb, fb = nbias_ref[b], fbias_ref[b]
        near_w = softmax_rows(dot_nt(qs, kvx_ref[near, c]) + jnp.concatenate([nb, nb], axis=0))
        far_w = softmax_rows(dot_nt(qs, pkvx_ref[far, c]) + jnp.concatenate([fb, fb], axis=0))
        out = dot_nn(near_w.astype(BF16), kvx_ref[near, cv]) + dot_nn(far_w.astype(BF16), pkvx_ref[far, cv])
        mix_ref[rows, c] = merge_pair(out).astype(BF16)
        return carry

    lax.fori_loop(0, blocks * PAIRS, attend, 0)

    def residual(b, carry):
        rows = rows_at(b * block, block, block)
        hidden = x_ref[rows, :].astype(F32) + dot_nn(mix_ref[rows, :], wo_ref[...]) + row_of(bo_ref)
        n, _ = norm_stats(hidden)
        n2_ref[rows, :] = (n * row_of(g2_ref) + row_of(s2_ref)).astype(BF16)
        acc_ref[rows, :] = hidden + row_of(bout_ref)
        return carry

    lax.fori_loop(0, blocks, residual, 0)
    load_in.wait()
    load_out.wait()
    high_rows = 256

    def feed(i, carry):
        t, b = i // (tok // high_rows), i % (tok // high_rows)
        c = cols(t, FF_TILE)
        rows = rows_at(b * high_rows, high_rows, high_rows)
        pre = dot_nn(n2_ref[rows, :], win_ref[:, c]) + bin_row[:, c]
        act = (pre * (0.5 * (1.0 + lax.erf(pre * SQRT_HALF)))).astype(BF16)
        acc_ref[rows, :] += dot_nn(act, wout_ref[rows_at(t * FF_TILE, FF_TILE, FF_TILE), :])
        return carry

    lax.fori_loop(0, FF // FF_TILE * (tok // high_rows), feed, 0)
    out_ref[...] = acc_ref[...].astype(BF16)


def dense(count, x, q, kvx, pkvx, wo, bo, g2, s2, w_in, b_in, w_out, b_out):
    tok = x.shape[0]
    blocks = tok // 128
    return pl.pallas_call(
        functools.partial(dense_kernel, count),
        out_shape=struct((tok, D), BF16),
        in_specs=[VMEM] * 8 + [ANY, VMEM, ANY, VMEM],
        out_specs=VMEM,
        scratch_shapes=[
            pltpu.VMEM((D, FF), BF16),
            pltpu.VMEM((FF, D), BF16),
            pltpu.VMEM((blocks, 128, 128 + WIN), F32),
            pltpu.VMEM((blocks, 128, (128 + POOL_SPAN) // STRIDE), F32),
            pltpu.VMEM((tok, D), BF16),
            pltpu.VMEM((tok, D), BF16),
            pltpu.VMEM((tok, D), F32),
            pltpu.VMEM((1, FF), F32),
            pltpu.SemaphoreType.DMA((2,)),
        ],
        compiler_params=pltpu.CompilerParams(vmem_limit_bytes=VMEM_LIMIT),
        name="dense_forward",
    )(x, q, kvx, pkvx, wo, bo, g2, s2, w_in, b_in, w_out, b_out)


def plain_reduce(actt, gpre, n2t, cot, mixt, gbr, nrmt, gq, gw, veca, vecb, binsum):
    def prod(a, b):
        return jnp.dot(a, b, preferred_element_type=F32)

    def total(value, axis=0):
        part = lax.psum_scatter(value.astype(BF16), "seq", scatter_dimension=axis, tiled=True)
        return lax.psum(part, "dp").astype(F32)

    cap = cot.shape[0]
    w_out = total(prod(actt.reshape(FF, cap), cot))
    w_in = total(prod(n2t, jnp.moveaxis(gpre, 0, 1).reshape(cap, FF)))
    w_o = total(prod(mixt, gbr))
    w_q = total(prod(nrmt, gq))
    gkv = jnp.moveaxis(gw, 0, 1).reshape(D, 2 * D)
    w_k, w_v = total(gkv[:, :D]), total(gkv[:, D:])
    return (
        total(vecb[0]), total(vecb[1]), w_q, total(veca[0]), w_k, w_v, total(vecb[2]), w_o, total(veca[1]),
        total(vecb[3:8], 1), total(vecb[8:13], 1), total(veca[2]), total(veca[3]),
        w_in, total(binsum[0]), w_out, total(veca[4]),
    )


def on_device(
    n_dp, n_seq, x_input, gain_one, shift_one, w_query, b_query, w_key, w_value, b_value, w_attn_out, b_attn_out,
    pool_key, pool_value, gain_two, shift_two, w_in, b_in, w_out, b_out, mask_slots, cot_rows,
):
    x = x_input[0]
    groups = None
    nrm, q, kv, pkv = project(
        x, gain_one, shift_one, w_query, b_query, w_key, w_value, b_value, pool_key, pool_value
    )
    kvx, pkvx = halo(n_seq, kv, pkv, pool_key, pool_value)
    (actt, gpre, n2t, cot, mixt, gbr, nrmt, gq, gnear, gfar, ghid, gqd, veca, binsum) = masked(
        n_seq, groups, x, nrm, q, kvx, pkvx, mask_slots, cot_rows[0, 0],
        w_attn_out, b_attn_out, gain_two, shift_two, w_in, b_in, w_out,
    )
    edges = halo_back(n_seq, gnear, gfar)
    grad_input, gw, vecb = finish(
        groups, x, nrm, gain_one, kvx, gnear, gfar, edges, gqd, ghid, w_query, w_key, w_value, pool_key, pool_value
    )
    output = dense(
        n_seq, x, q, kvx, pkvx, w_attn_out, b_attn_out, gain_two, shift_two, w_in, b_in, w_out, b_out
    )
    reduced = plain_reduce(actt, gpre, n2t, cot, mixt, gbr, nrmt, gq, gw, veca, vecb, binsum)
    return (output[None], grad_input[None]) + reduced


def solution(mesh):
    n_dp, n_seq = mesh.shape["dp"], mesh.shape["seq"]
    rows = P("dp", "seq", None)
    return jax.shard_map(
        functools.partial(on_device, n_dp, n_seq),
        mesh=mesh,
        in_specs=(rows,) + (P(),) * 17 + (rows, P("dp", "seq", None, None)),
        out_specs=(
            rows, rows, P("seq"), P("seq"), P("seq", None), P("seq"), P("seq", None), P("seq", None), P("seq"),
            P("seq", None), P("seq"), P(None, "seq"), P(None, "seq"), P("seq"), P("seq"), P("seq", None),
            P("seq"), P("seq", None), P("seq"),
        ),
        check_vma=False,
    )
```

time: 849 us -> 661 us (0.78)
  the two profiles are of different devices: /device:TPU:0 before, /device:TPU:8 now
where the time goes in v1:
time: 661 us; the launch traced here: 659 us
  waiting for transfers between devices  443 us (67%)
  Pallas kernels  101 us (15%)
  blocking collectives  55.7 us (8%)
  local copies, waits for them, and re-layouts  21.8 us (3%)
  between operations  15.4 us (2%)
  other arithmetic  11.7 us (2%)
  matrix products  10 us (2%)
    reduce_scatter x4, waiting for transfers between devices, total(): lax.psum_scatter(value.astype(BF16), 'seq', scatter_dimension=axis, tiled...  276 us
    unnamed x13, waiting for transfers between devices  134 us
    unnamed x1, blocking collectives  50.7 us
    psum x1, waiting for transfers between devices, total(): return lax.psum(part, 'dp').astype(F32)  32.1 us
    pallas_call x1, Pallas kernels, dense(): pl.pallas_call(functools.partial(dense_kernel, count), out_shape=struct((...  30.8 us
    pallas_call x1, Pallas kernels, masked(): pl.pallas_call(functools.partial(masked_kernel, count, groups), out_shape...  23 us
    unnamed x46, local copies, waits for them, and re-layouts  17.3 us
    pallas_call x1, Pallas kernels, finish(): pl.pallas_call(functools.partial(finish_kernel, groups), out_shape=(struc...  14.9 us
  transfers between devices with their start and end apart: 9, of which 8 were waited for; matrix products, arithmetic and copies ran while one was open for 4% of the time, Pallas kernels for 5%

profile of v1, /device:TPU:8, one launch (start us, length us, event | category | flops | bytes accessed | tf_op | source)
XLA Modules:
  0.0 658.8 jit_solution(15141202333904041096)
XLA Ops:
  7.2 7.6 %project.1 = (bf16[512,768]{1,0:T(8,128)(2,1)}, bf16[512,768]{1,0:T(8,128)(2,1)}, bf16[512,1536]{1,0:T(8,128)(2,1)}, bf16[128,1536]{1,0:T(8,128)(2,1)}) custom-call(bf16[512,768]{1,0:T(8,128)(2,1)} %bitcast.24, bf16[768]{0:T(1024)(128)(2,1)} %g1_ref.1, bf16[768]{0:T(1024)(128)(2,1)} %s_ref.1, bf16[768,768]{1,0:T(8,128)(2,1)} %wq_ref.3, ...), custom_call_target="tpu_custom_call" | custom-call | tf_op jit(solution)/shard_map/project/pallas_call | solution.py:138
  14.8 11.4 %halo.1 = (bf16[640,1536]{1,0:T(8,128)(2,1)}, bf16[256,1536]{1,0:T(8,128)(2,1)}) custom-call(bf16[512,1536]{1,0:T(8,128)(2,1)} %get-tuple-element.48.kv_ref, bf16[128,1536]{1,0:T(8,128)(2,1)} %get-tuple-element.49.pkv_ref, bf16[5,768]{1,0:T(8,128)(2,1)} %pk_ref.5, bf16[5,768]{1,0:T(8,128)(2,1)} %pv_ref.5), custom_call_target="tpu_custom_call" | custom-call | tf_op jit(solution)/shard_map/halo/pallas_call | solution.py:253
  26.3 23.0 %masked_rows.1 = (bf16[8,384,128]{2,1,0:T(8,128)(2,1)}, bf16[8,128,384]{2,1,0:T(8,128)(2,1)}, bf16[768,128]{1,0:T(8,128)(2,1)}, bf16[128,768]{1,0:T(8,128)(2,1)}...) custom-call(bf16[512,768]{1,0:T(8,128)(2,1)} %bitcast.25, ...), custom_call_target="tpu_custom_call" | custom-call | tf_op jit(solution)/shard_map/masked_rows/pallas_call | solution.py:500
  49.3 13.0 %halo_back.1 = (bf16[64,1536]{1,0:T(8,128)(2,1)}, bf16[64,1536]{1,0:T(8,128)(2,1)}, bf16[64,1536]{1,0:T(8,128)(2,1)}, bf16[64,1536]{1,0:T(8,128)(2,1)}, bf16[16,1536]{1,0:T(8,128)(2,1)}) custom-call(bf16[640,1536]{1,0:T(8,128)(2,1)} %get-tuple-element.53.near_ref.gnear_ref, bf16[256,1536]{1,0:T(8,128)(2,1)} %get-tuple-element.54.far_ref.gfar_ref), custom_call_target="tpu_custom_call" | custom-call | tf_op jit(solution)/shard_map/halo_back/pallas_call | solution.py:320
  62.3 14.9 %finish.1 = (f32[512,768]{1,0:T(8,128)}, bf16[6,768,256]{2,1,0:T(8,128)(2,1)}, f32[16,768]{1,0:T(8,128)}) custom-call(bf16[512,768]{1,0:T(8,128)(2,1)} %bitcast.26, bf16[512,768]{1,0:T(8,128)(2,1)} %get-tuple-element.52.nrm_ref, bf16[768]{0:T(1024)(128)(2,1)} %g1_ref.1, bf16[640,1536]{1,0:T(8,128)(2,1)} %get-tuple-element.50.kvx_ref, ...), custom_call_target="tpu_custom_call" | custom-call | tf_op jit(solution)/shard_map/finish/pallas_call | solution.py:622
  77.3 2.8 copy.43
  80.1 1.2 fusion
  81.3 2.4 copy.49
  83.8 1.5 copy.47
  85.4 1.5 convolution_convert_fusion.3
  87.0 1.5 convolution_convert_fusion.2
  89.4 3.5 convolution_convert_fusion.1
  93.2 0.9 copy-done
  94.1 3.5 convolution_convert_fusion
  97.7 0.7 copy-done.9
  98.4 0.8 copy.53
  99.3 0.8 copy.51
  100.2 46.6 %reduce-scatter.27.cloned.1.call-done = bf16[48,768]{1,0:T(8,128)(2,1)} async-done(((bf16[768,768]{1,0:T(8,128)(2,1)}), bf16[48,768]{1,0:T(8,128)(2,1)}) %reduce-scatter.27.cloned.1.call-update) | async-done | bytes 73744
  146.9 1.7 copy.50
  148.6 59.1 %reduce-scatter.25.cloned.1.call-done = bf16[48,768]{1,0:T(8,128)(2,1)} async-done(((bf16[768,768]{1,0:T(8,128)(2,1)}), bf16[48,768]{1,0:T(8,128)(2,1)}) %reduce-scatter.25.cloned.1.call-update) | async-done | bytes 73744
  207.7 1.7 copy.48
  209.4 59.2 %reduce-scatter.17.cloned.1.call-done = bf16[48,768]{1,0:T(8,128)(2,1)} async-done(((bf16[768,768]{1,0:T(8,128)(2,1)}), bf16[48,768]{1,0:T(8,128)(2,1)}) %reduce-scatter.17.cloned.1.call-update) | async-done | bytes 73744 | tf_op jit(solution)/shard_map/reduce_scatter | solution.py:738
  268.5 60.7 %reduce-scatter.19.cloned.1.call-done = bf16[48,768]{1,0:T(8,128)(2,1)} async-done(((bf16[768,768]{1,0:T(8,128)(2,1)}), bf16[48,768]{1,0:T(8,128)(2,1)}) %reduce-scatter.19.cloned.1.call-update) | async-done | bytes 73744 | tf_op jit(solution)/shard_map/reduce_scatter | solution.py:738
  329.2 77.9 %reduce-scatter.21.cloned.1.call-done = bf16[48,3072]{1,0:T(8,128)(2,1)} async-done(((bf16[768,3072]{1,0:T(8,128)(2,1)}), bf16[48,3072]{1,0:T(8,128)(2,1)}) %reduce-scatter.21.cloned.1.call-update) | async-done | bytes 294928 | tf_op jit(solution)/shard_map/reduce_scatter | solution.py:738
  407.2 78.5 %reduce-scatter.23.cloned.1.call-done = bf16[192,768]{1,0:T(8,128)(2,1)} async-done(((bf16[3072,768]{1,0:T(8,128)(2,1)}), bf16[192,768]{1,0:T(8,128)(2,1)}) %reduce-scatter.23.cloned.1.call-update) | async-done | bytes 294928 | tf_op jit(solution)/shard_map/reduce_scatter | solution.py:738
  485.7 0.6 dynamic-slice
  487.6 30.8 %dense_forward.1 = bf16[512,768]{1,0:T(8,128)(2,1)} custom-call(bf16[512,768]{1,0:T(8,128)(2,1)} %bitcast.27, bf16[512,768]{1,0:T(8,128)(2,1)} %get-tuple-element.47.q_ref, bf16[640,1536]{1,0:T(8,128)(2,1)} %get-tuple-element.50.kvx_ref, bf16[256,1536]{1,0:T(8,128)(2,1)} %get-tuple-element.51.pkvx_ref, bf16[768,768]{1,0:T(8,128)(2,1)} %wo_ref.3, ...), custom_call_target="tpu_custom_call" | custom-call | tf_op jit(solution)/shard_map/dense_forward/pallas_call | solution.py:712
  518.6 50.7 %all-reduce.9 = (bf16[768]{0:T(1024)(128)(2,1)S(1)}, bf16[768]{0:T(1024)(128)(2,1)S(1)}, bf16[768]{0:T(1024)(128)(2,1)S(1)}, bf16[768]{0:T(1024)(128)(2,1)S(1)},...) all-reduce(bf16[768]{0:T(1024)(128)(2,1)S(1)} %get-tuple-element.15, ...), channel_id=2, replica_groups=mesh['dp'=2,'seq'=16] {'seq'}, use_global_device_ids=true, to_apply=%region_0.0.clone | all-reduce | flops 9216 | bytes 36864
  569.9 0.8 copy.54
  570.7 28.5 %reduce-scatter.29.cloned.1.call-done = bf16[48,5]{1,0:T(8,128)(2,1)} async-done(((bf16[768,5]{1,0:T(8,128)(2,1)}), bf16[48,5]{1,0:T(8,128)(2,1)}) %reduce-scatter.29.cloned.1.call-update) | async-done | bytes 496
  599.3 0.8 copy.52
  600.0 5.0 all-reduce.10
  605.1 0.5 convert_element_type.104
  605.6 0.5 convert_element_type.106
  606.1 0.5 convert_element_type.110
  606.6 0.5 convert_element_type.114
  607.1 0.5 convert_element_type.118
  608.7 0.5 convert_element_type.133
  609.2 0.6 convert_element_type.129
  609.7 0.6 convert_element_type.119
  610.3 0.6 convert_element_type.120
  610.9 32.1 %all-reduce.14.cloned.1.call-done = (bf16[48,768]{0,1:T(8,128)(2,1)}, bf16[48,768]{0,1:T(8,128)(2,1)}, bf16[48,768]{1,0:T(8,128)(2,1)}, bf16[48,768]{1,0:T(8,128...) async-done(((bf16[48,768]{0,1:T(8,128)(2,1)}, bf16[48,768]{0,1:T(8,128)(2,1)}, bf16[48,768]{1,0:T(8,128)(2,1)}, bf16[48,768]{1,0:T(8,128)(2,1)}, ...) | async-done | bytes 884752 | tf_op jit(solution)/shard_map/psum | solution.py:739
  643.0 1.7 copy.45
  644.8 1.7 copy.46
  646.5 1.6 convert_element_type.108
  648.0 1.6 convert_element_type.116
  649.6 1.8 convert_element_type.126
  651.4 0.9 convert_element_type.131
  (60 shorter events, 3.5 us)
Async XLA Ops:
  7.2 139.7 %reduce-scatter.27.cloned.1.call-start = ((), (), s32[]{:S(2)}) async-start(), calls=%async_computation.13 | async-start | bytes 1253376
  83.7 124.0 %reduce-scatter.25.cloned.1.call-start = ((), (), s32[]{:S(2)}) async-start(), calls=%async_computation.12 | async-start | bytes 1253376
  83.8 1.6 copy-start.6
  83.8 1.6 copy-start.7
  85.3 1.6 copy-start.4
  85.3 1.6 copy-start.5
  85.3 183.2 %reduce-scatter.17.cloned.1.call-start = ((), (), s32[]{:S(2)}) async-start(), calls=%async_computation.8 | async-start | bytes 1253376 | tf_op jit(solution)/shard_map/reduce_scatter | solution.py:738
  86.9 1.7 copy-start.1
  86.9 242.3 %reduce-scatter.19.cloned.1.call-start = ((), (), s32[]{:S(2)}) async-start(), calls=%async_computation.9 | async-start | bytes 1253376 | tf_op jit(solution)/shard_map/reduce_scatter | solution.py:738
  88.5 0.9 copy-start.2
  88.5 318.7 %reduce-scatter.21.cloned.1.call-start = ((), (), s32[]{:S(2)}) async-start(), calls=%async_computation.10 | async-start | bytes 5013504 | tf_op jit(solution)/shard_map/reduce_scatter | solution.py:738
  92.9 1.1 copy-start
  92.9 1.2 copy-start.8
  92.9 392.8 %reduce-scatter.23.cloned.1.call-start = ((), (), s32[]{:S(2)}) async-start(), calls=%async_computation.11 | async-start | bytes 5013504 | tf_op jit(solution)/shard_map/reduce_scatter | solution.py:738
  97.6 0.8 copy-start.9
  97.6 388.1 %copy-start.12 = (u32[32]{0:T(128)S(1)}, u32[32]{0:T(128)}, u32[]{:S(2)}) copy-start(u32[32]{0:T(128)} %constant.5) | copy-start | bytes 388
  97.6 472.3 %reduce-scatter.31.cloned.1.call-start = ((), (), s32[]{:S(2)}) async-start(), calls=%async_computation.15 | async-start | bytes 208896
  99.3 500.0 %reduce-scatter.29.cloned.1.call-start = ((), (), s32[]{:S(2)}) async-start(), calls=%async_computation.14 | async-start | bytes 208896
  100.2 542.8 %all-reduce.14.cloned.1.call-start = ((), (), s32[]{:S(2)}) async-start(), calls=%async_computation.16 | async-start | bytes 2260992 | tf_op jit(solution)/shard_map/psum | solution.py:739
  487.6 30.8 %copy-start.10 = (f32[8,768]{1,0:T(8,128)S(1)}, f32[8,768]{1,0:T(8,128)}, u32[]{:S(2)}) copy-start(f32[8,768]{1,0:T(8,128)} %get-tuple-element.66) | copy-start | bytes 73732
  487.6 30.8 %copy-start.11 = (f32[1,3072]{1,0:T(1,128)S(1)}, f32[1,3072]{1,0:T(1,128)}, u32[]{:S(2)}) copy-start(f32[1,3072]{1,0:T(1,128)} %get-tuple-element.72) | copy-start | bytes 36868
  643.0 8.4 %copy-start.3 = (bf16[192,768]{1,0:T(8,128)(2,1)S(1)}, bf16[192,768]{1,0:T(8,128)(2,1)}, u32[]{:S(2)}) copy-start(bf16[192,768]{1,0:T(8,128)(2,1)} %get-tuple-element.146) | copy-start | bytes 884740
Sparse Core Ops, SparseCore 0:
  83.9 62.9 reduce-scatter.26
  150.5 57.1 reduce-scatter.24
  211.3 57.1 reduce-scatter.16
  272.0 57.1 reduce-scatter.18
  332.9 74.1 reduce-scatter.20
  410.9 74.7 reduce-scatter.22
  489.7 53.0 reduce-scatter.30
  546.9 52.3 reduce-scatter.28
  601.9 41.0 all-reduce.13

commit v2 on v1

--- a/solution.py
+++ b/solution.py
@@ -356,7 +356,7 @@
     x_ref, nrm_ref, q_ref, kvx_ref, pkvx_ref, slots_ref, cotr_ref, wo_ref, bo_ref, g2_ref, s2_ref,
     win_hbm, bin_ref, wout_hbm,
     actt_ref, gpre_ref, n2t_ref, cot_ref, mixt_ref, gbr_ref, nrmt_ref, gq_ref,
-    gnear_ref, gfar_ref, ghid_ref, gqd_ref, veca_ref, binsum_ref,
+    gnear_ref, gfar_ref, ghid_ref, gqd_ref, veca_ref,
     win_ref, wout_ref, wn_ref, wf_ref, qm_ref, mix_ref, gm_ref, nbias_ref, fbias_ref, n2_ref, acc_ref, bin_row, sems,
 ):
     s = lax.axis_index("seq")
@@ -377,7 +377,6 @@
     qm_ref[...] = (dot_tn(onehot_t, q_ref[...]) * (HD**-0.5)).astype(BF16)
     nrm_rows_t = jnp.transpose(nrm_rows).astype(BF16)
     store_rows(nrmt_ref, nrm_rows_t, groups)
-    live = jnp.where(slot_col >= 0, 1.0, 0.0)
     cot_ref[...] = jnp.where(slot_col >= 0, cotr_ref[...].astype(F32), 0.0).astype(BF16)
 
     nbias, fbias = window_biases(count, s, slot_col, near_keys, 0, far_keys, 0, tok)
@@ -412,6 +411,9 @@
     load_in.wait()
     load_out.wait()
 
+    half_tiles = FF // FF_TILE // 2
+    veca_ref[...] = jnp.zeros_like(veca_ref)
+
     def feed(t, carry):
         c = cols(t, FF_TILE)
         pre = dot_nn(n2_ref[...], win_ref[:, c]) + bin_row[:, c]
@@ -420,8 +422,8 @@
         slope = cdf + pre * (INV_SQRT_2PI * jnp.exp(-0.5 * pre * pre))
         grad_act = dot_nt(cot_ref[...], wout_ref[rows_at(t * FF_TILE, FF_TILE, FF_TILE), :])
         gpre = (grad_act * slope).astype(BF16)
-        gpre_ref[t] = gpre
-        binsum_ref[:, c] = col_sum(gpre.astype(F32))
+        gpre_ref[t // half_tiles, :, cols(t % half_tiles, FF_TILE)] = gpre
+        veca_ref[pl.ds(8 + t // 2, 1), cols(t % 2, FF_TILE)] = col_sum(gpre.astype(F32))
         acc_ref[...] += dot_nt(gpre, win_ref[:, c])
         return carry
 
@@ -461,7 +463,6 @@
     veca_ref[2:3, :] = col_sum(grad_n2 * n_two)
     veca_ref[3:4, :] = col_sum(grad_n2)
     veca_ref[4:5, :] = col_sum(cot)
-    veca_ref[5:8, :] = jnp.zeros((3, D), F32)
 
 
 def store_rows(ref, values, groups):
@@ -501,7 +502,7 @@
         functools.partial(masked_kernel, count, groups),
         out_shape=(
             struct(actt, BF16),
-            struct((tiles, cap, FF_TILE), BF16),
+            struct((2, cap, FF // 2), BF16),
             struct(rows_t, BF16),
             struct((cap, D), BF16),
             struct(rows_t, BF16),
@@ -512,11 +513,10 @@
             struct((far_keys, 2 * D), BF16),
             struct((tok, D), F32),
             struct((tok, D), BF16),
-            struct((8, D), F32),
-            struct((1, FF), F32),
+            struct((16, D), F32),
         ),
         in_specs=[VMEM] * 11 + [ANY, VMEM, ANY],
-        out_specs=(VMEM,) * 14,
+        out_specs=(VMEM,) * 13,
         scratch_shapes=[
             pltpu.VMEM((D, FF), BF16),
             pltpu.VMEM((FF, D), BF16),
@@ -583,7 +583,17 @@
 
     def weights(j, carry):
         c = cols(j, width)
-        gw_ref[j] = dot_tn(nrm_ref[...], gkv_ref[:, c]).astype(BF16)
+        product = dot_tn(nrm_ref[...], gkv_ref[:, c]).astype(BF16)
+        if groups is None:
+            gw_ref[j] = product
+        else:
+            tiles = D // width
+            shard = D // groups["seq"]
+            for k in range(groups["chips"]):
+                at = groups["place"](k) * shard
+                for core in range(2):
+                    start = (2 * k + core) * shard
+                    gw_ref[core, j // tiles, at : at + shard, cols(j % tiles, width)] = product[start : start + shard]
         return carry
 
     lax.fori_loop(0, 2 * D // width, weights, 0)
@@ -623,7 +633,7 @@
         functools.partial(finish_kernel, groups),
         out_shape=(
             struct((tok, D), F32),
-            struct((6, D, 256), BF16),
+            struct((6, D, 256) if groups is None else (2, 2, D // 2, D), BF16),
             struct((16, D), F32),
         ),
         in_specs=[VMEM] * 18,
@@ -640,97 +650,391 @@
     )(x, nrm, g1, kvx, gnear, gfar, *edges, gqd, ghid, wq, wk, wv, pk, pv)
 
 
-def dense_kernel(
+def dense_parts(
     count,
     x_ref, q_ref, kvx_ref, pkvx_ref, wo_ref, bo_ref, g2_ref, s2_ref, win_hbm, bin_ref, wout_hbm, bout_ref,
     out_ref,
     win_ref, wout_ref, nbias_ref, fbias_ref, mix_ref, n2_ref, acc_ref, bin_row, sems,
 ):
-    s = lax.axis_index("seq")
-    bin_row[...] = row_of(bin_ref)
     tok = x_ref.shape[0]
-    load_in = pltpu.make_async_copy(win_hbm, win_ref, sems.at[0])
-    load_out = pltpu.make_async_copy(wout_hbm, wout_ref, sems.at[1])
-    load_in.start()
-    load_out.start()
     block = 128
     near_keys, far_keys = block + WIN, (block + POOL_SPAN) // STRIDE
     step = block // STRIDE
     blocks = tok // block
+    load_in = pltpu.make_async_copy(win_hbm, win_ref, sems.at[0])
+    load_out = pltpu.make_async_copy(wout_hbm, wout_ref, sems.at[1])
+
+    def begin():
+        s = lax.axis_index("seq")
+        load_in.start()
+        load_out.start()
+        bin_row[...] = row_of(bin_ref)
+        for b in range(blocks):
+            pos = b * block + lax.broadcasted_iota(jnp.int32, (block, 1), 0)
+            nb, fb = window_biases(count, s, pos, near_keys, b * block, far_keys, b * step, tok)
+            nbias_ref[b] = nb
+            fbias_ref[b] = fb
+
+    def attend(b):
+        low, high = head_masks()
+        rows = pl.ds(b * block, block)
+        near = pl.ds(b * block, near_keys)
+        far = pl.ds(b * step, far_keys)
+
+        def pair(p, carry):
+            c, cv = cols(p), cols(p + PAIRS)
+            qs = stack_pair(q_ref[rows, c] * jnp.asarray(HD**-0.5, BF16), low, high)
+            nb, fb = nbias_ref[b], fbias_ref[b]
+            near_w = softmax_rows(dot_nt(qs, kvx_ref[near, c]) + jnp.concatenate([nb, nb], axis=0))
+            far_w = softmax_rows(dot_nt(qs, pkvx_ref[far, c]) + jnp.concatenate([fb, fb], axis=0))
+            out = dot_nn(near_w.astype(BF16), kvx_ref[near, cv]) + dot_nn(far_w.astype(BF16), pkvx_ref[far, cv])
+            mix_ref[rows, c] = merge_pair(out).astype(BF16)
+            return carry
+
+        lax.fori_loop(0, PAIRS, pair, 0)
+
+    def residual():
+        def one(b, carry):
+            rows = rows_at(b * block, block, block)
+            hidden = x_ref[rows, :].astype(F32) + dot_nn(mix_ref[rows, :], wo_ref[...]) + row_of(bo_ref)
+            n, _ = norm_stats(hidden)
+            n2_ref[rows, :] = (n * row_of(g2_ref) + row_of(s2_ref)).astype(BF16)
+            acc_ref[rows, :] = hidden + row_of(bout_ref)
+            return carry
+
+        lax.fori_loop(0, blocks, one, 0)
+        load_in.wait()
+        load_out.wait()
+
+    def feed(first, last):
+        high_rows = 256
+        halves = tok // high_rows
+
+        def one(i, carry):
+            t, b = i // halves, i % halves
+            c = cols(t, FF_TILE)
+            rows = rows_at(b * high_rows, high_rows, high_rows)
+            pre = dot_nn(n2_ref[rows, :], win_ref[:, c]) + bin_row[:, c]
+            act = (pre * (0.5 * (1.0 + lax.erf(pre * SQRT_HALF)))).astype(BF16)
+            acc_ref[rows, :] += dot_nn(act, wout_ref[rows_at(t * FF_TILE, FF_TILE, FF_TILE), :])
+            return carry
+
+        lax.fori_loop(first * halves, last * halves, one, 0)
+
+    def end():
+        out_ref[...] = acc_ref[...].astype(BF16)
+
+    return begin, attend, blocks, residual, feed, end
+
+
+def dense_kernel(count, *refs):
+    begin, attend, blocks, residual, feed, end = dense_parts(count, *refs)
+    begin()
     for b in range(blocks):
-        pos = b * block + lax.broadcasted_iota(jnp.int32, (block, 1), 0)
-        nb, fb = window_biases(count, s, pos, near_keys, b * block, far_keys, b * step, tok)
-        nbias_ref[b] = nb
-        fbias_ref[b] = fb
-    low, high = head_masks()
-
-    def attend(i, carry):
-        b, p = i // PAIRS, i % PAIRS
-        c, cv = cols(p), cols(p + PAIRS)
-        rows = rows_at(b * block, block, block)
-        near = rows_at(b * block, near_keys, block)
-        far = rows_at(b * step, far_keys, step)
-        qs = stack_pair(q_ref[rows, c] * jnp.asarray(HD**-0.5, BF16), low, high)
-        nb, fb = nbias_ref[b], fbias_ref[b]
-        near_w = softmax_rows(dot_nt(qs, kvx_ref[near, c]) + jnp.concatenate([nb, nb], axis=0))
-        far_w = softmax_rows(dot_nt(qs, pkvx_ref[far, c]) + jnp.concatenate([fb, fb], axis=0))
-        out = dot_nn(near_w.astype(BF16), kvx_ref[near, cv]) + dot_nn(far_w.astype(BF16), pkvx_ref[far, cv])
-        mix_ref[rows, c] = merge_pair(out).astype(BF16)
-        return carry
-
-    lax.fori_loop(0, blocks * PAIRS, attend, 0)
-
-    def residual(b, carry):
-        rows = rows_at(b * block, block, block)
-        hidden = x_ref[rows, :].astype(F32) + dot_nn(mix_ref[rows, :], wo_ref[...]) + row_of(bo_ref)
-        n, _ = norm_stats(hidden)
-        n2_ref[rows, :] = (n * row_of(g2_ref) + row_of(s2_ref)).astype(BF16)
-        acc_ref[rows, :] = hidden + row_of(bout_ref)
-        return carry
-
-    lax.fori_loop(0, blocks, residual, 0)
-    load_in.wait()
-    load_out.wait()
-    high_rows = 256
-
-    def feed(i, carry):
-        t, b = i // (tok // high_rows), i % (tok // high_rows)
-        c = cols(t, FF_TILE)
-        rows = rows_at(b * high_rows, high_rows, high_rows)
-        pre = dot_nn(n2_ref[rows, :], win_ref[:, c]) + bin_row[:, c]
-        act = (pre * (0.5 * (1.0 + lax.erf(pre * SQRT_HALF)))).astype(BF16)
-        acc_ref[rows, :] += dot_nn(act, wout_ref[rows_at(t * FF_TILE, FF_TILE, FF_TILE), :])
-        return carry
-
-    lax.fori_loop(0, FF // FF_TILE * (tok // high_rows), feed, 0)
-    out_ref[...] = acc_ref[...].astype(BF16)
+        attend(b)
+    residual()
+    feed(0, FF // FF_TILE)
+    end()
+
+
+def dense_scratch(tok):
+    blocks = tok // 128
+    return [
+        pltpu.VMEM((D, FF), BF16),
+        pltpu.VMEM((FF, D), BF16),
+        pltpu.VMEM((blocks, 128, 128 + WIN), F32),
+        pltpu.VMEM((blocks, 128, (128 + POOL_SPAN) // STRIDE), F32),
+        pltpu.VMEM((tok, D), BF16),
+        pltpu.VMEM((tok, D), BF16),
+        pltpu.VMEM((tok, D), F32),
+        pltpu.VMEM((1, FF), F32),
+        pltpu.SemaphoreType.DMA((2,)),
+    ]
 
 
 def dense(count, x, q, kvx, pkvx, wo, bo, g2, s2, w_in, b_in, w_out, b_out):
     tok = x.shape[0]
-    blocks = tok // 128
     return pl.pallas_call(
         functools.partial(dense_kernel, count),
         out_shape=struct((tok, D), BF16),
         in_specs=[VMEM] * 8 + [ANY, VMEM, ANY, VMEM],
         out_specs=VMEM,
-        scratch_shapes=[
-            pltpu.VMEM((D, FF), BF16),
-            pltpu.VMEM((FF, D), BF16),
-            pltpu.VMEM((blocks, 128, 128 + WIN), F32),
-            pltpu.VMEM((blocks, 128, (128 + POOL_SPAN) // STRIDE), F32),
-            pltpu.VMEM((tok, D), BF16),
-            pltpu.VMEM((tok, D), BF16),
-            pltpu.VMEM((tok, D), F32),
-            pltpu.VMEM((1, FF), F32),
-            pltpu.SemaphoreType.DMA((2,)),
-        ],
+        scratch_shapes=dense_scratch(tok),
         compiler_params=pltpu.CompilerParams(vmem_limit_bytes=VMEM_LIMIT),
         name="dense_forward",
     )(x, q, kvx, pkvx, wo, bo, g2, s2, w_in, b_in, w_out, b_out)
 
 
-def plain_reduce(actt, gpre, n2t, cot, mixt, gbr, nrmt, gq, gw, veca, vecb, binsum):
+SEQ, CHIPS, NZ = 16, 8, 4
+SH, SF, PART = D // SEQ, FF // SEQ, FF // SEQ // 2
+
+
+def place(k):
+    return (k % 2) * NZ + k // 2
+
+
+GROUPS = {"seq": SEQ, "chips": CHIPS, "place": place}
+COPIES = 64
+
+
+def reduce_kernel(
+    count,
+    actt, gpre, n2t, cot, mixt, gbr, nrmt, gq, gw, veca, vecb,
+    x_ref, q_ref, kvx_ref, pkvx_ref, wo_ref, bo_ref, g2_ref, s2_ref, win_hbm, bin_ref, wout_hbm, bout_ref,
+    out_ref, f_out, f_in, f_att, f_vec,
+    a_all, c_all, n_all, p_all, a_fwd, n_fwd,
+    m_all, b_all, r_all, g_all, kv_rx, va_rx, vb_rx, vs, vy_rx, vx_rx, vz_rx, vsum,
+    att, att_y, att_x, att_xr, att_z, att_zr,
+    wo_g, wo_y, wo_z, wo_zr, wi_g, wi_y, wi_z, wi_zr,
+    send, recv, *dense_refs,
+):
+    cap = cot.shape[0]
+    d, s = lax.axis_index("dp"), lax.axis_index("seq")
+    c, chip = s % 2, s // 2
+    y, z = chip % 2, chip // 2
+    e, f, w = 1 - c, 1 - d, 1 - y
+    core_dev = (d, chip * 2 + e)
+    x_dev = (f, s)
+    y_dev = (d, z * 4 + w * 2 + c)
+    z_at = [(z + t) % NZ for t in range(1, NZ)]
+    z_dev = [(d, zt * 4 + y * 2 + c) for zt in z_at]
+    barrier = pltpu.get_barrier_semaphore()
+    peers = [core_dev, x_dev, y_dev] + z_dev
+    for peer in peers:
+        pl.semaphore_signal(barrier, inc=1, device_id=peer, device_id_type=MESH)
+    pl.semaphore_wait(barrier, len(peers))
+    used = [0]
+    started = []
+
+    def go(src, dst, device):
+        i = used[0]
+        used[0] += 1
+        copy = remote(src, dst, send.at[i], recv.at[i], device)
+        copy.start()
+        started.append(copy)
+        return copy
+
+    def arrive(copies):
+        for copy in copies:
+            copy.wait_recv()
+
+    def lane(g):
+        return pl.ds(128 * g, 128)
+
+    def slab(g):
+        return pl.ds(cap * g, cap)
+
+    begin, attend, blocks, residual, feed, end = dense_parts(
+        count, x_ref, q_ref, kvx_ref, pkvx_ref, wo_ref, bo_ref, g2_ref, s2_ref, win_hbm, bin_ref, wout_hbm,
+        bout_ref, out_ref, *dense_refs
+    )
+
+    out_x = [
+        go(actt.at[c, f], a_all.at[:, lane(2)], x_dev),
+        go(actt.at[e, f], a_fwd, x_dev),
+        go(cot, c_all.at[slab(2)], x_dev),
+    ]
+    out_core = [go(actt.at[e, d], a_all.at[:, lane(1)], core_dev), go(cot, c_all.at[slab(1)], core_dev)]
+    att_core = [
+        go(gw.at[e], kv_rx, core_dev),
+        go(mixt.at[e], m_all.at[:, lane(1)], core_dev),
+        go(gbr, b_all.at[slab(1)], core_dev),
+        go(nrmt.at[e], r_all.at[:, lane(1)], core_dev),
+        go(gq, g_all.at[slab(1)], core_dev),
+        go(veca, va_rx, core_dev),
+        go(vecb, vb_rx, core_dev),
+    ]
+    in_x = [
+        go(n2t.at[c], n_all.at[:, lane(2)], x_dev),
+        go(n2t.at[e], n_fwd, x_dev),
+        go(gpre.at[f], p_all.at[slab(2)], x_dev),
+    ]
+    in_core = [go(n2t.at[e], n_all.at[:, lane(1)], core_dev), go(gpre.at[d], p_all.at[slab(1)], core_dev)]
+    a_all[:, lane(0)] = actt[c, d]
+    c_all[slab(0), :] = cot[...]
+    n_all[:, lane(0)] = n2t[c]
+    p_all[slab(0), :] = gpre[d]
+    m_all[:, lane(0)] = mixt[c]
+    b_all[slab(0), :] = gbr[...]
+    r_all[:, lane(0)] = nrmt[c]
+    g_all[slab(0), :] = gq[...]
+    begin()
+
+    arrive(att_core)
+    rows = NZ * SH
+
+    def halves(ref, values, g):
+        ref[0, g] = values[:rows].astype(BF16)
+        ref[1, g] = values[rows:].astype(BF16)
+
+    halves(att, dot_nn(m_all[...], b_all[...]), 0)
+    halves(att, dot_nn(r_all[...], g_all[...]), 1)
+    for g in range(2):
+        for half in range(2):
+            part = pl.ds(half * rows, rows)
+            att[half, 2 + g] = (gw[c, g, part].astype(F32) + kv_rx[g, part].astype(F32)).astype(BF16)
+    vs[0:16, :] = (veca[...] + va_rx[...]).astype(BF16)
+    vs[16:32, :] = (vecb[...] + vb_rx[...]).astype(BF16)
+    attend(0)
+    att_to_y = [go(att.at[w], att_y, y_dev), go(vs, vy_rx, y_dev)]
+    attend(1)
+
+    arrive(out_x)
+    out_fwd = [go(a_fwd, a_all.at[:, lane(3)], core_dev), go(c_all.at[slab(2)], c_all.at[slab(3)], core_dev)]
+    attend(2)
+    arrive(out_core + out_fwd)
+    quarter = NZ * PART // 2
+
+    def out_product(i, carry):
+        r = rows_at(i * quarter, quarter, quarter)
+        wo_g[i // 2, rows_at((i % 2) * quarter, quarter, quarter), :] = dot_nn(a_all[r, :], c_all[...]).astype(BF16)
+        return carry
+
+    lax.fori_loop(0, 4, out_product, 0)
+    attend(3)
+    out_to_y = [go(wo_g.at[w], wo_y, y_dev)]
+    arrive(in_x)
+    in_fwd = [go(n_fwd, n_all.at[:, lane(3)], core_dev), go(p_all.at[slab(2)], p_all.at[slab(3)], core_dev)]
+    residual()
+    arrive(in_core + in_fwd)
+
+    def in_product(i, carry):
+        r = rows_at((i // 4) * rows, rows, rows)
+        cc = cols(i % 4, FF // 8)
+        wi_g[i // 4, :, cc] = dot_nn(n_all[r, :], p_all[:, cc]).astype(BF16)
+        return carry
+
+    lax.fori_loop(0, 8, in_product, 0)
+    feed(0, 2)
+    in_to_y = [go(wi_g.at[w], wi_y, y_dev)]
+
+    arrive(att_to_y)
+    wide = D // 2
+    for g in range(4):
+        total = att[y, g].astype(F32) + att_y[g].astype(F32)
+        att_x[0, g] = total[:, :wide].astype(BF16)
+        att_x[1, g] = total[:, wide:].astype(BF16)
+    vs2 = vsum.at[0]
+    vs2[...] = (vs[...].astype(F32) + vy_rx[...].astype(F32)).astype(BF16)
+    feed(2, 4)
+    att_to_x = [go(att_x.at[f], att_xr, x_dev), go(vs2, vx_rx, x_dev)]
+    feed(4, 6)
+
+    arrive(out_to_y)
+    for zz in range(NZ):
+        r = pl.ds(zz * PART, PART)
+        wo_z[zz] = (wo_g[y, r].astype(F32) + wo_y[r].astype(F32)).astype(BF16)
+    feed(6, 7)
+    out_to_z = [go(wo_z.at[z_at[t]], wo_zr.at[t], z_dev[t]) for t in range(NZ - 1)]
+    arrive(att_to_x)
+    for zz in range(NZ):
+        r = pl.ds(zz * SH, SH)
+        for g in range(4):
+            att_z[zz, g] = (att_x[d, g, r].astype(F32) + att_xr[g, r].astype(F32)).astype(BF16)
+    vs3 = vsum.at[1]
+    vs3[...] = (vs2[...].astype(F32) + vx_rx[...].astype(F32)).astype(BF16)
+    feed(7, 8)
+    att_to_z = [go(att_z.at[z_at[t]], att_zr.at[t], z_dev[t]) for t in range(NZ - 1)]
+    vec_to_z = [go(vs3, vz_rx.at[t], z_dev[t]) for t in range(NZ - 1)]
+    end()
+    arrive(in_to_y)
+    for zz in range(NZ):
+        r = pl.ds(zz * SH, SH)
+        wi_z[zz] = (wi_g[y, r].astype(F32) + wi_y[r].astype(F32)).astype(BF16)
+    in_to_z = [go(wi_z.at[z_at[t]], wi_zr.at[t], z_dev[t]) for t in range(NZ - 1)]
+
+    def gathered(own, parts):
+        total = own.astype(F32)
+        for t in range(NZ - 1):
+            total = total + parts[t].astype(F32)
+        return total
+
+    arrive(out_to_z)
+    f_out[d] = gathered(wo_z[z], wo_zr).astype(BF16)
+    last = [go(f_out.at[d], f_out.at[d], x_dev)]
+    arrive(att_to_z)
+    f_att[d] = gathered(att_z[z], att_zr).astype(BF16)
+    last.append(go(f_att.at[d], f_att.at[d], x_dev))
+    arrive(vec_to_z)
+    f_vec[...] = gathered(vs3[...], vz_rx)
+    arrive(in_to_z)
+    f_in[d] = gathered(wi_z[z], wi_zr).astype(BF16)
+    last.append(go(f_in.at[d], f_in.at[d], x_dev))
+    arrive(last)
+    for copy in started:
+        copy.wait_send()
+
+
+def reduce_all(count, grads, dense_args):
+    cap = grads[3].shape[0]
+    tok = dense_args[0].shape[0]
+    half, rows = D // 2, NZ * SH
+    b16 = functools.partial(pltpu.VMEM, dtype=BF16)
+    return pl.pallas_call(
+        functools.partial(reduce_kernel, count),
+        out_shape=(
+            struct((tok, D), BF16),
+            struct((2, PART, D), BF16),
+            struct((2, SH, FF // 2), BF16),
+            struct((2, 4, SH, D // 2), BF16),
+            struct((32, D), F32),
+        ),
+        in_specs=[VMEM] * 11 + [VMEM] * 8 + [ANY, VMEM, ANY, VMEM],
+        out_specs=(VMEM,) * 5,
+        scratch_shapes=[
+            b16((FF // 4, 4 * cap)), b16((4 * cap, D)), b16((half, 4 * cap)), b16((4 * cap, FF // 2)),
+            b16((FF // 4, cap)), b16((half, cap)),
+            b16((half, 2 * cap)), b16((2 * cap, D)), b16((half, 2 * cap)), b16((2 * cap, D)),
+            b16((2, half, D)), pltpu.VMEM((16, D), F32), pltpu.VMEM((16, D), F32),
+            b16((32, D)), b16((32, D)), b16((32, D)), b16((NZ - 1, 32, D)), b16((2, 32, D)),
+            b16((2, 4, rows, D)), b16((4, rows, D)), b16((2, 4, rows, half)), b16((4, rows, half)),
+            b16((NZ, 4, SH, half)), b16((NZ - 1, 4, SH, half)),
+            b16((2, NZ * PART, D)), b16((NZ * PART, D)), b16((NZ, PART, D)), b16((NZ - 1, PART, D)),
+            b16((2, rows, FF // 2)), b16((rows, FF // 2)), b16((NZ, SH, FF // 2)), b16((NZ - 1, SH, FF // 2)),
+            pltpu.SemaphoreType.DMA((COPIES,)), pltpu.SemaphoreType.DMA((COPIES,)),
+        ] + dense_scratch(tok),
+        compiler_params=pltpu.CompilerParams(
+            collective_id=2, has_side_effects=True, vmem_limit_bytes=VMEM_LIMIT
+        ),
+        name="reduce",
+    )(*grads, *dense_args)
+
+
+def unpack_kernel(f_out, f_in, f_att, f_vec, g1, s1, wq, bq, wk, wv, bv, wo, bo, pk, pv, g2, s2, wi, bi, wu, bu):
+    s = lax.axis_index("seq")
+    wu[0:PART, :] = f_out[0].astype(F32)
+    wu[PART : 2 * PART, :] = f_out[1].astype(F32)
+    for h in range(2):
+        wi[:, h * (FF // 2) : (h + 1) * (FF // 2)] = f_in[h].astype(F32)
+        for g, ref in enumerate((wo, wq, wk, wv)):
+            ref[:, h * (D // 2) : (h + 1) * (D // 2)] = f_att[h, g].astype(F32)
+    own = pltpu.roll(f_vec[...], lax.rem(D - SH * s, D), 1)
+    for row, ref in ((0, bq), (1, bo), (2, g2), (3, s2), (4, bu), (16, g1), (17, s1), (18, bv)):
+        ref[...] = own[row, :SH]
+    pk[...] = own[19:24, :SH]
+    pv[...] = own[24:29, :SH]
+    rows = lax.broadcasted_iota(jnp.int32, (4, 1), 0)
+    part = jnp.sum(jnp.where(rows == s // 4, f_vec[8:12, :], 0.0), axis=0, keepdims=True)
+    part = jnp.broadcast_to(part, (8, D))
+    bi[...] = pltpu.roll(part, lax.rem(D - SF * (s % 4), D), 1)[0, :SF]
+
+
+def unpack(f_out, f_in, f_att, f_vec):
+    one, square, taps = struct((SH,), F32), struct((SH, D), F32), struct((KERNEL, SH), F32)
+    return pl.pallas_call(
+        unpack_kernel,
+        out_shape=(
+            one, one, square, one, square, square, one, square, one, taps, taps, one, one,
+            struct((SH, FF), F32), struct((SF,), F32), struct((SF, D), F32), one,
+        ),
+        in_specs=[VMEM] * 4,
+        out_specs=(VMEM,) * 17,
+        compiler_params=pltpu.CompilerParams(vmem_limit_bytes=VMEM_LIMIT),
+        name="unpack",
+    )(f_out, f_in, f_att, f_vec)
+
+
+def plain_reduce(actt, gpre, n2t, cot, mixt, gbr, nrmt, gq, gw, veca, vecb):
     def prod(a, b):
         return jnp.dot(a, b, preferred_element_type=F32)
 
@@ -748,7 +1052,7 @@
     return (
         total(vecb[0]), total(vecb[1]), w_q, total(veca[0]), w_k, w_v, total(vecb[2]), w_o, total(veca[1]),
         total(vecb[3:8], 1), total(vecb[8:13], 1), total(veca[2]), total(veca[3]),
-        w_in, total(binsum[0]), w_out, total(veca[4]),
+        w_in, total(veca[8:12].reshape(FF)), w_out, total(veca[4]),
     )
 
 
@@ -757,12 +1061,12 @@
     pool_key, pool_value, gain_two, shift_two, w_in, b_in, w_out, b_out, mask_slots, cot_rows,
 ):
     x = x_input[0]
-    groups = None
+    groups = GROUPS if (n_dp, n_seq) == (2, SEQ) else None
     nrm, q, kv, pkv = project(
         x, gain_one, shift_one, w_query, b_query, w_key, w_value, b_value, pool_key, pool_value
     )
     kvx, pkvx = halo(n_seq, kv, pkv, pool_key, pool_value)
-    (actt, gpre, n2t, cot, mixt, gbr, nrmt, gq, gnear, gfar, ghid, gqd, veca, binsum) = masked(
+    (actt, gpre, n2t, cot, mixt, gbr, nrmt, gq, gnear, gfar, ghid, gqd, veca) = masked(
         n_seq, groups, x, nrm, q, kvx, pkvx, mask_slots, cot_rows[0, 0],
         w_attn_out, b_attn_out, gain_two, shift_two, w_in, b_in, w_out,
     )
@@ -770,11 +1074,15 @@
     grad_input, gw, vecb = finish(
         groups, x, nrm, gain_one, kvx, gnear, gfar, edges, gqd, ghid, w_query, w_key, w_value, pool_key, pool_value
     )
-    output = dense(
-        n_seq, x, q, kvx, pkvx, w_attn_out, b_attn_out, gain_two, shift_two, w_in, b_in, w_out, b_out
-    )
-    reduced = plain_reduce(actt, gpre, n2t, cot, mixt, gbr, nrmt, gq, gw, veca, vecb, binsum)
-    return (output[None], grad_input[None]) + reduced
+    grads = (actt, gpre, n2t, cot, mixt, gbr, nrmt, gq, gw, veca, vecb)
+    dense_args = (x, q, kvx, pkvx, w_attn_out, b_attn_out, gain_two, shift_two, w_in, b_in, w_out, b_out)
+    if groups is None:
+        output = dense(n_seq, *dense_args)
+        reduced = plain_reduce(*grads)
+    else:
+        output, *finals = reduce_all(n_seq, grads, dense_args)
+        reduced = unpack(*finals)
+    return (output[None], grad_input[None]) + tuple(reduced)
 
 
 def solution(mesh):

time: 661 us -> 189 us (0.29)
  waiting for transfers between devices: 443 us -> 0 us
  Pallas kernels: 101 us -> 185 us
  blocking collectives: 55.7 us -> 0 us
  local copies, waits for them, and re-layouts: 21.8 us -> 2.06 us
  between operations: 15.4 us -> 0.69 us
  other arithmetic: 11.7 us -> 0 us
  matrix products: 10 us -> 0 us
    reduce_scatter x4 -> x0, waiting for transfers between devices: 276 us -> none  [total(): lax.psum_scatter(value.astype(BF16), 'seq', scatter_dimension=axis, tiled...]
    unnamed x13 -> x0, waiting for transfers between devices: 134 us -> none
    pallas_call x1 -> x2, Pallas kernels: 30.8 us -> 115 us  [the longest x1 113 us: reduce_all(): pl.pallas_call(functools.partial(reduce_kernel, count), out_shape=(struct...]
    unnamed x1 -> x0, blocking collectives: 50.7 us -> none
    psum x1 -> x0, waiting for transfers between devices: 32.1 us -> none  [total(): return lax.psum(part, 'dp').astype(F32)]
    unnamed x46 -> x1, local copies, waits for them, and re-layouts: 17.3 us -> 2.06 us
    convert_element_type x16 -> x0, other arithmetic: 11.7 us -> none  [the longest x15 11.6 us: total(): return lax.psum(part, 'dp').astype(F32)]
    dot_general x4 -> x0, matrix products: 10 us -> none  [prod(): return jnp.dot(a, b, preferred_element_type=F32)]
  transfers between devices with their start and end apart: 9 -> 0, of which waited for: 8 -> 0; matrix products, arithmetic and copies ran while one was open for 4% -> 0% of each run, Pallas kernels for 5% -> 0%
where the time goes in v2:
time: 189 us; the launch traced here: 188 us
  Pallas kernels  185 us (98%)
  local copies, waits for them, and re-layouts  2.06 us (1%)
    pallas_call x1, Pallas kernels, reduce_all(): pl.pallas_call(functools.partial(reduce_kernel, count), out_shape=(struct...  113 us
    pallas_call x1, Pallas kernels, masked(): pl.pallas_call(functools.partial(masked_kernel, count, groups), out_shape...  23.2 us
    pallas_call x1, Pallas kernels, finish(): pl.pallas_call(functools.partial(finish_kernel, groups), out_shape=(struc...  15 us
    pallas_call x1, Pallas kernels, halo_back(): pl.pallas_call(functools.partial(halo_back_kernel, count), out_shape=(str...  13 us
    pallas_call x1, Pallas kernels, halo(): pl.pallas_call(functools.partial(halo_kernel, count), out_shape=(struct((...  11.5 us
    pallas_call x1, Pallas kernels, project(): pl.pallas_call(project_kernel, out_shape=(struct((tok, D), BF16), struct(...  7.57 us

profile of v2, /device:TPU:8, one launch (start us, length us, event | category | flops | bytes accessed | tf_op | source)
XLA Modules:
  0.0 188.2 jit_solution(2780424076746399710)
XLA Ops:
  0.7 7.6 %project.1 = (bf16[512,768]{1,0:T(8,128)(2,1)}, bf16[512,768]{1,0:T(8,128)(2,1)}, bf16[512,1536]{1,0:T(8,128)(2,1)}, bf16[128,1536]{1,0:T(8,128)(2,1)}) custom-call(bf16[512,768]{1,0:T(8,128)(2,1)} %bitcast.4, bf16[768]{0:T(1024)(128)(2,1)} %g1_ref.1, bf16[768]{0:T(1024)(128)(2,1)} %s_ref.1, bf16[768,768]{1,0:T(8,128)(2,1)} %wq_ref.3, ...), custom_call_target="tpu_custom_call" | custom-call | tf_op jit(solution)/shard_map/project/pallas_call | solution.py:138
  8.2 11.5 %halo.1 = (bf16[640,1536]{1,0:T(8,128)(2,1)}, bf16[256,1536]{1,0:T(8,128)(2,1)}) custom-call(bf16[512,1536]{1,0:T(8,128)(2,1)} %get-tuple-element.70.kv_ref, bf16[128,1536]{1,0:T(8,128)(2,1)} %get-tuple-element.71.pkv_ref, bf16[5,768]{1,0:T(8,128)(2,1)} %pk_ref.5, bf16[5,768]{1,0:T(8,128)(2,1)} %pv_ref.5), custom_call_target="tpu_custom_call" | custom-call | tf_op jit(solution)/shard_map/halo/pallas_call | solution.py:253
  19.8 23.2 %masked_rows.1 = (bf16[2,2,768,128]{3,2,1,0:T(8,128)(2,1)}, bf16[2,128,1536]{2,1,0:T(8,128)(2,1)}, bf16[2,384,128]{2,1,0:T(8,128)(2,1)}, bf16[128,768]{1,0:T(8,1...) custom-call(bf16[512,768]{1,0:T(8,128)(2,1)} %bitcast.5, ...), custom_call_target="tpu_custom_call" | custom-call | tf_op jit(solution)/shard_map/masked_rows/pallas_call | solution.py:501
  43.0 13.0 %halo_back.1 = (bf16[64,1536]{1,0:T(8,128)(2,1)}, bf16[64,1536]{1,0:T(8,128)(2,1)}, bf16[64,1536]{1,0:T(8,128)(2,1)}, bf16[64,1536]{1,0:T(8,128)(2,1)}, bf16[16,1536]{1,0:T(8,128)(2,1)}) custom-call(bf16[640,1536]{1,0:T(8,128)(2,1)} %get-tuple-element.82.near_ref.gnear_ref, bf16[256,1536]{1,0:T(8,128)(2,1)} %get-tuple-element.83.far_ref.gfar_ref), custom_call_target="tpu_custom_call" | custom-call | tf_op jit(solution)/shard_map/halo_back/pallas_call | solution.py:320
  56.0 15.0 %finish.1 = (f32[512,768]{1,0:T(8,128)}, bf16[2,2,384,768]{3,2,1,0:T(8,128)(2,1)}, f32[16,768]{1,0:T(8,128)}) custom-call(bf16[512,768]{1,0:T(8,128)(2,1)} %bitcast.6, bf16[512,768]{1,0:T(8,128)(2,1)} %get-tuple-element.68.nrm_ref, bf16[768]{0:T(1024)(128)(2,1)} %g1_ref.1, bf16[640,1536]{1,0:T(8,128)(2,1)} %get-tuple-element.72.kvx_ref, ...), custom_call_target="tpu_custom_call" | custom-call | tf_op jit(solution)/shard_map/finish/pallas_call | solution.py:632
  71.0 112.7 %reduce.1 = (bf16[512,768]{1,0:T(8,128)(2,1)}, bf16[2,96,768]{2,1,0:T(8,128)(2,1)}, bf16[2,48,1536]{2,1,0:T(8,128)(2,1)}, bf16[2,4,48,384]{3,2,1,0:T(8,128)(2,1)}, f32[32,768]{1,0:T(8,128)}) custom-call(bf16[2,2,768,128]{3,2,1,0:T(8,128)(2,1)} %get-tuple-element.74.actt, bf16[2,128,1536]{2,1,0:T(8,128)(2,1)} %get-tuple-element.75.gpre, ...), custom_call_target="tpu_custom_call" | custom-call | tf_op jit(solution)/shard_map/reduce/pallas_call | solution.py:973
  183.7 2.4 %unpack.1 = (f32[48]{0:T(128)}, f32[48]{0:T(128)}, f32[48,768]{1,0:T(8,128)}, f32[48]{0:T(128)}, f32[48,768]{1,0:T(8,128)}, /*index=5*/f32[48,768]{1,0:T(8,128)}...) custom-call(bf16[2,96,768]{2,1,0:T(8,128)(2,1)} %get-tuple-element.9, ...), custom_call_target="tpu_custom_call" | custom-call | tf_op jit(solution)/shard_map/unpack/pallas_call | solution.py:1024
  186.2 2.1 %copy.40 = bf16[1,512,768]{2,1,0:T(8,128)(2,1)} copy(bf16[1,512,768]{2,1,0:T(8,128)(2,1)} %bitcast.8) | data formatting | bytes 1572864

commit v3 on v2

--- a/solution.py
+++ b/solution.py
@@ -99,12 +99,14 @@
 
 def project_kernel(
     x_ref, g_ref, s_ref, wq_ref, bq_ref, wk_ref, wv_ref, bv_ref, pk_ref, pv_ref,
-    nrm_ref, q_ref, kv_ref, pkv_ref, lanes,
+    nrmt_ref, q_ref, kv_ref, pkv_ref, nrm_ref, lanes,
 ):
     tok = x_ref.shape[0]
     pooled = tok // STRIDE
     n, _ = norm_stats(x_ref[...].astype(F32))
-    nrm_ref[...] = (n * row_of(g_ref) + row_of(s_ref)).astype(BF16)
+    normed = n * row_of(g_ref) + row_of(s_ref)
+    nrm_ref[...] = normed.astype(BF16)
+    nrmt_ref[...] = jnp.transpose(normed).astype(BF16)
     width = 256
 
     def tile(j, carry):
@@ -138,14 +140,14 @@
     return pl.pallas_call(
         project_kernel,
         out_shape=(
-            struct((tok, D), BF16),
+            struct((D, tok), BF16),
             struct((tok, D), BF16),
             struct((tok, 2 * D), BF16),
             struct((tok // STRIDE, 2 * D), BF16),
         ),
         in_specs=[VMEM] * 10,
         out_specs=(VMEM,) * 4,
-        scratch_shapes=[pltpu.VMEM((tok + 16, 128), F32)],
+        scratch_shapes=[pltpu.VMEM((tok, D), BF16), pltpu.VMEM((tok + 16, 128), F32)],
         compiler_params=pltpu.CompilerParams(vmem_limit_bytes=VMEM_LIMIT),
         name="project",
     )(x, g, s, wq, bq, wk, wv, bv, pk, pv)
@@ -352,7 +354,7 @@
 
 
 def masked_kernel(
-    count, groups,
+    count,
     x_ref, nrm_ref, q_ref, kvx_ref, pkvx_ref, slots_ref, cotr_ref, wo_ref, bo_ref, g2_ref, s2_ref,
     win_hbm, bin_ref, wout_hbm,
     actt_ref, gpre_ref, n2t_ref, cot_ref, mixt_ref, gbr_ref, nrmt_ref, gq_ref,
@@ -376,7 +378,7 @@
     nrm_rows = dot_tn(onehot_t, nrm_ref[...])
     qm_ref[...] = (dot_tn(onehot_t, q_ref[...]) * (HD**-0.5)).astype(BF16)
     nrm_rows_t = jnp.transpose(nrm_rows).astype(BF16)
-    store_rows(nrmt_ref, nrm_rows_t, groups)
+    nrmt_ref[...] = nrm_rows_t
     cot_ref[...] = jnp.where(slot_col >= 0, cotr_ref[...].astype(F32), 0.0).astype(BF16)
 
     nbias, fbias = window_biases(count, s, slot_col, near_keys, 0, far_keys, 0, tok)
@@ -400,13 +402,13 @@
 
     lax.fori_loop(0, PAIRS, attend, 0)
     mixed = mix_ref[...]
-    store_rows(mixt_ref, jnp.transpose(mixed.astype(F32)).astype(BF16), groups)
+    mixt_ref[...] = jnp.transpose(mixed.astype(F32)).astype(BF16)
     hidden = x_rows + dot_nn(mixed, wo_ref[...]) + row_of(bo_ref)
     gain_two = row_of(g2_ref)
     n_two, inv_two = norm_stats(hidden)
     normed_two = n_two * gain_two + row_of(s2_ref)
     n2_ref[...] = normed_two.astype(BF16)
-    store_rows(n2t_ref, jnp.transpose(normed_two).astype(BF16), groups)
+    n2t_ref[...] = jnp.transpose(normed_two).astype(BF16)
     acc_ref[...] = jnp.zeros_like(acc_ref)
     load_in.wait()
     load_out.wait()
@@ -418,7 +420,7 @@
         c = cols(t, FF_TILE)
         pre = dot_nn(n2_ref[...], win_ref[:, c]) + bin_row[:, c]
         cdf = 0.5 * (1.0 + lax.erf(pre * SQRT_HALF))
-        store_act(actt_ref, t, jnp.transpose(pre * cdf), groups)
+        actt_ref[t] = jnp.transpose(pre * cdf).astype(BF16)
         slope = cdf + pre * (INV_SQRT_2PI * jnp.exp(-0.5 * pre * pre))
         grad_act = dot_nt(cot_ref[...], wout_ref[rows_at(t * FF_TILE, FF_TILE, FF_TILE), :])
         gpre = (grad_act * slope).astype(BF16)
@@ -465,41 +467,13 @@
     veca_ref[4:5, :] = col_sum(cot)
 
 
-def store_rows(ref, values, groups):
-    if groups is None:
-        ref[...] = values
-        return
-    shard = D // groups["seq"]
-    for k in range(groups["chips"]):
-        at = groups["place"](k) * shard
-        for core in range(2):
-            start = (2 * k + core) * shard
-            ref[core, at : at + shard, :] = values[start : start + shard]
-
-
-def store_act(ref, t, values, groups):
-    if groups is None:
-        ref[t] = values.astype(BF16)
-        return
-    part = FF // groups["seq"] // 2
-    values = values.astype(BF16)
-    at = groups["place"](t) * part
-    for core in range(2):
-        for half in range(2):
-            start = (2 * core + half) * part
-            ref[core, half, rows_at(at, part, part), :] = values[start : start + part]
-
-
-def masked(count, groups, x, nrm, q, kvx, pkvx, slots, cot_rows, wo, bo, g2, s2, w_in, b_in, w_out):
+def masked(count, x, nrm, q, kvx, pkvx, slots, cot_rows, wo, bo, g2, s2, w_in, b_in, w_out):
     tok, cap = x.shape[0], cot_rows.shape[0]
     near_keys, far_keys = kvx.shape[0], pkvx.shape[0]
     tiles = FF // FF_TILE
-    if groups is None:
-        actt, rows_t = (tiles, FF_TILE, cap), (D, cap)
-    else:
-        actt, rows_t = (2, 2, FF // 4, cap), (2, D // 2, cap)
+    actt, rows_t = (tiles, FF_TILE, cap), (D, cap)
     return pl.pallas_call(
-        functools.partial(masked_kernel, count, groups),
+        functools.partial(masked_kernel, count),
         out_shape=(
             struct(actt, BF16),
             struct((2, cap, FF // 2), BF16),
@@ -538,7 +512,6 @@
 
 
 def finish_kernel(
-    groups,
     x_ref, nrm_ref, g1_ref, kvx_ref, gnear_ref, gfar_ref, nb_ref, na_ref, fb_ref, fa_ref, p0_ref,
     gqd_ref, ghid_ref, wq_ref, wk_ref, wv_ref, pk_ref, pv_ref,
     gin_ref, gw_ref, vecb_ref,
@@ -583,17 +556,7 @@
 
     def weights(j, carry):
         c = cols(j, width)
-        product = dot_tn(nrm_ref[...], gkv_ref[:, c]).astype(BF16)
-        if groups is None:
-            gw_ref[j] = product
-        else:
-            tiles = D // width
-            shard = D // groups["seq"]
-            for k in range(groups["chips"]):
-                at = groups["place"](k) * shard
-                for core in range(2):
-                    start = (2 * k + core) * shard
-                    gw_ref[core, j // tiles, at : at + shard, cols(j % tiles, width)] = product[start : start + shard]
+        gw_ref[j] = dot_tn(nrm_ref[...], gkv_ref[:, c]).astype(BF16)
         return carry
 
     lax.fori_loop(0, 2 * D // width, weights, 0)
@@ -627,13 +590,13 @@
         vecb_ref[i : i + 1, :] = sums[i]
 
 
-def finish(groups, x, nrm, g1, kvx, gnear, gfar, edges, gqd, ghid, wq, wk, wv, pk, pv):
+def finish(x, nrm, g1, kvx, gnear, gfar, edges, gqd, ghid, wq, wk, wv, pk, pv):
     tok = x.shape[0]
     return pl.pallas_call(
-        functools.partial(finish_kernel, groups),
+        finish_kernel,
         out_shape=(
             struct((tok, D), F32),
-            struct((6, D, 256) if groups is None else (2, 2, D // 2, D), BF16),
+            struct((6, D, 256), BF16),
             struct((16, D), F32),
         ),
         in_specs=[VMEM] * 18,
@@ -767,28 +730,173 @@
 
 SEQ, CHIPS, NZ = 16, 8, 4
 SH, SF, PART = D // SEQ, FF // SEQ, FF // SEQ // 2
+PAIR = 2 * 128
+BEFORE_ROWS, AFTER_ROWS = HALF + REACH + 16, HALF + REACH
 
 
 def place(k):
     return (k % 2) * NZ + k // 2
 
 
-GROUPS = {"seq": SEQ, "chips": CHIPS, "place": place}
-COPIES = 64
-
-
-def reduce_kernel(
+def store_rows(ref, values):
+    for k in range(CHIPS):
+        at = place(k) * SH
+        for core in range(2):
+            start = (2 * k + core) * SH
+            ref[core, at : at + SH, :] = values[start : start + SH]
+
+
+def front_kernel(
     count,
-    actt, gpre, n2t, cot, mixt, gbr, nrmt, gq, gw, veca, vecb,
-    x_ref, q_ref, kvx_ref, pkvx_ref, wo_ref, bo_ref, g2_ref, s2_ref, win_hbm, bin_ref, wout_hbm, bout_ref,
-    out_ref, f_out, f_in, f_att, f_vec,
-    a_all, c_all, n_all, p_all, a_fwd, n_fwd,
-    m_all, b_all, r_all, g_all, kv_rx, va_rx, vb_rx, vs, vy_rx, vx_rx, vz_rx, vsum,
+    x_ref, nrmt_full, q_ref, kvx_ref, pkvx_ref, slots_ref, cotr_ref, wo_ref, bo_ref, g2_ref, s2_ref,
+    win_hbm, bin_ref, wout_hbm,
+    actt_ref, gpre_ref, n2t_ref, cot_ref, mixt_ref, gbr_ref, nrmt_ref, qm_ref, gm_ref, wn_ref, wf_ref,
+    ghid_ref, veca_ref,
+    win_ref, wout_ref, mix_ref, nbias_ref, fbias_ref, n2_ref, acc_ref, bin_row, sems,
+):
+    s = lax.axis_index("seq")
+    bin_row[...] = row_of(bin_ref)
+    tok = x_ref.shape[0]
+    cap = cotr_ref.shape[0]
+    near_keys, far_keys = kvx_ref.shape[0], pkvx_ref.shape[0]
+    load_in = pltpu.make_async_copy(win_hbm, win_ref, sems.at[0])
+    load_out = pltpu.make_async_copy(wout_hbm, wout_ref, sems.at[1])
+    load_in.start()
+    load_out.start()
+
+    slots = slots_ref[0, 0].reshape(1, cap)
+    onehot_t = jnp.where(lax.broadcasted_iota(jnp.int32, (tok, cap), 0) == slots, 1.0, 0.0).astype(BF16)
+    slot_col = jnp.transpose(jnp.broadcast_to(slots, (cap, cap)))[:, 0:1]
+    x_rows = dot_tn(onehot_t, x_ref[...])
+    qm_ref[...] = (dot_tn(onehot_t, q_ref[...]) * (HD**-0.5)).astype(BF16)
+    store_rows(nrmt_ref, dot_nn(nrmt_full[...], onehot_t).astype(BF16))
+    cot_ref[...] = jnp.where(slot_col >= 0, cotr_ref[...].astype(F32), 0.0).astype(BF16)
+
+    nbias, fbias = window_biases(count, s, slot_col, near_keys, 0, far_keys, 0, tok)
+    nbias_ref[...] = nbias
+    fbias_ref[...] = fbias
+    low, high = head_masks()
+
+    def attend(p, carry):
+        c, cv = cols(p), cols(p + PAIRS)
+        qs = stack_pair(qm_ref[:, c], low, high)
+        nb, fb = nbias_ref[...], fbias_ref[...]
+        near_w = softmax_rows(dot_nt(qs, kvx_ref[:, c]) + jnp.concatenate([nb, nb], axis=0)).astype(BF16)
+        wn_ref[p] = near_w
+        far_w = softmax_rows(dot_nt(qs, pkvx_ref[:, c]) + jnp.concatenate([fb, fb], axis=0)).astype(BF16)
+        wf_ref[p] = far_w
+        out = dot_nn(near_w, kvx_ref[:, cv]) + dot_nn(far_w, pkvx_ref[:, cv])
+        mix_ref[:, c] = merge_pair(out).astype(BF16)
+        return carry
+
+    lax.fori_loop(0, PAIRS, attend, 0)
+    mixed = mix_ref[...]
+    store_rows(mixt_ref, jnp.transpose(mixed.astype(F32)).astype(BF16))
+    hidden = x_rows + dot_nn(mixed, wo_ref[...]) + row_of(bo_ref)
+    gain_two = row_of(g2_ref)
+    n_two, inv_two = norm_stats(hidden)
+    normed_two = n_two * gain_two + row_of(s2_ref)
+    n2_ref[...] = normed_two.astype(BF16)
+    store_rows(n2t_ref, jnp.transpose(normed_two).astype(BF16))
+    acc_ref[...] = jnp.zeros_like(acc_ref)
+    veca_ref[...] = jnp.zeros_like(veca_ref)
+    load_in.wait()
+    load_out.wait()
+    half_tiles = FF // FF_TILE // 2
+
+    def feed(t, carry):
+        c = cols(t, FF_TILE)
+        pre = dot_nn(n2_ref[...], win_ref[:, c]) + bin_row[:, c]
+        cdf = 0.5 * (1.0 + lax.erf(pre * SQRT_HALF))
+        act_t = jnp.transpose(pre * cdf).astype(BF16)
+        at = rows_at(place(t) * PART, PART, PART)
+        for core in range(2):
+            for half in range(2):
+                start = (2 * core + half) * PART
+                actt_ref[core, half, at, :] = act_t[start : start + PART]
+        slope = cdf + pre * (INV_SQRT_2PI * jnp.exp(-0.5 * pre * pre))
+        grad_act = dot_nt(cot_ref[...], wout_ref[rows_at(t * FF_TILE, FF_TILE, FF_TILE), :])
+        gpre = (grad_act * slope).astype(BF16)
+        gpre_ref[t // half_tiles, :, cols(t % half_tiles, FF_TILE)] = gpre
+        veca_ref[pl.ds(8 + t // 2, 1), cols(t % 2, FF_TILE)] = col_sum(gpre.astype(F32))
+        acc_ref[...] += dot_nt(gpre, win_ref[:, c])
+        return carry
+
+    lax.fori_loop(0, FF // FF_TILE, feed, 0)
+    cot = cot_ref[...].astype(F32)
+    grad_n2 = acc_ref[...]
+    grad_hidden = cot + norm_back(n_two, inv_two, gain_two, grad_n2)
+    ghid_ref[...] = grad_hidden
+    grad_branch = grad_hidden.astype(BF16)
+    gbr_ref[...] = grad_branch
+    gm_ref[...] = dot_nt(grad_branch, wo_ref[...]).astype(BF16)
+    veca_ref[1:2, :] = col_sum(grad_branch.astype(F32))
+    veca_ref[2:3, :] = col_sum(grad_n2 * n_two)
+    veca_ref[3:4, :] = col_sum(grad_n2)
+    veca_ref[4:5, :] = col_sum(cot)
+
+
+def front(count, x, nrmt, q, kvx, pkvx, slots, cot_rows, wo, bo, g2, s2, w_in, b_in, w_out):
+    cap = cot_rows.shape[0]
+    near_keys, far_keys = kvx.shape[0], pkvx.shape[0]
+    rows_t = (2, D // 2, cap)
+    return pl.pallas_call(
+        functools.partial(front_kernel, count),
+        out_shape=(
+            struct((2, 2, FF // 4, cap), BF16),
+            struct((2, cap, FF // 2), BF16),
+            struct(rows_t, BF16),
+            struct((cap, D), BF16),
+            struct(rows_t, BF16),
+            struct((cap, D), BF16),
+            struct(rows_t, BF16),
+            struct((cap, D), BF16),
+            struct((cap, D), BF16),
+            struct((PAIRS, 2 * cap, near_keys), BF16),
+            struct((PAIRS, 2 * cap, far_keys), BF16),
+            struct((cap, D), F32),
+            struct((16, D), F32),
+        ),
+        in_specs=[VMEM] * 11 + [ANY, VMEM, ANY],
+        out_specs=(VMEM,) * 13,
+        scratch_shapes=[
+            pltpu.VMEM((D, FF), BF16),
+            pltpu.VMEM((FF, D), BF16),
+            pltpu.VMEM((cap, D), BF16),
+            pltpu.VMEM((cap, near_keys), F32),
+            pltpu.VMEM((cap, far_keys), F32),
+            pltpu.VMEM((cap, D), BF16),
+            pltpu.VMEM((cap, D), F32),
+            pltpu.VMEM((1, FF), F32),
+            pltpu.SemaphoreType.DMA((2,)),
+        ],
+        compiler_params=pltpu.CompilerParams(vmem_limit_bytes=VMEM_LIMIT),
+        name="masked_rows",
+    )(x, nrmt, q, kvx, pkvx, slots, cot_rows, wo, bo, g2, s2, w_in, b_in, w_out)
+
+
+COPIES = 80
+LOADS = 24
+
+
+def tail_kernel(
+    count,
+    actt, gpre, n2t, cot, mixt, gbr, nrmt, qm_hbm, gm_hbm, wn_hbm, wf_hbm, ghid_hbm, veca,
+    x_hbm, nrmt_hbm, q_hbm, kvx_hbm, pkvx_hbm, wq_hbm, wk_hbm, wv_hbm, wo_hbm, win_hbm, wout_hbm,
+    slots_ref, bo_ref, g1_ref, g2_ref, s2_ref, bin_ref, bout_ref, pk_ref, pv_ref,
+    out_ref, gin_ref, f_out, f_in, f_oq, f_kv, f_vec,
+    qm, gm, wn, wf, ghid, x_ref, nrmt_full, q_ref, kvx_ref, pkvx_ref, wq_ref, wk_ref, wv_ref, wo_ref,
+    hb, ha, rb, ra, gown, fown, keys, grads, gkv_ref, gq_ref,
+    a_all, c_all, n_all, p_all, a_fwd, n_fwd, m_all, b_all, r_all, g_all,
+    va_rx, vb_rx, vecb_ref, vs, vy_rx, vx_rx, vz_rx,
+    gw, kv_rx, kv_s, kv_xr, kv_t, kv_yr, kv_z, kv_zr,
     att, att_y, att_x, att_xr, att_z, att_zr,
     wo_g, wo_y, wo_z, wo_zr, wi_g, wi_y, wi_z, wi_zr,
-    send, recv, *dense_refs,
+    send, recv, hsend, hrecv, ksend, krecv, loads, *dense_refs,
 ):
-    cap = cot.shape[0]
+    cap = ghid.shape[0]
+    tok = x_ref.shape[0]
+    pooled = tok // STRIDE
     d, s = lax.axis_index("dp"), lax.axis_index("seq")
     c, chip = s % 2, s // 2
     y, z = chip % 2, chip // 2
@@ -798,11 +906,53 @@
     y_dev = (d, z * 4 + w * 2 + c)
     z_at = [(z + t) % NZ for t in range(1, NZ)]
     z_dev = [(d, zt * 4 + y * 2 + c) for zt in z_at]
+    before, after = (d, s - 1), (d, s + 1)
+    has_before, has_after = s > 0, s < count - 1
+    far_side = s + 2 * c - 1
+    has_far = jnp.logical_and(far_side >= 0, far_side < count)
+
     barrier = pltpu.get_barrier_semaphore()
     peers = [core_dev, x_dev, y_dev] + z_dev
     for peer in peers:
         pl.semaphore_signal(barrier, inc=1, device_id=peer, device_id_type=MESH)
-    pl.semaphore_wait(barrier, len(peers))
+
+    @pl.when(has_far)
+    def _():
+        pl.semaphore_signal(barrier, inc=1, device_id=(d, far_side), device_id_type=MESH)
+
+    loaded = []
+
+    def load(src, dst):
+        copy = pltpu.make_async_copy(src, dst, loads.at[len(loaded)])
+        copy.start()
+        loaded.append(copy)
+        return copy
+
+    def lane(g):
+        return pl.ds(128 * g, 128)
+
+    def slab(g):
+        return pl.ds(cap * g, cap)
+
+    first = [load(qm_hbm, qm), load(gm_hbm, gm), load(wn_hbm, wn), load(wf_hbm, wf)]
+    first += [load(kvx_hbm, kvx_ref), load(pkvx_hbm, pkvx_ref)]
+    own_o = [load(mixt.at[c], m_all.at[:, lane(0)]), load(gbr, b_all.at[slab(0)])]
+    own_q = load(nrmt.at[c], r_all.at[:, lane(0)])
+    own_out = [load(actt.at[c, d], a_all.at[:, lane(0)]), load(cot, c_all.at[slab(0)])]
+    own_in = [load(n2t.at[c], n_all.at[:, lane(0)]), load(gpre.at[d], p_all.at[slab(0)])]
+    second = [load(nrmt_hbm, nrmt_full)]
+    third = [load(wq_hbm, wq_ref), load(wk_hbm, wk_ref), load(wv_hbm, wv_ref), load(x_hbm, x_ref)]
+    third += [load(ghid_hbm, ghid), load(veca, vecb_ref.at[pl.ds(16, 16)])]
+    fourth = [load(q_hbm, q_ref), load(wo_hbm, wo_ref)]
+
+    @pl.when(has_far)
+    def _():
+        pl.semaphore_wait(barrier, len(peers) + 1)
+
+    @pl.when(jnp.logical_not(has_far))
+    def _():
+        pl.semaphore_wait(barrier, len(peers))
+
     used = [0]
     started = []
 
@@ -818,71 +968,183 @@
         for copy in copies:
             copy.wait_recv()
 
-    def lane(g):
-        return pl.ds(128 * g, 128)
-
-    def slab(g):
-        return pl.ds(cap * g, cap)
+    def wait(copies):
+        for copy in copies:
+            copy.wait()
 
     begin, attend, blocks, residual, feed, end = dense_parts(
         count, x_ref, q_ref, kvx_ref, pkvx_ref, wo_ref, bo_ref, g2_ref, s2_ref, win_hbm, bin_ref, wout_hbm,
         bout_ref, out_ref, *dense_refs
     )
+    acc_ref = dense_refs[6]
 
     out_x = [
         go(actt.at[c, f], a_all.at[:, lane(2)], x_dev),
         go(actt.at[e, f], a_fwd, x_dev),
         go(cot, c_all.at[slab(2)], x_dev),
     ]
+    o_core = [go(mixt.at[e], m_all.at[:, lane(1)], core_dev), go(gbr, b_all.at[slab(1)], core_dev)]
+    q_core = [go(nrmt.at[e], r_all.at[:, lane(1)], core_dev)]
     out_core = [go(actt.at[e, d], a_all.at[:, lane(1)], core_dev), go(cot, c_all.at[slab(1)], core_dev)]
-    att_core = [
-        go(gw.at[e], kv_rx, core_dev),
-        go(mixt.at[e], m_all.at[:, lane(1)], core_dev),
-        go(gbr, b_all.at[slab(1)], core_dev),
-        go(nrmt.at[e], r_all.at[:, lane(1)], core_dev),
-        go(gq, g_all.at[slab(1)], core_dev),
-        go(veca, va_rx, core_dev),
-        go(vecb, vb_rx, core_dev),
-    ]
     in_x = [
         go(n2t.at[c], n_all.at[:, lane(2)], x_dev),
         go(n2t.at[e], n_fwd, x_dev),
         go(gpre.at[f], p_all.at[slab(2)], x_dev),
     ]
     in_core = [go(n2t.at[e], n_all.at[:, lane(1)], core_dev), go(gpre.at[d], p_all.at[slab(1)], core_dev)]
-    a_all[:, lane(0)] = actt[c, d]
-    c_all[slab(0), :] = cot[...]
-    n_all[:, lane(0)] = n2t[c]
-    p_all[slab(0), :] = gpre[d]
-    m_all[:, lane(0)] = mixt[c]
-    b_all[slab(0), :] = gbr[...]
-    r_all[:, lane(0)] = nrmt[c]
-    g_all[slab(0), :] = gq[...]
-    begin()
-
-    arrive(att_core)
+    vec_core = [go(veca, va_rx, core_dev)]
+
+    def to_before(p):
+        return remote(hb.at[p], ra.at[p], hsend.at[p], hrecv.at[p], before)
+
+    def to_after(p):
+        return remote(ha.at[p], rb.at[p], hsend.at[PAIRS + p], hrecv.at[PAIRS + p], after)
+
+    def send_halo(p):
+        @pl.when(has_before)
+        def _():
+            to_before(p).start()
+
+        @pl.when(has_after)
+        def _():
+            to_after(p).start()
+
+    def pair_at(i):
+        return (i + (PAIRS // 2) * f) % PAIRS
+
+    wait(first)
+    low, high = head_masks()
+
+    def attend_back(i, carry):
+        p = pair_at(i)
+
+        @pl.when(i > 0)
+        def _():
+            send_halo(pair_at(i + PAIRS - 1))
+
+        cc, cv = cols(p), cols(p + PAIRS)
+        qs = stack_pair(qm[:, cc], low, high)
+        gs = stack_pair(gm[:, cc], low, high)
+        near_low, far_low = wn[p], wf[p]
+        near_w, far_w = near_low.astype(F32), far_low.astype(F32)
+        dn = dot_nt(gs, kvx_ref[:, cv])
+        ds = (near_w * (dn - jnp.sum(near_w * dn, axis=-1, keepdims=True))).astype(BF16)
+        df = dot_nt(gs, pkvx_ref[:, cv])
+        dsf = (far_w * (df - jnp.sum(far_w * df, axis=-1, keepdims=True))).astype(BF16)
+        gq = dot_nn(ds, kvx_ref[:, cc]) + dot_nn(dsf, pkvx_ref[:, cc])
+        gq_ref[:, cc] = (merge_pair(gq) * (HD**-0.5)).astype(BF16)
+        for h, near, far in (
+            (0, dot_tn(ds, qs), dot_tn(dsf, qs)),
+            (1, dot_tn(near_low, gs), dot_tn(far_low, gs)),
+        ):
+            near, far = near.astype(BF16), far.astype(BF16)
+            hb[p, 0:HALF, lane(h)] = near[0:HALF]
+            hb[p, HALF:BEFORE_ROWS, lane(h)] = far[0 : REACH + 16]
+            ha[p, 0:HALF, lane(h)] = near[HALF + tok :]
+            ha[p, HALF:AFTER_ROWS, lane(h)] = far[REACH + pooled :]
+            gown[p, :, lane(h)] = near[HALF : HALF + tok]
+            fown[p, :, lane(h)] = far[REACH : REACH + pooled + 16]
+        return carry
+
+    lax.fori_loop(0, PAIRS, attend_back, 0)
     rows = NZ * SH
 
-    def halves(ref, values, g):
-        ref[0, g] = values[:rows].astype(BF16)
-        ref[1, g] = values[rows:].astype(BF16)
-
-    halves(att, dot_nn(m_all[...], b_all[...]), 0)
-    halves(att, dot_nn(r_all[...], g_all[...]), 1)
-    for g in range(2):
-        for half in range(2):
-            part = pl.ds(half * rows, rows)
-            att[half, 2 + g] = (gw[c, g, part].astype(F32) + kv_rx[g, part].astype(F32)).astype(BF16)
-    vs[0:16, :] = (veca[...] + va_rx[...]).astype(BF16)
-    vs[16:32, :] = (vecb[...] + vb_rx[...]).astype(BF16)
-    attend(0)
-    att_to_y = [go(att.at[w], att_y, y_dev), go(vs, vy_rx, y_dev)]
-    attend(1)
-
+    def halves(values, g):
+        att[0, g] = values[:rows].astype(BF16)
+        att[1, g] = values[rows:].astype(BF16)
+
+    wait(own_o)
+    own_q.wait()
+    arrive(o_core)
+    halves(dot_nn(m_all[...], b_all[...]), 0)
+    g_all[slab(0), :] = gq_ref[...]
+    vecb_ref[0:16, :] = jnp.zeros((16, D), F32)
+    send_halo(pair_at(PAIRS - 1))
+    q_core.append(go(gq_ref, g_all.at[slab(1)], core_dev))
+    wait(second)
+
+    @pl.when(jnp.logical_not(has_before))
+    def _():
+        rb[...] = jnp.zeros_like(rb)
+
+    @pl.when(jnp.logical_not(has_after))
+    def _():
+        ra[...] = jnp.zeros_like(ra)
+
+    vecb_ref[13:14, :] = col_sum(gq_ref[...].astype(F32))
+    arrive(q_core)
+    halves(dot_nn(r_all[...], g_all[...]), 1)
+
+    def kv_copy(p):
+        return remote(gw.at[p, e], kv_rx.at[p], ksend.at[p], krecv.at[p], core_dev)
+
+    grads[0:8, :] = jnp.zeros((8, 128), F32)
+    half_pool = pooled - REACH
+
+    def pool(i, carry):
+        p = pair_at(i)
+
+        @pl.when(has_before)
+        def _():
+            to_after(p).wait_recv()
+
+        @pl.when(has_after)
+        def _():
+            to_before(p).wait_recv()
+
+        parts = []
+        for h, start, taps_ref in ((0, 3, pk_ref), (1, 8, pv_ref)):
+            ln = lane(h)
+            cc = cols(p + PAIRS * h)
+            taps = taps_ref[:, cols(p)].astype(F32)
+            mine = fown[p, 0:pooled, ln].astype(F32)
+            head = mine[0:REACH] + rb[p, HALF : HALF + REACH, ln].astype(F32)
+            foot = mine[half_pool:] + ra[p, HALF : HALF + REACH, ln].astype(F32)
+            gp = jnp.concatenate([head, mine[REACH:half_pool], foot], axis=0) if half_pool > REACH else (
+                jnp.concatenate([head, foot], axis=0)
+            )
+            gp = gp.astype(BF16).astype(F32)
+            nxt = fown[p, pooled : pooled + 16, ln].astype(F32) + ra[p, HALF + REACH :, ln].astype(F32)
+            nxt = nxt[0:1].astype(BF16).astype(F32)
+            keys[...] = kvx_ref[HALF - 16 : HALF + tok, cc].astype(F32)
+            grads[8 : 8 + tok, :] = gown[p, :, ln].astype(F32)
+            grads[8 : 8 + HALF, :] += rb[p, 0:HALF, ln].astype(F32)
+            grads[8 + tok - HALF : 8 + tok, :] += ra[p, 0:HALF, ln].astype(F32)
+            for t in range(KERNEL):
+                at = pl.ds(6 + t, pooled, stride=STRIDE)
+                grads[at, :] += gp * taps[t : t + 1]
+                key_rows = keys[pl.ds(14 + t, pooled, stride=STRIDE), :]
+                vecb_ref[start + t : start + t + 1, cols(p)] = col_sum(key_rows * gp)
+            rim = jnp.concatenate([jnp.zeros((6, 128), F32), nxt * taps[0:1], nxt * taps[1:2]], axis=0)
+            grads[tok : tok + 8, :] += rim
+            done = grads[8 : 8 + tok, :].astype(BF16)
+            gkv_ref[:, cc] = done
+            parts.append(done)
+
+        @pl.when(i > 0)
+        def _():
+            kv_copy(pair_at(i + PAIRS - 1)).start()
+
+        product = dot_nn(nrmt_full[...], jnp.concatenate(parts, axis=1)).astype(BF16)
+        for k in range(CHIPS):
+            at = place(k) * SH
+            for core in range(2):
+                row = (2 * k + core) * SH
+                gw[p, core, at : at + SH, :] = product[row : row + SH]
+        return carry
+
+    def pool_range(a, b):
+        lax.fori_loop(a, b, pool, 0)
+
+    att_to_y = [go(att.at[w], att_y, y_dev)]
+    pool_range(0, 2)
     arrive(out_x)
     out_fwd = [go(a_fwd, a_all.at[:, lane(3)], core_dev), go(c_all.at[slab(2)], c_all.at[slab(3)], core_dev)]
-    attend(2)
+    pool_range(2, PAIRS)
+
+    wait(own_out)
     arrive(out_core + out_fwd)
+    kv_copy(pair_at(PAIRS - 1)).start()
     quarter = NZ * PART // 2
 
     def out_product(i, carry):
@@ -891,11 +1153,67 @@
         return carry
 
     lax.fori_loop(0, 4, out_product, 0)
-    attend(3)
-    out_to_y = [go(wo_g.at[w], wo_y, y_dev)]
     arrive(in_x)
     in_fwd = [go(n_fwd, n_all.at[:, lane(3)], core_dev), go(p_all.at[slab(2)], p_all.at[slab(3)], core_dev)]
-    residual()
+
+    triple = PAIRS // 2
+
+    def kv_sum(i, carry):
+        p = pair_at(i)
+        kv_copy(p).wait()
+        kv_s[p] = (gw[p, c].astype(F32) + kv_rx[p].astype(F32)).astype(BF16)
+        return carry
+
+    lax.fori_loop(0, triple, kv_sum, 0)
+    out_to_y = [go(wo_g.at[w], wo_y, y_dev)]
+    lax.fori_loop(triple, PAIRS, kv_sum, 0)
+    kv_to_x = [go(kv_s.at[pl.ds(f * triple, triple)], kv_xr, x_dev)]
+
+    wait(third)
+    high_part = ghid[...].astype(BF16)
+    low_part = (ghid[...] - high_part.astype(F32)).astype(BF16)
+    hid_parts = jnp.concatenate([high_part, low_part], axis=0)
+    width = 256
+
+    def query_back(j, carry):
+        gm_f = dot_nt(gq_ref[...], wq_ref[rows_at(j * width, width, width), :])
+        top = gm_f.astype(BF16)
+        b_all[0:cap, cols(j, width)] = top
+        b_all[cap : 2 * cap, cols(j, width)] = (gm_f - top.astype(F32)).astype(BF16)
+        return carry
+
+    lax.fori_loop(0, D // width, query_back, 0)
+    slots = slots_ref[0, 0].reshape(1, cap)
+    slots = jnp.concatenate([slots, slots], axis=1)
+
+    def back(j, carry):
+        r = rows_at(j * width, width, width)
+        total = dot_nt(gkv_ref[:, 0:D], wk_ref[r, :]) + dot_nt(gkv_ref[:, D : 2 * D], wv_ref[r, :])
+        acc_ref[:, cols(j, width)] = total
+        return carry
+
+    lax.fori_loop(0, D // width, back, 0)
+    block = 128
+    gain = row_of(g1_ref)
+
+    def norm(j, sums):
+        r = rows_at(j * block, block, block)
+        at = j * block + lax.broadcasted_iota(jnp.int32, (block, 2 * cap), 0)
+        onehot = jnp.where(at == slots, 1.0, 0.0).astype(BF16)
+        n, inv = norm_stats(x_ref[r, :].astype(F32))
+        grad = acc_ref[r, :] + dot_nn(onehot, b_all[...])
+        gin_ref[r, :] = dot_nn(onehot, hid_parts) + norm_back(n, inv, gain, grad)
+        return (
+            sums[0] + col_sum(grad * n),
+            sums[1] + col_sum(grad),
+            sums[2] + col_sum(gkv_ref[r, D : 2 * D].astype(F32)),
+        )
+
+    zero = jnp.zeros((1, D), F32)
+    sums = lax.fori_loop(0, tok // block, norm, (zero, zero, zero))
+    for i in range(3):
+        vecb_ref[i : i + 1, :] = sums[i]
+    wait(own_in)
     arrive(in_core + in_fwd)
 
     def in_product(i, carry):
@@ -905,43 +1223,65 @@
         return carry
 
     lax.fori_loop(0, 8, in_product, 0)
-    feed(0, 2)
+    vec_core.append(go(vecb_ref.at[pl.ds(0, 16)], vb_rx, core_dev))
+    begin()
     in_to_y = [go(wi_g.at[w], wi_y, y_dev)]
+    wait(fourth)
+    attend(0)
 
     arrive(att_to_y)
     wide = D // 2
-    for g in range(4):
+    for g in range(2):
         total = att[y, g].astype(F32) + att_y[g].astype(F32)
         att_x[0, g] = total[:, :wide].astype(BF16)
         att_x[1, g] = total[:, wide:].astype(BF16)
-    vs2 = vsum.at[0]
-    vs2[...] = (vs[...].astype(F32) + vy_rx[...].astype(F32)).astype(BF16)
-    feed(2, 4)
-    att_to_x = [go(att_x.at[f], att_xr, x_dev), go(vs2, vx_rx, x_dev)]
-    feed(4, 6)
-
+    arrive(vec_core)
+    vs[0, 0:16, :] = (vecb_ref[16:32, :] + va_rx[...]).astype(BF16)
+    vs[0, 16:32, :] = (vecb_ref[0:16, :] + vb_rx[...]).astype(BF16)
+    arrive(kv_to_x)
+    for q in range(triple):
+        total = kv_s[d * triple + q].astype(F32) + kv_xr[q].astype(F32)
+        kv_t[0, q] = total[:rows].astype(BF16)
+        kv_t[1, q] = total[rows:].astype(BF16)
+    attend(1)
+    kv_to_y = [go(kv_t.at[w], kv_yr, y_dev)]
+    vec_to_y = [go(vs.at[0], vy_rx, y_dev)]
+    att_to_x = [go(att_x.at[f], att_xr, x_dev)]
+    attend(2)
     arrive(out_to_y)
     for zz in range(NZ):
         r = pl.ds(zz * PART, PART)
         wo_z[zz] = (wo_g[y, r].astype(F32) + wo_y[r].astype(F32)).astype(BF16)
-    feed(6, 7)
+    attend(3)
     out_to_z = [go(wo_z.at[z_at[t]], wo_zr.at[t], z_dev[t]) for t in range(NZ - 1)]
+    residual()
     arrive(att_to_x)
     for zz in range(NZ):
         r = pl.ds(zz * SH, SH)
-        for g in range(4):
+        for g in range(2):
             att_z[zz, g] = (att_x[d, g, r].astype(F32) + att_xr[g, r].astype(F32)).astype(BF16)
-    vs3 = vsum.at[1]
-    vs3[...] = (vs2[...].astype(F32) + vx_rx[...].astype(F32)).astype(BF16)
-    feed(7, 8)
+    arrive(vec_to_y)
+    vs[1] = (vs[0].astype(F32) + vy_rx[...].astype(F32)).astype(BF16)
+    feed(0, 2)
+    vec_to_x = [go(vs.at[1], vx_rx, x_dev)]
     att_to_z = [go(att_z.at[z_at[t]], att_zr.at[t], z_dev[t]) for t in range(NZ - 1)]
-    vec_to_z = [go(vs3, vz_rx.at[t], z_dev[t]) for t in range(NZ - 1)]
-    end()
+    feed(2, 4)
     arrive(in_to_y)
     for zz in range(NZ):
         r = pl.ds(zz * SH, SH)
         wi_z[zz] = (wi_g[y, r].astype(F32) + wi_y[r].astype(F32)).astype(BF16)
+    feed(4, 5)
     in_to_z = [go(wi_z.at[z_at[t]], wi_zr.at[t], z_dev[t]) for t in range(NZ - 1)]
+    arrive(kv_to_y)
+    for zz in range(NZ):
+        r = pl.ds(zz * SH, SH)
+        for q in range(triple):
+            kv_z[zz, q] = (kv_t[y, q, r].astype(F32) + kv_yr[q, r].astype(F32)).astype(BF16)
+    arrive(vec_to_x)
+    vs[2] = (vs[1].astype(F32) + vx_rx[...].astype(F32)).astype(BF16)
+    feed(5, 6)
+    kv_to_z = [go(kv_z.at[z_at[t]], kv_zr.at[t], z_dev[t]) for t in range(NZ - 1)]
+    vec_to_z = [go(vs.at[2], vz_rx.at[t], z_dev[t]) for t in range(NZ - 1)]
 
     def gathered(own, parts):
         total = own.astype(F32)
@@ -949,67 +1289,119 @@
             total = total + parts[t].astype(F32)
         return total
 
+    last = []
+
+    def share(ref, value):
+        ref[d] = value.astype(BF16)
+        last.append(go(ref.at[d], ref.at[d], x_dev))
+
     arrive(out_to_z)
-    f_out[d] = gathered(wo_z[z], wo_zr).astype(BF16)
-    last = [go(f_out.at[d], f_out.at[d], x_dev)]
+    share(f_out, gathered(wo_z[z], wo_zr))
+    feed(6, 8)
+    end()
     arrive(att_to_z)
-    f_att[d] = gathered(att_z[z], att_zr).astype(BF16)
-    last.append(go(f_att.at[d], f_att.at[d], x_dev))
+    share(f_oq, gathered(att_z[z], att_zr))
+    arrive(in_to_z)
+    share(f_in, gathered(wi_z[z], wi_zr))
+    arrive(kv_to_z)
+    share(f_kv, gathered(kv_z[z], kv_zr))
     arrive(vec_to_z)
-    f_vec[...] = gathered(vs3[...], vz_rx)
-    arrive(in_to_z)
-    f_in[d] = gathered(wi_z[z], wi_zr).astype(BF16)
-    last.append(go(f_in.at[d], f_in.at[d], x_dev))
+    f_vec[...] = gathered(vs[2], vz_rx)
     arrive(last)
     for copy in started:
         copy.wait_send()
 
-
-def reduce_all(count, grads, dense_args):
-    cap = grads[3].shape[0]
-    tok = dense_args[0].shape[0]
-    half, rows = D // 2, NZ * SH
-    b16 = functools.partial(pltpu.VMEM, dtype=BF16)
+    def drain(p, carry):
+        @pl.when(has_before)
+        def _():
+            to_before(p).wait_send()
+
+        @pl.when(has_after)
+        def _():
+            to_after(p).wait_send()
+
+        return carry
+
+    lax.fori_loop(0, PAIRS, drain, 0)
+
+
+def tail(count, rows, *args):
+    cap = rows[3].shape[0]
+    x, nrmt, q, kvx, pkvx = args[:5]
+    tok = x.shape[0]
+    pooled = tok // STRIDE
+    half, sums, triple = D // 2, NZ * SH, PAIRS // 2
+
+    def b16(*shape):
+        return pltpu.VMEM(shape, BF16)
+
+    def f32(*shape):
+        return pltpu.VMEM(shape, F32)
+
+    def like(a):
+        return pltpu.VMEM(a.shape, a.dtype)
+
+    dma = pltpu.SemaphoreType.DMA
     return pl.pallas_call(
-        functools.partial(reduce_kernel, count),
+        functools.partial(tail_kernel, count),
         out_shape=(
             struct((tok, D), BF16),
+            struct((tok, D), F32),
             struct((2, PART, D), BF16),
             struct((2, SH, FF // 2), BF16),
-            struct((2, 4, SH, D // 2), BF16),
+            struct((2, 2, SH, half), BF16),
+            struct((2, triple, SH, PAIR), BF16),
             struct((32, D), F32),
         ),
-        in_specs=[VMEM] * 11 + [VMEM] * 8 + [ANY, VMEM, ANY, VMEM],
-        out_specs=(VMEM,) * 5,
+        in_specs=[ANY] * 24 + [VMEM] * 9,
+        out_specs=(VMEM,) * 7,
         scratch_shapes=[
-            b16((FF // 4, 4 * cap)), b16((4 * cap, D)), b16((half, 4 * cap)), b16((4 * cap, FF // 2)),
-            b16((FF // 4, cap)), b16((half, cap)),
-            b16((half, 2 * cap)), b16((2 * cap, D)), b16((half, 2 * cap)), b16((2 * cap, D)),
-            b16((2, half, D)), pltpu.VMEM((16, D), F32), pltpu.VMEM((16, D), F32),
-            b16((32, D)), b16((32, D)), b16((32, D)), b16((NZ - 1, 32, D)), b16((2, 32, D)),
-            b16((2, 4, rows, D)), b16((4, rows, D)), b16((2, 4, rows, half)), b16((4, rows, half)),
-            b16((NZ, 4, SH, half)), b16((NZ - 1, 4, SH, half)),
-            b16((2, NZ * PART, D)), b16((NZ * PART, D)), b16((NZ, PART, D)), b16((NZ - 1, PART, D)),
-            b16((2, rows, FF // 2)), b16((rows, FF // 2)), b16((NZ, SH, FF // 2)), b16((NZ - 1, SH, FF // 2)),
-            pltpu.SemaphoreType.DMA((COPIES,)), pltpu.SemaphoreType.DMA((COPIES,)),
+            b16(cap, D), b16(cap, D), like(rows[9]), like(rows[10]), f32(cap, D), like(x), like(nrmt), like(q),
+            like(kvx), like(pkvx), b16(D, D), b16(D, D), b16(D, D), b16(D, D),
+            b16(PAIRS, BEFORE_ROWS, PAIR), b16(PAIRS, AFTER_ROWS, PAIR),
+            b16(PAIRS, AFTER_ROWS, PAIR), b16(PAIRS, BEFORE_ROWS, PAIR),
+            b16(PAIRS, tok, PAIR), b16(PAIRS, pooled + 16, PAIR), f32(tok + 16, 128), f32(tok + 16, 128),
+            b16(tok, 2 * D), b16(cap, D),
+            b16(FF // 4, 4 * cap), b16(4 * cap, D), b16(half, 4 * cap), b16(4 * cap, FF // 2),
+            b16(FF // 4, cap), b16(half, cap),
+            b16(half, 2 * cap), b16(2 * cap, D), b16(half, 2 * cap), b16(2 * cap, D),
+            f32(16, D), f32(16, D), f32(32, D), b16(3, 32, D), b16(32, D), b16(32, D), b16(NZ - 1, 32, D),
+            b16(PAIRS, 2, half, PAIR), b16(PAIRS, half, PAIR), b16(PAIRS, half, PAIR), b16(triple, half, PAIR),
+            b16(2, triple, sums, PAIR), b16(triple, sums, PAIR), b16(NZ, triple, SH, PAIR),
+            b16(NZ - 1, triple, SH, PAIR),
+            b16(2, 2, sums, D), b16(2, sums, D), b16(2, 2, sums, half), b16(2, sums, half),
+            b16(NZ, 2, SH, half), b16(NZ - 1, 2, SH, half),
+            b16(2, NZ * PART, D), b16(NZ * PART, D), b16(NZ, PART, D), b16(NZ - 1, PART, D),
+            b16(2, sums, FF // 2), b16(sums, FF // 2), b16(NZ, SH, FF // 2), b16(NZ - 1, SH, FF // 2),
+            dma((COPIES,)), dma((COPIES,)), dma((2 * PAIRS,)), dma((2 * PAIRS,)), dma((PAIRS,)), dma((PAIRS,)),
+            dma((LOADS,)),
         ] + dense_scratch(tok),
         compiler_params=pltpu.CompilerParams(
             collective_id=2, has_side_effects=True, vmem_limit_bytes=VMEM_LIMIT
         ),
-        name="reduce",
-    )(*grads, *dense_args)
-
-
-def unpack_kernel(f_out, f_in, f_att, f_vec, g1, s1, wq, bq, wk, wv, bv, wo, bo, pk, pv, g2, s2, wi, bi, wu, bu):
+        name="tail",
+    )(*rows, *args)
+
+
+def unpack_kernel(
+    out_hbm, gin_hbm, f_out, f_in, f_oq, f_kv, f_vec,
+    out_ref, gin_ref, g1, s1, wq, bq, wk, wv, bv, wo, bo, pk, pv, g2, s2, wi, bi, wu, bu,
+):
     s = lax.axis_index("seq")
+    out_ref[...] = out_hbm[...]
+    gin_ref[...] = gin_hbm[...]
     wu[0:PART, :] = f_out[0].astype(F32)
     wu[PART : 2 * PART, :] = f_out[1].astype(F32)
     for h in range(2):
         wi[:, h * (FF // 2) : (h + 1) * (FF // 2)] = f_in[h].astype(F32)
-        for g, ref in enumerate((wo, wq, wk, wv)):
-            ref[:, h * (D // 2) : (h + 1) * (D // 2)] = f_att[h, g].astype(F32)
+        for g, ref in enumerate((wo, wq)):
+            ref[:, h * (D // 2) : (h + 1) * (D // 2)] = f_oq[h, g].astype(F32)
+        for q in range(PAIRS // 2):
+            at = (h * (PAIRS // 2) + q) * 128
+            wk[:, at : at + 128] = f_kv[h, q, :, 0:128].astype(F32)
+            wv[:, at : at + 128] = f_kv[h, q, :, 128:256].astype(F32)
     own = pltpu.roll(f_vec[...], lax.rem(D - SH * s, D), 1)
-    for row, ref in ((0, bq), (1, bo), (2, g2), (3, s2), (4, bu), (16, g1), (17, s1), (18, bv)):
+    for row, ref in ((29, bq), (1, bo), (2, g2), (3, s2), (4, bu), (16, g1), (17, s1), (18, bv)):
         ref[...] = own[row, :SH]
     pk[...] = own[19:24, :SH]
     pv[...] = own[24:29, :SH]
@@ -1019,19 +1411,20 @@
     bi[...] = pltpu.roll(part, lax.rem(D - SF * (s % 4), D), 1)[0, :SF]
 
 
-def unpack(f_out, f_in, f_att, f_vec):
+def unpack(output, grad_input, *finals):
     one, square, taps = struct((SH,), F32), struct((SH, D), F32), struct((KERNEL, SH), F32)
     return pl.pallas_call(
         unpack_kernel,
         out_shape=(
+            struct(output.shape, BF16), struct(grad_input.shape, F32),
             one, one, square, one, square, square, one, square, one, taps, taps, one, one,
             struct((SH, FF), F32), struct((SF,), F32), struct((SF, D), F32), one,
         ),
-        in_specs=[VMEM] * 4,
-        out_specs=(VMEM,) * 17,
+        in_specs=[VMEM] * 7,
+        out_specs=(VMEM,) * 19,
         compiler_params=pltpu.CompilerParams(vmem_limit_bytes=VMEM_LIMIT),
         name="unpack",
-    )(f_out, f_in, f_att, f_vec)
+    )(output, grad_input, *finals)
 
 
 def plain_reduce(actt, gpre, n2t, cot, mixt, gbr, nrmt, gq, gw, veca, vecb):
@@ -1061,27 +1454,35 @@
     pool_key, pool_value, gain_two, shift_two, w_in, b_in, w_out, b_out, mask_slots, cot_rows,
 ):
     x = x_input[0]
-    groups = GROUPS if (n_dp, n_seq) == (2, SEQ) else None
-    nrm, q, kv, pkv = project(
+    cot = cot_rows[0, 0]
+    nrmt, q, kv, pkv = project(
         x, gain_one, shift_one, w_query, b_query, w_key, w_value, b_value, pool_key, pool_value
     )
     kvx, pkvx = halo(n_seq, kv, pkv, pool_key, pool_value)
+    if (n_dp, n_seq) == (2, SEQ):
+        rows = front(
+            n_seq, x, nrmt, q, kvx, pkvx, mask_slots, cot, w_attn_out, b_attn_out, gain_two, shift_two,
+            w_in, b_in, w_out,
+        )
+        done = tail(
+            n_seq, rows, x, nrmt, q, kvx, pkvx, w_query, w_key, w_value, w_attn_out, w_in, w_out,
+            mask_slots, b_attn_out, gain_one, gain_two, shift_two, b_in, b_out, pool_key, pool_value,
+        )
+        output, grad_input, *reduced = unpack(*done)
+        return (output[None], grad_input[None]) + tuple(reduced)
+    nrm = nrmt.T
     (actt, gpre, n2t, cot, mixt, gbr, nrmt, gq, gnear, gfar, ghid, gqd, veca) = masked(
-        n_seq, groups, x, nrm, q, kvx, pkvx, mask_slots, cot_rows[0, 0],
-        w_attn_out, b_attn_out, gain_two, shift_two, w_in, b_in, w_out,
+        n_seq, x, nrm, q, kvx, pkvx, mask_slots, cot, w_attn_out, b_attn_out, gain_two, shift_two,
+        w_in, b_in, w_out,
     )
     edges = halo_back(n_seq, gnear, gfar)
     grad_input, gw, vecb = finish(
-        groups, x, nrm, gain_one, kvx, gnear, gfar, edges, gqd, ghid, w_query, w_key, w_value, pool_key, pool_value
+        x, nrm, gain_one, kvx, gnear, gfar, edges, gqd, ghid, w_query, w_key, w_value, pool_key, pool_value
     )
-    grads = (actt, gpre, n2t, cot, mixt, gbr, nrmt, gq, gw, veca, vecb)
-    dense_args = (x, q, kvx, pkvx, w_attn_out, b_attn_out, gain_two, shift_two, w_in, b_in, w_out, b_out)
-    if groups is None:
-        output = dense(n_seq, *dense_args)
-        reduced = plain_reduce(*grads)
-    else:
-        output, *finals = reduce_all(n_seq, grads, dense_args)
-        reduced = unpack(*finals)
+    output = dense(
+        n_seq, x, q, kvx, pkvx, w_attn_out, b_attn_out, gain_two, shift_two, w_in, b_in, w_out, b_out
+    )
+    reduced = plain_reduce(actt, gpre, n2t, cot, mixt, gbr, nrmt, gq, gw, veca, vecb)
     return (output[None], grad_input[None]) + tuple(reduced)
 
 

time: 189 us -> 150 us (0.79)
  Pallas kernels: 185 us -> 147 us
  local copies, waits for them, and re-layouts: 2.06 us -> 0 us
    pallas_call x6 -> x4, Pallas kernels: 174 us -> 136 us  [the longest x1 107 us: tail(): pl.pallas_call(functools.partial(tail_kernel, count), out_shape=(struct((...]
    unnamed x1 -> x0, local copies, waits for them, and re-layouts: 2.06 us -> none
where the time goes in v3:
time: 150 us; the launch traced here: 148 us
  Pallas kernels  147 us (98%)
    pallas_call x1, Pallas kernels, tail(): pl.pallas_call(functools.partial(tail_kernel, count), out_shape=(struct((...  107 us
    pallas_call x1, Pallas kernels, front(): pl.pallas_call(functools.partial(front_kernel, count), out_shape=(struct(...  17 us
    pallas_call x1, Pallas kernels, halo(): pl.pallas_call(functools.partial(halo_kernel, count), out_shape=(struct((...  11.4 us
    pallas_call x1, Pallas kernels, project(): pl.pallas_call(project_kernel, out_shape=(struct((D, tok), BF16), struct(...  7.7 us
    pallas_call x1, Pallas kernels, unpack(): pl.pallas_call(unpack_kernel, out_shape=(struct(output.shape, BF16), stru...  4.01 us

profile of v3, /device:TPU:8, one launch (start us, length us, event | category | flops | bytes accessed | tf_op | source)
XLA Modules:
  0.0 148.2 jit_solution(2624188600495450876)
XLA Ops:
  0.7 7.7 %project.1 = (bf16[768,512]{1,0:T(8,128)(2,1)}, bf16[512,768]{1,0:T(8,128)(2,1)}, bf16[512,1536]{1,0:T(8,128)(2,1)}, bf16[128,1536]{1,0:T(8,128)(2,1)}) custom-call(bf16[512,768]{1,0:T(8,128)(2,1)} %bitcast.4, bf16[768]{0:T(1024)(128)(2,1)} %g1_ref.1, bf16[768]{0:T(1024)(128)(2,1)} %s_ref.1, bf16[768,768]{1,0:T(8,128)(2,1)} %wq_hbm.1, ...), custom_call_target="tpu_custom_call" | custom-call | tf_op jit(solution)/shard_map/project/pallas_call | solution.py:140
  8.4 11.4 %halo.1 = (bf16[640,1536]{1,0:T(8,128)(2,1)}, bf16[256,1536]{1,0:T(8,128)(2,1)}) custom-call(bf16[512,1536]{1,0:T(8,128)(2,1)} %get-tuple-element.66.kv_ref, bf16[128,1536]{1,0:T(8,128)(2,1)} %get-tuple-element.67.pkv_ref, bf16[5,768]{1,0:T(8,128)(2,1)} %pk_ref.5, bf16[5,768]{1,0:T(8,128)(2,1)} %pv_ref.5), custom_call_target="tpu_custom_call" | custom-call | tf_op jit(solution)/shard_map/halo/pallas_call | solution.py:255
  19.8 17.0 %masked_rows.1 = (bf16[2,2,768,128]{3,2,1,0:T(8,128)(2,1)}, bf16[2,128,1536]{2,1,0:T(8,128)(2,1)}, bf16[2,384,128]{2,1,0:T(8,128)(2,1)}, bf16[128,768]{1,0:T(8,1...) custom-call(bf16[512,768]{1,0:T(8,128)(2,1)} %bitcast.5, ...), custom_call_target="tpu_custom_call" | custom-call | tf_op jit(solution)/shard_map/masked_rows/pallas_call | solution.py:843
  36.8 107.2 %tail.1 = (bf16[512,768]{1,0:T(8,128)(2,1)}, f32[512,768]{1,0:T(8,128)}, bf16[2,96,768]{2,1,0:T(8,128)(2,1)}, bf16[2,48,1536]{2,1,0:T(8,128)(2,1)}, bf16[2,2,48,...) custom-call(bf16[2,2,768,128]{3,2,1,0:T(8,128)(2,1)} %get-tuple-element.70.actt, ...), custom_call_target="tpu_custom_call" | custom-call | tf_op jit(solution)/shard_map/tail/pallas_call | solution.py:1345
  144.0 4.0 %unpack.1 = (bf16[512,768]{1,0:T(8,128)(2,1)}, f32[512,768]{1,0:T(8,128)}, f32[48]{0:T(128)}, f32[48]{0:T(128)}, f32[48,768]{1,0:T(8,128)}, /*index=5*/f32[48]{0...) custom-call(bf16[512,768]{1,0:T(8,128)(2,1)} %get-tuple-element.83.o, ...), custom_call_target="tpu_custom_call" | custom-call | tf_op jit(solution)/shard_map/unpack/pallas_call | solution.py:1416

commit v4 on v3

--- a/solution.py
+++ b/solution.py
@@ -624,13 +624,15 @@
     near_keys, far_keys = block + WIN, (block + POOL_SPAN) // STRIDE
     step = block // STRIDE
     blocks = tok // block
-    load_in = pltpu.make_async_copy(win_hbm, win_ref, sems.at[0])
-    load_out = pltpu.make_async_copy(wout_hbm, wout_ref, sems.at[1])
+    weights = []
+    if sems is not None:
+        weights.append(pltpu.make_async_copy(win_hbm, win_ref, sems.at[0]))
+        weights.append(pltpu.make_async_copy(wout_hbm, wout_ref, sems.at[1]))
 
     def begin():
         s = lax.axis_index("seq")
-        load_in.start()
-        load_out.start()
+        for copy in weights:
+            copy.start()
         bin_row[...] = row_of(bin_ref)
         for b in range(blocks):
             pos = b * block + lax.broadcasted_iota(jnp.int32, (block, 1), 0)
@@ -666,8 +668,8 @@
             return carry
 
         lax.fori_loop(0, blocks, one, 0)
-        load_in.wait()
-        load_out.wait()
+        for copy in weights:
+            copy.wait()
 
     def feed(first, last):
         high_rows = 256
@@ -746,153 +748,25 @@
             ref[core, at : at + SH, :] = values[start : start + SH]
 
 
-def front_kernel(
+COPIES = 80
+LOADS = 16
+LAYER_VMEM = 65472 * 1024
+
+
+def layer_kernel(
     count,
-    x_ref, nrmt_full, q_ref, kvx_ref, pkvx_ref, slots_ref, cotr_ref, wo_ref, bo_ref, g2_ref, s2_ref,
-    win_hbm, bin_ref, wout_hbm,
-    actt_ref, gpre_ref, n2t_ref, cot_ref, mixt_ref, gbr_ref, nrmt_ref, qm_ref, gm_ref, wn_ref, wf_ref,
-    ghid_ref, veca_ref,
-    win_ref, wout_ref, mix_ref, nbias_ref, fbias_ref, n2_ref, acc_ref, bin_row, sems,
-):
-    s = lax.axis_index("seq")
-    bin_row[...] = row_of(bin_ref)
-    tok = x_ref.shape[0]
-    cap = cotr_ref.shape[0]
-    near_keys, far_keys = kvx_ref.shape[0], pkvx_ref.shape[0]
-    load_in = pltpu.make_async_copy(win_hbm, win_ref, sems.at[0])
-    load_out = pltpu.make_async_copy(wout_hbm, wout_ref, sems.at[1])
-    load_in.start()
-    load_out.start()
-
-    slots = slots_ref[0, 0].reshape(1, cap)
-    onehot_t = jnp.where(lax.broadcasted_iota(jnp.int32, (tok, cap), 0) == slots, 1.0, 0.0).astype(BF16)
-    slot_col = jnp.transpose(jnp.broadcast_to(slots, (cap, cap)))[:, 0:1]
-    x_rows = dot_tn(onehot_t, x_ref[...])
-    qm_ref[...] = (dot_tn(onehot_t, q_ref[...]) * (HD**-0.5)).astype(BF16)
-    store_rows(nrmt_ref, dot_nn(nrmt_full[...], onehot_t).astype(BF16))
-    cot_ref[...] = jnp.where(slot_col >= 0, cotr_ref[...].astype(F32), 0.0).astype(BF16)
-
-    nbias, fbias = window_biases(count, s, slot_col, near_keys, 0, far_keys, 0, tok)
-    nbias_ref[...] = nbias
-    fbias_ref[...] = fbias
-    low, high = head_masks()
-
-    def attend(p, carry):
-        c, cv = cols(p), cols(p + PAIRS)
-        qs = stack_pair(qm_ref[:, c], low, high)
-        nb, fb = nbias_ref[...], fbias_ref[...]
-        near_w = softmax_rows(dot_nt(qs, kvx_ref[:, c]) + jnp.concatenate([nb, nb], axis=0)).astype(BF16)
-        wn_ref[p] = near_w
-        far_w = softmax_rows(dot_nt(qs, pkvx_ref[:, c]) + jnp.concatenate([fb, fb], axis=0)).astype(BF16)
-        wf_ref[p] = far_w
-        out = dot_nn(near_w, kvx_ref[:, cv]) + dot_nn(far_w, pkvx_ref[:, cv])
-        mix_ref[:, c] = merge_pair(out).astype(BF16)
-        return carry
-
-    lax.fori_loop(0, PAIRS, attend, 0)
-    mixed = mix_ref[...]
-    store_rows(mixt_ref, jnp.transpose(mixed.astype(F32)).astype(BF16))
-    hidden = x_rows + dot_nn(mixed, wo_ref[...]) + row_of(bo_ref)
-    gain_two = row_of(g2_ref)
-    n_two, inv_two = norm_stats(hidden)
-    normed_two = n_two * gain_two + row_of(s2_ref)
-    n2_ref[...] = normed_two.astype(BF16)
-    store_rows(n2t_ref, jnp.transpose(normed_two).astype(BF16))
-    acc_ref[...] = jnp.zeros_like(acc_ref)
-    veca_ref[...] = jnp.zeros_like(veca_ref)
-    load_in.wait()
-    load_out.wait()
-    half_tiles = FF // FF_TILE // 2
-
-    def feed(t, carry):
-        c = cols(t, FF_TILE)
-        pre = dot_nn(n2_ref[...], win_ref[:, c]) + bin_row[:, c]
-        cdf = 0.5 * (1.0 + lax.erf(pre * SQRT_HALF))
-        act_t = jnp.transpose(pre * cdf).astype(BF16)
-        at = rows_at(place(t) * PART, PART, PART)
-        for core in range(2):
-            for half in range(2):
-                start = (2 * core + half) * PART
-                actt_ref[core, half, at, :] = act_t[start : start + PART]
-        slope = cdf + pre * (INV_SQRT_2PI * jnp.exp(-0.5 * pre * pre))
-        grad_act = dot_nt(cot_ref[...], wout_ref[rows_at(t * FF_TILE, FF_TILE, FF_TILE), :])
-        gpre = (grad_act * slope).astype(BF16)
-        gpre_ref[t // half_tiles, :, cols(t % half_tiles, FF_TILE)] = gpre
-        veca_ref[pl.ds(8 + t // 2, 1), cols(t % 2, FF_TILE)] = col_sum(gpre.astype(F32))
-        acc_ref[...] += dot_nt(gpre, win_ref[:, c])
-        return carry
-
-    lax.fori_loop(0, FF // FF_TILE, feed, 0)
-    cot = cot_ref[...].astype(F32)
-    grad_n2 = acc_ref[...]
-    grad_hidden = cot + norm_back(n_two, inv_two, gain_two, grad_n2)
-    ghid_ref[...] = grad_hidden
-    grad_branch = grad_hidden.astype(BF16)
-    gbr_ref[...] = grad_branch
-    gm_ref[...] = dot_nt(grad_branch, wo_ref[...]).astype(BF16)
-    veca_ref[1:2, :] = col_sum(grad_branch.astype(F32))
-    veca_ref[2:3, :] = col_sum(grad_n2 * n_two)
-    veca_ref[3:4, :] = col_sum(grad_n2)
-    veca_ref[4:5, :] = col_sum(cot)
-
-
-def front(count, x, nrmt, q, kvx, pkvx, slots, cot_rows, wo, bo, g2, s2, w_in, b_in, w_out):
-    cap = cot_rows.shape[0]
-    near_keys, far_keys = kvx.shape[0], pkvx.shape[0]
-    rows_t = (2, D // 2, cap)
-    return pl.pallas_call(
-        functools.partial(front_kernel, count),
-        out_shape=(
-            struct((2, 2, FF // 4, cap), BF16),
-            struct((2, cap, FF // 2), BF16),
-            struct(rows_t, BF16),
-            struct((cap, D), BF16),
-            struct(rows_t, BF16),
-            struct((cap, D), BF16),
-            struct(rows_t, BF16),
-            struct((cap, D), BF16),
-            struct((cap, D), BF16),
-            struct((PAIRS, 2 * cap, near_keys), BF16),
-            struct((PAIRS, 2 * cap, far_keys), BF16),
-            struct((cap, D), F32),
-            struct((16, D), F32),
-        ),
-        in_specs=[VMEM] * 11 + [ANY, VMEM, ANY],
-        out_specs=(VMEM,) * 13,
-        scratch_shapes=[
-            pltpu.VMEM((D, FF), BF16),
-            pltpu.VMEM((FF, D), BF16),
-            pltpu.VMEM((cap, D), BF16),
-            pltpu.VMEM((cap, near_keys), F32),
-            pltpu.VMEM((cap, far_keys), F32),
-            pltpu.VMEM((cap, D), BF16),
-            pltpu.VMEM((cap, D), F32),
-            pltpu.VMEM((1, FF), F32),
-            pltpu.SemaphoreType.DMA((2,)),
-        ],
-        compiler_params=pltpu.CompilerParams(vmem_limit_bytes=VMEM_LIMIT),
-        name="masked_rows",
-    )(x, nrmt, q, kvx, pkvx, slots, cot_rows, wo, bo, g2, s2, w_in, b_in, w_out)
-
-
-COPIES = 80
-LOADS = 24
-
-
-def tail_kernel(
-    count,
-    actt, gpre, n2t, cot, mixt, gbr, nrmt, qm_hbm, gm_hbm, wn_hbm, wf_hbm, ghid_hbm, veca,
-    x_hbm, nrmt_hbm, q_hbm, kvx_hbm, pkvx_hbm, wq_hbm, wk_hbm, wv_hbm, wo_hbm, win_hbm, wout_hbm,
-    slots_ref, bo_ref, g1_ref, g2_ref, s2_ref, bin_ref, bout_ref, pk_ref, pv_ref,
+    x_hbm, cotr_hbm, wq_hbm, wk_hbm, wv_hbm, wo_hbm, win_hbm, wout_hbm,
+    slots_ref, g1_ref, s1_ref, bq_ref, bv_ref, bo_ref, g2_ref, s2_ref, bin_ref, bout_ref, pk_ref, pv_ref,
     out_ref, gin_ref, f_out, f_in, f_oq, f_kv, f_vec,
-    qm, gm, wn, wf, ghid, x_ref, nrmt_full, q_ref, kvx_ref, pkvx_ref, wq_ref, wk_ref, wv_ref, wo_ref,
+    x_ref, nrm_ref, nrmt_full, q_ref, kvx_ref, pkvx_ref, wq_ref, wk_ref, wv_ref, wo_ref, cotr_ref,
+    actt, gpre, n2t, cot, mixt, gbr, nrmt, qm, gm, wn, wf, ghid, mixm, nbias_m, fbias_m, n2m, accm,
     hb, ha, rb, ra, gown, fown, keys, grads, gkv_ref, gq_ref,
     a_all, c_all, n_all, p_all, a_fwd, n_fwd, m_all, b_all, r_all, g_all,
     va_rx, vb_rx, vecb_ref, vs, vy_rx, vx_rx, vz_rx,
     gw, kv_rx, kv_s, kv_xr, kv_t, kv_yr, kv_z, kv_zr,
     att, att_y, att_x, att_xr, att_z, att_zr,
     wo_g, wo_y, wo_z, wo_zr, wi_g, wi_y, wi_z, wi_zr,
-    send, recv, hsend, hrecv, ksend, krecv, loads, *dense_refs,
+    send, recv, hsend, hrecv, ksend, krecv, fsend, frecv, loads, *dense_refs,
 ):
     cap = ghid.shape[0]
     tok = x_ref.shape[0]
@@ -934,25 +808,6 @@
     def slab(g):
         return pl.ds(cap * g, cap)
 
-    first = [load(qm_hbm, qm), load(gm_hbm, gm), load(wn_hbm, wn), load(wf_hbm, wf)]
-    first += [load(kvx_hbm, kvx_ref), load(pkvx_hbm, pkvx_ref)]
-    own_o = [load(mixt.at[c], m_all.at[:, lane(0)]), load(gbr, b_all.at[slab(0)])]
-    own_q = load(nrmt.at[c], r_all.at[:, lane(0)])
-    own_out = [load(actt.at[c, d], a_all.at[:, lane(0)]), load(cot, c_all.at[slab(0)])]
-    own_in = [load(n2t.at[c], n_all.at[:, lane(0)]), load(gpre.at[d], p_all.at[slab(0)])]
-    second = [load(nrmt_hbm, nrmt_full)]
-    third = [load(wq_hbm, wq_ref), load(wk_hbm, wk_ref), load(wv_hbm, wv_ref), load(x_hbm, x_ref)]
-    third += [load(ghid_hbm, ghid), load(veca, vecb_ref.at[pl.ds(16, 16)])]
-    fourth = [load(q_hbm, q_ref), load(wo_hbm, wo_ref)]
-
-    @pl.when(has_far)
-    def _():
-        pl.semaphore_wait(barrier, len(peers) + 1)
-
-    @pl.when(jnp.logical_not(has_far))
-    def _():
-        pl.semaphore_wait(barrier, len(peers))
-
     used = [0]
     started = []
 
@@ -972,27 +827,234 @@
         for copy in copies:
             copy.wait()
 
+    (win_ref, wout_ref), acc_ref = dense_refs[:2], dense_refs[6]
     begin, attend, blocks, residual, feed, end = dense_parts(
-        count, x_ref, q_ref, kvx_ref, pkvx_ref, wo_ref, bo_ref, g2_ref, s2_ref, win_hbm, bin_ref, wout_hbm,
-        bout_ref, out_ref, *dense_refs
+        count, x_ref, q_ref, kvx_ref, pkvx_ref, wo_ref, bo_ref, g2_ref, s2_ref, None, bin_ref, None,
+        bout_ref, out_ref, *dense_refs, None
     )
-    acc_ref = dense_refs[6]
-
-    out_x = [
-        go(actt.at[c, f], a_all.at[:, lane(2)], x_dev),
-        go(actt.at[e, f], a_fwd, x_dev),
-        go(cot, c_all.at[slab(2)], x_dev),
-    ]
-    o_core = [go(mixt.at[e], m_all.at[:, lane(1)], core_dev), go(gbr, b_all.at[slab(1)], core_dev)]
+    bin_row = dense_refs[7]
+
+    x_load = [load(x_hbm, x_ref)]
+    kv_load = [load(wk_hbm, wk_ref), load(wv_hbm, wv_ref)]
+    cot_load = [load(cotr_hbm, cotr_ref)]
+    q_load = [load(wq_hbm, wq_ref)]
+    zero_rows = jnp.zeros((8, 128), F32)
+    keys[0:8, :] = zero_rows
+    grads[0:8, :] = zero_rows
+    vecb_ref[...] = jnp.zeros_like(vecb_ref)
+
+    @pl.when(has_far)
+    def _():
+        pl.semaphore_wait(barrier, len(peers) + 1)
+
+    @pl.when(jnp.logical_not(has_far))
+    def _():
+        pl.semaphore_wait(barrier, len(peers))
+
+    wait(x_load)
+    n_one, _ = norm_stats(x_ref[...].astype(F32))
+    nrm_ref[...] = (n_one * row_of(g1_ref) + row_of(s1_ref)).astype(BF16)
+    width = 256
+    inner = pl.ds(HALF, tok)
+    wait(kv_load)
+
+    def key_tile(j, carry):
+        cc = cols(j, width)
+        nrm = nrm_ref[...]
+        kvx_ref[inner, cc] = dot_nn(nrm, wk_ref[:, cc]).astype(BF16)
+        vals = dot_nn(nrm, wv_ref[:, cc]) + row_of(bv_ref.at[cc])
+        kvx_ref[inner, cols(j + D // width, width)] = vals.astype(BF16)
+        return carry
+
+    lax.fori_loop(0, D // width, key_tile, 0)
+    slots = slots_ref[0, 0].reshape(1, cap)
+    slot_col = jnp.transpose(jnp.broadcast_to(slots, (cap, cap)))[:, 0:1]
+    wait(cot_load)
+    cot[...] = jnp.where(slot_col >= 0, cotr_ref[...].astype(F32), 0.0).astype(BF16)
+
+    def edges(i, ref, edge, size):
+        return (
+            remote(ref.at[pl.ds(edge, edge)], ref.at[pl.ds(edge + size, edge)], fsend.at[i], frecv.at[i], before),
+            remote(ref.at[pl.ds(size, edge)], ref.at[pl.ds(0, edge)], fsend.at[i + 1], frecv.at[i + 1], after),
+        )
+
+    near_edge = edges(0, kvx_ref, HALF, tok)
+    far_edge = edges(2, pkvx_ref, REACH, pooled)
+
+    def both(pair, act_before, act_after):
+        @pl.when(has_before)
+        def _():
+            act_before(pair)
+
+        @pl.when(has_after)
+        def _():
+            act_after(pair)
+
+    def start_edges(pair):
+        both(pair, lambda p: p[0].start(), lambda p: p[1].start())
+
+    def wait_edges(pair):
+        both(
+            pair,
+            lambda p: (p[0].wait_send(), p[1].wait_recv()),
+            lambda p: (p[1].wait_send(), p[0].wait_recv()),
+        )
+
+    wo_load = [load(wo_hbm, wo_ref)]
+    ff_load = [load(win_hbm, win_ref), load(wout_hbm, wout_ref)]
+    start_edges(near_edge)
+    out_x = [go(cot, c_all.at[slab(2)], x_dev)]
+    out_core = [go(cot, c_all.at[slab(1)], core_dev)]
+    own_out = [load(cot, c_all.at[slab(0)])]
+    for base, taps_ref in ((0, pk_ref), (D // 128, pv_ref)):
+
+        def shrink(j, carry):
+            taps = taps_ref[:, cols(j)].astype(F32)
+            keys[8 : 8 + tok, :] = kvx_ref[inner, cols(base + j)].astype(F32)
+            total = jnp.zeros((pooled, 128), F32)
+            for t in range(KERNEL):
+                total = total + keys[pl.ds(6 + t, pooled, stride=STRIDE), :] * taps[t : t + 1]
+            pkvx_ref[REACH : REACH + pooled, cols(base + j)] = total.astype(BF16)
+            return carry
+
+        lax.fori_loop(0, D // 128, shrink, 0)
+
+    @pl.when(jnp.logical_not(has_before))
+    def _():
+        kvx_ref[0:HALF, :] = jnp.zeros((HALF, 2 * D), BF16)
+        pkvx_ref[0:REACH, :] = jnp.zeros((REACH, 2 * D), BF16)
+        rb[...] = jnp.zeros_like(rb)
+
+    @pl.when(jnp.logical_not(has_after))
+    def _():
+        kvx_ref[HALF + tok :, :] = jnp.zeros((HALF, 2 * D), BF16)
+        pkvx_ref[REACH + pooled :, :] = jnp.zeros((REACH, 2 * D), BF16)
+        ra[...] = jnp.zeros_like(ra)
+
+    start_edges(far_edge)
+
+    wait(q_load)
+
+    def query_tile(j, carry):
+        cc = cols(j, width)
+        qs = dot_nn(nrm_ref[...], wq_ref[:, cc]) + row_of(bq_ref.at[cc])
+        q_ref[:, cc] = qs.astype(BF16)
+        return carry
+
+    lax.fori_loop(0, D // width, query_tile, 0)
+    nrmt_full[...] = jnp.transpose(nrm_ref[...].astype(F32)).astype(BF16)
+    onehot_t = jnp.where(lax.broadcasted_iota(jnp.int32, (tok, cap), 0) == slots, 1.0, 0.0).astype(BF16)
+    store_rows(nrmt, dot_nn(nrmt_full[...], onehot_t).astype(BF16))
+    x_rows = dot_tn(onehot_t, x_ref[...])
+    qm[...] = (dot_tn(onehot_t, q_ref[...]) * (HD**-0.5)).astype(BF16)
+    near_keys, far_keys = kvx_ref.shape[0], pkvx_ref.shape[0]
+    nbias, fbias = window_biases(count, s, slot_col, near_keys, 0, far_keys, 0, tok)
+    nbias_m[...] = nbias
+    fbias_m[...] = fbias
     q_core = [go(nrmt.at[e], r_all.at[:, lane(1)], core_dev)]
-    out_core = [go(actt.at[e, d], a_all.at[:, lane(1)], core_dev), go(cot, c_all.at[slab(1)], core_dev)]
-    in_x = [
-        go(n2t.at[c], n_all.at[:, lane(2)], x_dev),
-        go(n2t.at[e], n_fwd, x_dev),
-        go(gpre.at[f], p_all.at[slab(2)], x_dev),
-    ]
-    in_core = [go(n2t.at[e], n_all.at[:, lane(1)], core_dev), go(gpre.at[d], p_all.at[slab(1)], core_dev)]
-    vec_core = [go(veca, va_rx, core_dev)]
+    own_q = [load(nrmt.at[c], r_all.at[:, lane(0)])]
+    begin()
+    wait_edges(near_edge)
+    wait_edges(far_edge)
+    tap_rows = jnp.concatenate([pk_ref[...].astype(F32), pv_ref[...].astype(F32)], axis=1)
+
+    def fix(key_row, pooled_row):
+        near = kvx_ref[key_row - 16 : key_row + 16, :].astype(F32)[14 : 14 + KERNEL]
+        value = jnp.sum(near * tap_rows, axis=0, keepdims=True)
+        old = pkvx_ref[pooled_row : pooled_row + 16, :].astype(F32)
+        row = lax.broadcasted_iota(jnp.int32, (16, 1), 0)
+        pkvx_ref[pooled_row : pooled_row + 16, :] = jnp.where(row == 0, value, old).astype(BF16)
+
+    fix(HALF, REACH)
+
+    @pl.when(has_after)
+    def _():
+        fix(HALF + tok, REACH + pooled)
+
+    arrive(out_x)
+    out_fwd = [go(c_all.at[slab(2)], c_all.at[slab(3)], core_dev)]
+    low, high = head_masks()
+
+    def attend_rows(p, carry):
+        cc, cv = cols(p), cols(p + PAIRS)
+        qs = stack_pair(qm[:, cc], low, high)
+        nb, fb = nbias_m[...], fbias_m[...]
+        near_w = softmax_rows(dot_nt(qs, kvx_ref[:, cc]) + jnp.concatenate([nb, nb], axis=0)).astype(BF16)
+        wn[p] = near_w
+        far_w = softmax_rows(dot_nt(qs, pkvx_ref[:, cc]) + jnp.concatenate([fb, fb], axis=0)).astype(BF16)
+        wf[p] = far_w
+        mixed_pair = dot_nn(near_w, kvx_ref[:, cv]) + dot_nn(far_w, pkvx_ref[:, cv])
+        mixm[:, cc] = merge_pair(mixed_pair).astype(BF16)
+        return carry
+
+    lax.fori_loop(0, PAIRS, attend_rows, 0)
+    wait(wo_load)
+    mixed = mixm[...]
+    store_rows(mixt, jnp.transpose(mixed.astype(F32)).astype(BF16))
+    hidden = x_rows + dot_nn(mixed, wo_ref[...]) + row_of(bo_ref)
+    gain_two = row_of(g2_ref)
+    n_two, inv_two = norm_stats(hidden)
+    normed_two = n_two * gain_two + row_of(s2_ref)
+    n2m[...] = normed_two.astype(BF16)
+    store_rows(n2t, jnp.transpose(normed_two).astype(BF16))
+    o_core = [go(mixt.at[e], m_all.at[:, lane(1)], core_dev)]
+    own_o = [load(mixt.at[c], m_all.at[:, lane(0)])]
+    accm[...] = jnp.zeros_like(accm)
+    wait(ff_load)
+    in_x = [go(n2t.at[e], n_fwd, x_dev), go(n2t.at[c], n_all.at[:, lane(2)], x_dev)]
+    in_core = [go(n2t.at[e], n_all.at[:, lane(1)], core_dev)]
+    own_in = [load(n2t.at[c], n_all.at[:, lane(0)])]
+    tiles = FF // FF_TILE
+    half_tiles = tiles // 2
+
+    def feed_rows(i, carry):
+        t = (i % NZ) * 2 + i // NZ
+        cc = cols(t, FF_TILE)
+        pre = dot_nn(n2m[...], win_ref[:, cc]) + bin_row[:, cc]
+        cdf = 0.5 * (1.0 + lax.erf(pre * SQRT_HALF))
+        act_t = jnp.transpose(pre * cdf).astype(BF16)
+        at = rows_at(i * PART, PART, PART)
+        for core in range(2):
+            for half in range(2):
+                start = (2 * core + half) * PART
+                actt[core, half, at, :] = act_t[start : start + PART]
+        slope = cdf + pre * (INV_SQRT_2PI * jnp.exp(-0.5 * pre * pre))
+        grad_act = dot_nt(cot[...], wout_ref[rows_at(t * FF_TILE, FF_TILE, FF_TILE), :])
+        grad_pre = (grad_act * slope).astype(BF16)
+        gpre[t // half_tiles, :, cols(t % half_tiles, FF_TILE)] = grad_pre
+        vecb_ref[pl.ds(24 + t // 2, 1), cols(t % 2, FF_TILE)] = col_sum(grad_pre.astype(F32))
+        accm[...] += dot_nt(grad_pre, win_ref[:, cc])
+        return carry
+
+    out_half = NZ * PART
+
+    def send_act(k):
+        r = pl.ds(k * out_half, out_half)
+        out_x.append(go(actt.at[e, f, r], a_fwd.at[r], x_dev))
+        out_x.append(go(actt.at[c, f, r], a_all.at[r, lane(2)], x_dev))
+
+    lax.fori_loop(0, NZ, feed_rows, 0)
+    send_act(0)
+    lax.fori_loop(NZ, tiles, feed_rows, 0)
+    cot_f = cot[...].astype(F32)
+    grad_n2 = accm[...]
+    grad_hidden = cot_f + norm_back(n_two, inv_two, gain_two, grad_n2)
+    send_act(1)
+    in_x.append(go(gpre.at[f], p_all.at[slab(2)], x_dev))
+    out_core.append(go(actt.at[e, d], a_all.at[:, lane(1)], core_dev))
+    own_out.append(load(actt.at[c, d], a_all.at[:, lane(0)]))
+    in_core.append(go(gpre.at[d], p_all.at[slab(1)], core_dev))
+    own_in.append(load(gpre.at[d], p_all.at[slab(0)]))
+    ghid[...] = grad_hidden
+    grad_branch = grad_hidden.astype(BF16)
+    gbr[...] = grad_branch
+    gm[...] = dot_nt(grad_branch, wo_ref[...]).astype(BF16)
+    vecb_ref[17:18, :] = col_sum(grad_branch.astype(F32))
+    vecb_ref[18:19, :] = col_sum(grad_n2 * n_two)
+    vecb_ref[19:20, :] = col_sum(grad_n2)
+    vecb_ref[20:21, :] = col_sum(cot_f)
+    o_core.append(go(gbr, b_all.at[slab(1)], core_dev))
+    own_o.append(load(gbr, b_all.at[slab(0)]))
 
     def to_before(p):
         return remote(hb.at[p], ra.at[p], hsend.at[p], hrecv.at[p], before)
@@ -1011,9 +1073,6 @@
 
     def pair_at(i):
         return (i + (PAIRS // 2) * f) % PAIRS
-
-    wait(first)
-    low, high = head_masks()
 
     def attend_back(i, carry):
         p = pair_at(i)
@@ -1046,39 +1105,30 @@
             fown[p, :, lane(h)] = far[REACH : REACH + pooled + 16]
         return carry
 
-    lax.fori_loop(0, PAIRS, attend_back, 0)
     rows = NZ * SH
 
     def halves(values, g):
         att[0, g] = values[:rows].astype(BF16)
         att[1, g] = values[rows:].astype(BF16)
 
+    lax.fori_loop(0, 2, attend_back, 0)
+    arrive(in_x[:1])
+    in_fwd = [go(n_fwd, n_all.at[:, lane(3)], core_dev)]
     wait(own_o)
-    own_q.wait()
     arrive(o_core)
     halves(dot_nn(m_all[...], b_all[...]), 0)
+    lax.fori_loop(2, 3, attend_back, 0)
+    att_to_y = [go(att.at[w, 0], att_y.at[0], y_dev)]
+    lax.fori_loop(3, PAIRS, attend_back, 0)
+    vec_core = [go(vecb_ref.at[pl.ds(16, 16)], va_rx, core_dev)]
     g_all[slab(0), :] = gq_ref[...]
-    vecb_ref[0:16, :] = jnp.zeros((16, D), F32)
+    vecb_ref[13:14, :] = col_sum(gq_ref[...].astype(F32))
     send_halo(pair_at(PAIRS - 1))
     q_core.append(go(gq_ref, g_all.at[slab(1)], core_dev))
-    wait(second)
-
-    @pl.when(jnp.logical_not(has_before))
-    def _():
-        rb[...] = jnp.zeros_like(rb)
-
-    @pl.when(jnp.logical_not(has_after))
-    def _():
-        ra[...] = jnp.zeros_like(ra)
-
-    vecb_ref[13:14, :] = col_sum(gq_ref[...].astype(F32))
-    arrive(q_core)
-    halves(dot_nn(r_all[...], g_all[...]), 1)
 
     def kv_copy(p):
         return remote(gw.at[p, e], kv_rx.at[p], ksend.at[p], krecv.at[p], core_dev)
 
-    grads[0:8, :] = jnp.zeros((8, 128), F32)
     half_pool = pooled - REACH
 
     def pool(i, carry):
@@ -1136,25 +1186,18 @@
     def pool_range(a, b):
         lax.fori_loop(a, b, pool, 0)
 
-    att_to_y = [go(att.at[w], att_y, y_dev)]
-    pool_range(0, 2)
-    arrive(out_x)
-    out_fwd = [go(a_fwd, a_all.at[:, lane(3)], core_dev), go(c_all.at[slab(2)], c_all.at[slab(3)], core_dev)]
-    pool_range(2, PAIRS)
-
-    wait(own_out)
-    arrive(out_core + out_fwd)
-    kv_copy(pair_at(PAIRS - 1)).start()
-    quarter = NZ * PART // 2
+    quarter = out_half // 2
 
     def out_product(i, carry):
         r = rows_at(i * quarter, quarter, quarter)
         wo_g[i // 2, rows_at((i % 2) * quarter, quarter, quarter), :] = dot_nn(a_all[r, :], c_all[...]).astype(BF16)
         return carry
 
-    lax.fori_loop(0, 4, out_product, 0)
-    arrive(in_x)
-    in_fwd = [go(n_fwd, n_all.at[:, lane(3)], core_dev), go(p_all.at[slab(2)], p_all.at[slab(3)], core_dev)]
+    def in_product(i, carry):
+        r = rows_at((i // 4) * rows, rows, rows)
+        cc = cols(i % 4, FF // 8)
+        wi_g[i // 4, :, cc] = dot_nn(n_all[r, :], p_all[:, cc]).astype(BF16)
+        return carry
 
     triple = PAIRS // 2
 
@@ -1164,16 +1207,36 @@
         kv_s[p] = (gw[p, c].astype(F32) + kv_rx[p].astype(F32)).astype(BF16)
         return carry
 
+    pool_range(0, 1)
+    wait(own_q)
+    arrive(q_core)
+    halves(dot_nn(r_all[...], g_all[...]), 1)
+    pool_range(1, 2)
+    att_to_y.append(go(att.at[w, 1], att_y.at[1], y_dev))
+    arrive(out_x[1:])
+    out_fwd.append(go(a_fwd, a_all.at[:, lane(3)], core_dev))
+    pool_range(2, 4)
+    wait(own_out)
+    arrive(out_core + out_fwd)
+    lax.fori_loop(0, 4, out_product, 0)
+    pool_range(4, 5)
+    out_to_y = [go(wo_g.at[w], wo_y, y_dev)]
+    arrive(in_x[1:])
+    in_fwd.append(go(p_all.at[slab(2)], p_all.at[slab(3)], core_dev))
+    pool_range(5, PAIRS)
     lax.fori_loop(0, triple, kv_sum, 0)
-    out_to_y = [go(wo_g.at[w], wo_y, y_dev)]
-    lax.fori_loop(triple, PAIRS, kv_sum, 0)
+    kv_copy(pair_at(PAIRS - 1)).start()
+    lax.fori_loop(triple, PAIRS - 1, kv_sum, 0)
+    wait(own_in)
+    arrive(in_core + in_fwd)
+    lax.fori_loop(0, 8, in_product, 0)
+    lax.fori_loop(PAIRS - 1, PAIRS, kv_sum, 0)
     kv_to_x = [go(kv_s.at[pl.ds(f * triple, triple)], kv_xr, x_dev)]
-
-    wait(third)
+    in_to_y = [go(wi_g.at[w], wi_y, y_dev)]
+
     high_part = ghid[...].astype(BF16)
     low_part = (ghid[...] - high_part.astype(F32)).astype(BF16)
     hid_parts = jnp.concatenate([high_part, low_part], axis=0)
-    width = 256
 
     def query_back(j, carry):
         gm_f = dot_nt(gq_ref[...], wq_ref[rows_at(j * width, width, width), :])
@@ -1183,8 +1246,7 @@
         return carry
 
     lax.fori_loop(0, D // width, query_back, 0)
-    slots = slots_ref[0, 0].reshape(1, cap)
-    slots = jnp.concatenate([slots, slots], axis=1)
+    slots_two = jnp.concatenate([slots, slots], axis=1)
 
     def back(j, carry):
         r = rows_at(j * width, width, width)
@@ -1199,7 +1261,7 @@
     def norm(j, sums):
         r = rows_at(j * block, block, block)
         at = j * block + lax.broadcasted_iota(jnp.int32, (block, 2 * cap), 0)
-        onehot = jnp.where(at == slots, 1.0, 0.0).astype(BF16)
+        onehot = jnp.where(at == slots_two, 1.0, 0.0).astype(BF16)
         n, inv = norm_stats(x_ref[r, :].astype(F32))
         grad = acc_ref[r, :] + dot_nn(onehot, b_all[...])
         gin_ref[r, :] = dot_nn(onehot, hid_parts) + norm_back(n, inv, gain, grad)
@@ -1213,21 +1275,6 @@
     sums = lax.fori_loop(0, tok // block, norm, (zero, zero, zero))
     for i in range(3):
         vecb_ref[i : i + 1, :] = sums[i]
-    wait(own_in)
-    arrive(in_core + in_fwd)
-
-    def in_product(i, carry):
-        r = rows_at((i // 4) * rows, rows, rows)
-        cc = cols(i % 4, FF // 8)
-        wi_g[i // 4, :, cc] = dot_nn(n_all[r, :], p_all[:, cc]).astype(BF16)
-        return carry
-
-    lax.fori_loop(0, 8, in_product, 0)
-    vec_core.append(go(vecb_ref.at[pl.ds(0, 16)], vb_rx, core_dev))
-    begin()
-    in_to_y = [go(wi_g.at[w], wi_y, y_dev)]
-    wait(fourth)
-    attend(0)
 
     arrive(att_to_y)
     wide = D // 2
@@ -1235,52 +1282,54 @@
         total = att[y, g].astype(F32) + att_y[g].astype(F32)
         att_x[0, g] = total[:, :wide].astype(BF16)
         att_x[1, g] = total[:, wide:].astype(BF16)
+    vec_core.append(go(vecb_ref.at[pl.ds(0, 16)], vb_rx, core_dev))
+    attend(0)
+    att_to_x = [go(att_x.at[f], att_xr, x_dev)]
     arrive(vec_core)
     vs[0, 0:16, :] = (vecb_ref[16:32, :] + va_rx[...]).astype(BF16)
     vs[0, 16:32, :] = (vecb_ref[0:16, :] + vb_rx[...]).astype(BF16)
+    arrive(out_to_y)
+    for zz in range(NZ):
+        r = pl.ds(zz * PART, PART)
+        wo_z[zz] = (wo_g[y, r].astype(F32) + wo_y[r].astype(F32)).astype(BF16)
+    attend(1)
+    vec_to_y = [go(vs.at[0], vy_rx, y_dev)]
+    out_to_z = [go(wo_z.at[z_at[t]], wo_zr.at[t], z_dev[t]) for t in range(NZ - 1)]
     arrive(kv_to_x)
     for q in range(triple):
         total = kv_s[d * triple + q].astype(F32) + kv_xr[q].astype(F32)
         kv_t[0, q] = total[:rows].astype(BF16)
         kv_t[1, q] = total[rows:].astype(BF16)
-    attend(1)
+    attend(2)
     kv_to_y = [go(kv_t.at[w], kv_yr, y_dev)]
-    vec_to_y = [go(vs.at[0], vy_rx, y_dev)]
-    att_to_x = [go(att_x.at[f], att_xr, x_dev)]
-    attend(2)
-    arrive(out_to_y)
+    arrive(in_to_y)
     for zz in range(NZ):
-        r = pl.ds(zz * PART, PART)
-        wo_z[zz] = (wo_g[y, r].astype(F32) + wo_y[r].astype(F32)).astype(BF16)
+        r = pl.ds(zz * SH, SH)
+        wi_z[zz] = (wi_g[y, r].astype(F32) + wi_y[r].astype(F32)).astype(BF16)
     attend(3)
-    out_to_z = [go(wo_z.at[z_at[t]], wo_zr.at[t], z_dev[t]) for t in range(NZ - 1)]
-    residual()
+    in_to_z = [go(wi_z.at[z_at[t]], wi_zr.at[t], z_dev[t]) for t in range(NZ - 1)]
     arrive(att_to_x)
     for zz in range(NZ):
         r = pl.ds(zz * SH, SH)
         for g in range(2):
             att_z[zz, g] = (att_x[d, g, r].astype(F32) + att_xr[g, r].astype(F32)).astype(BF16)
+    residual()
+    att_to_z = [go(att_z.at[z_at[t]], att_zr.at[t], z_dev[t]) for t in range(NZ - 1)]
     arrive(vec_to_y)
     vs[1] = (vs[0].astype(F32) + vy_rx[...].astype(F32)).astype(BF16)
-    feed(0, 2)
+    feed(0, 1)
     vec_to_x = [go(vs.at[1], vx_rx, x_dev)]
-    att_to_z = [go(att_z.at[z_at[t]], att_zr.at[t], z_dev[t]) for t in range(NZ - 1)]
-    feed(2, 4)
-    arrive(in_to_y)
-    for zz in range(NZ):
-        r = pl.ds(zz * SH, SH)
-        wi_z[zz] = (wi_g[y, r].astype(F32) + wi_y[r].astype(F32)).astype(BF16)
-    feed(4, 5)
-    in_to_z = [go(wi_z.at[z_at[t]], wi_zr.at[t], z_dev[t]) for t in range(NZ - 1)]
+    feed(1, 2)
     arrive(kv_to_y)
     for zz in range(NZ):
         r = pl.ds(zz * SH, SH)
         for q in range(triple):
             kv_z[zz, q] = (kv_t[y, q, r].astype(F32) + kv_yr[q, r].astype(F32)).astype(BF16)
+    feed(2, 3)
+    kv_to_z = [go(kv_z.at[z_at[t]], kv_zr.at[t], z_dev[t]) for t in range(NZ - 1)]
     arrive(vec_to_x)
     vs[2] = (vs[1].astype(F32) + vx_rx[...].astype(F32)).astype(BF16)
-    feed(5, 6)
-    kv_to_z = [go(kv_z.at[z_at[t]], kv_zr.at[t], z_dev[t]) for t in range(NZ - 1)]
+    feed(3, 4)
     vec_to_z = [go(vs.at[2], vz_rx.at[t], z_dev[t]) for t in range(NZ - 1)]
 
     def gathered(own, parts):
@@ -1291,20 +1340,26 @@
 
     last = []
 
-    def share(ref, value):
-        ref[d] = value.astype(BF16)
+    def share(ref):
         last.append(go(ref.at[d], ref.at[d], x_dev))
 
     arrive(out_to_z)
-    share(f_out, gathered(wo_z[z], wo_zr))
-    feed(6, 8)
+    f_out[d] = gathered(wo_z[z], wo_zr).astype(BF16)
+    feed(4, 5)
+    share(f_out)
+    arrive(in_to_z)
+    f_in[d] = gathered(wi_z[z], wi_zr).astype(BF16)
+    feed(5, 6)
+    share(f_in)
+    arrive(att_to_z)
+    f_oq[d] = gathered(att_z[z], att_zr).astype(BF16)
+    feed(6, 7)
+    share(f_oq)
+    arrive(kv_to_z)
+    f_kv[d] = gathered(kv_z[z], kv_zr).astype(BF16)
+    feed(7, 8)
+    share(f_kv)
     end()
-    arrive(att_to_z)
-    share(f_oq, gathered(att_z[z], att_zr))
-    arrive(in_to_z)
-    share(f_in, gathered(wi_z[z], wi_zr))
-    arrive(kv_to_z)
-    share(f_kv, gathered(kv_z[z], kv_zr))
     arrive(vec_to_z)
     f_vec[...] = gathered(vs[2], vz_rx)
     arrive(last)
@@ -1325,11 +1380,13 @@
     lax.fori_loop(0, PAIRS, drain, 0)
 
 
-def tail(count, rows, *args):
-    cap = rows[3].shape[0]
-    x, nrmt, q, kvx, pkvx = args[:5]
+def layer(
+    count, x, cot_rows, wq, wk, wv, wo, w_in, w_out, slots, g1, s1, bq, bv, bo, g2, s2, b_in, b_out, pk, pv
+):
+    cap = cot_rows.shape[0]
     tok = x.shape[0]
     pooled = tok // STRIDE
+    near_keys, far_keys = tok + WIN, pooled + 2 * REACH
     half, sums, triple = D // 2, NZ * SH, PAIRS // 2
 
     def b16(*shape):
@@ -1338,12 +1395,9 @@
     def f32(*shape):
         return pltpu.VMEM(shape, F32)
 
-    def like(a):
-        return pltpu.VMEM(a.shape, a.dtype)
-
     dma = pltpu.SemaphoreType.DMA
     return pl.pallas_call(
-        functools.partial(tail_kernel, count),
+        functools.partial(layer_kernel, count),
         out_shape=(
             struct((tok, D), BF16),
             struct((tok, D), F32),
@@ -1353,11 +1407,15 @@
             struct((2, triple, SH, PAIR), BF16),
             struct((32, D), F32),
         ),
-        in_specs=[ANY] * 24 + [VMEM] * 9,
+        in_specs=[ANY] * 8 + [VMEM] * 12,
         out_specs=(VMEM,) * 7,
         scratch_shapes=[
-            b16(cap, D), b16(cap, D), like(rows[9]), like(rows[10]), f32(cap, D), like(x), like(nrmt), like(q),
-            like(kvx), like(pkvx), b16(D, D), b16(D, D), b16(D, D), b16(D, D),
+            b16(tok, D), b16(tok, D), b16(D, tok), b16(tok, D), b16(near_keys, 2 * D), b16(far_keys, 2 * D),
+            b16(D, D), b16(D, D), b16(D, D), b16(D, D), b16(cap, D),
+            b16(2, 2, FF // 4, cap), b16(2, cap, FF // 2), b16(2, half, cap), b16(cap, D), b16(2, half, cap),
+            b16(cap, D), b16(2, half, cap), b16(cap, D), b16(cap, D), b16(PAIRS, 2 * cap, near_keys),
+            b16(PAIRS, 2 * cap, far_keys), f32(cap, D), b16(cap, D), f32(cap, near_keys), f32(cap, far_keys),
+            b16(cap, D), f32(cap, D),
             b16(PAIRS, BEFORE_ROWS, PAIR), b16(PAIRS, AFTER_ROWS, PAIR),
             b16(PAIRS, AFTER_ROWS, PAIR), b16(PAIRS, BEFORE_ROWS, PAIR),
             b16(PAIRS, tok, PAIR), b16(PAIRS, pooled + 16, PAIR), f32(tok + 16, 128), f32(tok + 16, 128),
@@ -1374,13 +1432,13 @@
             b16(2, NZ * PART, D), b16(NZ * PART, D), b16(NZ, PART, D), b16(NZ - 1, PART, D),
             b16(2, sums, FF // 2), b16(sums, FF // 2), b16(NZ, SH, FF // 2), b16(NZ - 1, SH, FF // 2),
             dma((COPIES,)), dma((COPIES,)), dma((2 * PAIRS,)), dma((2 * PAIRS,)), dma((PAIRS,)), dma((PAIRS,)),
-            dma((LOADS,)),
-        ] + dense_scratch(tok),
+            dma((4,)), dma((4,)), dma((LOADS,)),
+        ] + dense_scratch(tok)[:-1],
         compiler_params=pltpu.CompilerParams(
-            collective_id=2, has_side_effects=True, vmem_limit_bytes=VMEM_LIMIT
+            collective_id=2, has_side_effects=True, vmem_limit_bytes=LAYER_VMEM
         ),
-        name="tail",
-    )(*rows, *args)
+        name="layer",
+    )(x, cot_rows, wq, wk, wv, wo, w_in, w_out, slots, g1, s1, bq, bv, bo, g2, s2, b_in, b_out, pk, pv)
 
 
 def unpack_kernel(
@@ -1455,21 +1513,17 @@
 ):
     x = x_input[0]
     cot = cot_rows[0, 0]
+    if (n_dp, n_seq) == (2, SEQ):
+        done = layer(
+            n_seq, x, cot, w_query, w_key, w_value, w_attn_out, w_in, w_out, mask_slots, gain_one, shift_one,
+            b_query, b_value, b_attn_out, gain_two, shift_two, b_in, b_out, pool_key, pool_value,
+        )
+        output, grad_input, *reduced = unpack(*done)
+        return (output[None], grad_input[None]) + tuple(reduced)
     nrmt, q, kv, pkv = project(
         x, gain_one, shift_one, w_query, b_query, w_key, w_value, b_value, pool_key, pool_value
     )
     kvx, pkvx = halo(n_seq, kv, pkv, pool_key, pool_value)
-    if (n_dp, n_seq) == (2, SEQ):
-        rows = front(
-            n_seq, x, nrmt, q, kvx, pkvx, mask_slots, cot, w_attn_out, b_attn_out, gain_two, shift_two,
-            w_in, b_in, w_out,
-        )
-        done = tail(
-            n_seq, rows, x, nrmt, q, kvx, pkvx, w_query, w_key, w_value, w_attn_out, w_in, w_out,
-            mask_slots, b_attn_out, gain_one, gain_two, shift_two, b_in, b_out, pool_key, pool_value,
-        )
-        output, grad_input, *reduced = unpack(*done)
-        return (output[None], grad_input[None]) + tuple(reduced)
     nrm = nrmt.T
     (actt, gpre, n2t, cot, mixt, gbr, nrmt, gq, gnear, gfar, ghid, gqd, veca) = masked(
         n_seq, x, nrm, q, kvx, pkvx, mask_slots, cot, w_attn_out, b_attn_out, gain_two, shift_two,

time: 150 us -> 126 us (0.84)
  Pallas kernels: 147 us -> 124 us
    pallas_call x4 -> x1, Pallas kernels: 143 us -> 120 us  [layer(): pl.pallas_call(functools.partial(layer_kernel, count), out_shape=(struct(...]
where the time goes in v4:
time: 126 us; the launch traced here: 124 us
  Pallas kernels  124 us (98%)
    pallas_call x1, Pallas kernels, layer(): pl.pallas_call(functools.partial(layer_kernel, count), out_shape=(struct(...  120 us
    pallas_call x1, Pallas kernels, unpack(): pl.pallas_call(unpack_kernel, out_shape=(struct(output.shape, BF16), stru...  4.01 us

profile of v4, /device:TPU:8, one launch (start us, length us, event | category | flops | bytes accessed | tf_op | source)
XLA Modules:
  0.0 124.4 jit_solution(8122783113375132141)
XLA Ops:
  0.7 119.6 %layer.1 = (bf16[512,768]{1,0:T(8,128)(2,1)}, f32[512,768]{1,0:T(8,128)}, bf16[2,96,768]{2,1,0:T(8,128)(2,1)}, bf16[2,48,1536]{2,1,0:T(8,128)(2,1)}, bf16[2,2,48...) custom-call(bf16[512,768]{1,0:T(8,128)(2,1)} %bitcast.4, bf16[128,768]{1,0:T(8,128)(2,1)} %bitcast.5, ...), custom_call_target="tpu_custom_call" | custom-call | tf_op jit(solution)/shard_map/layer/pallas_call | solution.py:1399
  120.3 4.0 %unpack.1 = (bf16[512,768]{1,0:T(8,128)(2,1)}, f32[512,768]{1,0:T(8,128)}, f32[48]{0:T(128)}, f32[48]{0:T(128)}, f32[48,768]{1,0:T(8,128)}, /*index=5*/f32[48]{0...) custom-call(bf16[512,768]{1,0:T(8,128)(2,1)} %get-tuple-element.45.o, ...), custom_call_target="tpu_custom_call" | custom-call | tf_op jit(solution)/shard_map/unpack/pallas_call | solution.py:1474

commit v5 on v4

--- a/solution.py
+++ b/solution.py
@@ -764,8 +764,8 @@
     a_all, c_all, n_all, p_all, a_fwd, n_fwd, m_all, b_all, r_all, g_all,
     va_rx, vb_rx, vecb_ref, vs, vy_rx, vx_rx, vz_rx,
     gw, kv_rx, kv_s, kv_xr, kv_t, kv_yr, kv_z, kv_zr,
-    att, att_y, att_x, att_xr, att_z, att_zr,
-    wo_g, wo_y, wo_z, wo_zr, wi_g, wi_y, wi_z, wi_zr,
+    att, att_xr, att_s, att_yr, att_z, att_zr,
+    wo_g, wo_xr, wo_s, wo_yr, wi_g, wi_y, wi_z, wi_zr,
     send, recv, hsend, hrecv, ksend, krecv, fsend, frecv, loads, *dense_refs,
 ):
     cap = ghid.shape[0]
@@ -903,7 +903,6 @@
     wo_load = [load(wo_hbm, wo_ref)]
     ff_load = [load(win_hbm, win_ref), load(wout_hbm, wout_ref)]
     start_edges(near_edge)
-    out_x = [go(cot, c_all.at[slab(2)], x_dev)]
     out_core = [go(cot, c_all.at[slab(1)], core_dev)]
     own_out = [load(cot, c_all.at[slab(0)])]
     for base, taps_ref in ((0, pk_ref), (D // 128, pv_ref)):
@@ -971,9 +970,14 @@
     def _():
         fix(HALF + tok, REACH + pooled)
 
-    arrive(out_x)
-    out_fwd = [go(c_all.at[slab(2)], c_all.at[slab(3)], core_dev)]
     low, high = head_masks()
+    cot_z = []
+
+    def send_cot(t):
+        cot_z.append(go(cot, c_all.at[slab(2 * t)], z_dev[t - 1]))
+
+    send_cot(1)
+    send_cot(2)
 
     def attend_rows(p, carry):
         cc, cv = cols(p), cols(p + PAIRS)
@@ -1008,16 +1012,15 @@
     half_tiles = tiles // 2
 
     def feed_rows(i, carry):
-        t = (i % NZ) * 2 + i // NZ
+        zt = (z + 1 + i // 2) % NZ
+        yt = i % 2
+        t = zt * 2 + yt
         cc = cols(t, FF_TILE)
         pre = dot_nn(n2m[...], win_ref[:, cc]) + bin_row[:, cc]
         cdf = 0.5 * (1.0 + lax.erf(pre * SQRT_HALF))
         act_t = jnp.transpose(pre * cdf).astype(BF16)
-        at = rows_at(i * PART, PART, PART)
         for core in range(2):
-            for half in range(2):
-                start = (2 * core + half) * PART
-                actt[core, half, at, :] = act_t[start : start + PART]
+            actt[core, zt, rows_at(yt * SF, SF, SF), :] = act_t[core * SF : (core + 1) * SF]
         slope = cdf + pre * (INV_SQRT_2PI * jnp.exp(-0.5 * pre * pre))
         grad_act = dot_nt(cot[...], wout_ref[rows_at(t * FF_TILE, FF_TILE, FF_TILE), :])
         grad_pre = (grad_act * slope).astype(BF16)
@@ -1026,23 +1029,21 @@
         accm[...] += dot_nt(grad_pre, win_ref[:, cc])
         return carry
 
-    out_half = NZ * PART
-
-    def send_act(k):
-        r = pl.ds(k * out_half, out_half)
-        out_x.append(go(actt.at[e, f, r], a_fwd.at[r], x_dev))
-        out_x.append(go(actt.at[c, f, r], a_all.at[r, lane(2)], x_dev))
+    act_z = []
+
+    def send_act(t):
+        act_z.append(go(actt.at[e, z_at[t - 1]], a_fwd.at[t - 1], z_dev[t - 1]))
+        act_z.append(go(actt.at[c, z_at[t - 1]], a_all.at[:, lane(2 * t)], z_dev[t - 1]))
 
     lax.fori_loop(0, NZ, feed_rows, 0)
-    send_act(0)
+    send_cot(3)
     lax.fori_loop(NZ, tiles, feed_rows, 0)
     cot_f = cot[...].astype(F32)
     grad_n2 = accm[...]
     grad_hidden = cot_f + norm_back(n_two, inv_two, gain_two, grad_n2)
-    send_act(1)
     in_x.append(go(gpre.at[f], p_all.at[slab(2)], x_dev))
-    out_core.append(go(actt.at[e, d], a_all.at[:, lane(1)], core_dev))
-    own_out.append(load(actt.at[c, d], a_all.at[:, lane(0)]))
+    out_core.append(go(actt.at[e, z], a_all.at[:, lane(1)], core_dev))
+    own_out.append(load(actt.at[c, z], a_all.at[:, lane(0)]))
     in_core.append(go(gpre.at[d], p_all.at[slab(1)], core_dev))
     own_in.append(load(gpre.at[d], p_all.at[slab(0)]))
     ghid[...] = grad_hidden
@@ -1053,6 +1054,7 @@
     vecb_ref[18:19, :] = col_sum(grad_n2 * n_two)
     vecb_ref[19:20, :] = col_sum(grad_n2)
     vecb_ref[20:21, :] = col_sum(cot_f)
+    vec_a = [go(vecb_ref.at[pl.ds(16, 16)], va_rx, core_dev)]
     o_core.append(go(gbr, b_all.at[slab(1)], core_dev))
     own_o.append(load(gbr, b_all.at[slab(0)]))
 
@@ -1107,9 +1109,12 @@
 
     rows = NZ * SH
 
+    wide = D // 2
+
     def halves(values, g):
-        att[0, g] = values[:rows].astype(BF16)
-        att[1, g] = values[rows:].astype(BF16)
+        for h in range(2):
+            for k in range(2):
+                att[h, g, k] = values[k * rows : (k + 1) * rows, h * wide : (h + 1) * wide].astype(BF16)
 
     lax.fori_loop(0, 2, attend_back, 0)
     arrive(in_x[:1])
@@ -1118,9 +1123,8 @@
     arrive(o_core)
     halves(dot_nn(m_all[...], b_all[...]), 0)
     lax.fori_loop(2, 3, attend_back, 0)
-    att_to_y = [go(att.at[w, 0], att_y.at[0], y_dev)]
+    att_to_x = [go(att.at[f, 0], att_xr.at[0], x_dev)]
     lax.fori_loop(3, PAIRS, attend_back, 0)
-    vec_core = [go(vecb_ref.at[pl.ds(16, 16)], va_rx, core_dev)]
     g_all[slab(0), :] = gq_ref[...]
     vecb_ref[13:14, :] = col_sum(gq_ref[...].astype(F32))
     send_halo(pair_at(PAIRS - 1))
@@ -1186,11 +1190,13 @@
     def pool_range(a, b):
         lax.fori_loop(a, b, pool, 0)
 
-    quarter = out_half // 2
-
-    def out_product(i, carry):
-        r = rows_at(i * quarter, quarter, quarter)
-        wo_g[i // 2, rows_at((i % 2) * quarter, quarter, quarter), :] = dot_nn(a_all[r, :], c_all[...]).astype(BF16)
+    def out_product(j, carry):
+        cc = cols(j, width)
+        product = dot_nn(a_all[...], c_all[:, cc]).astype(BF16)
+        for k in range(2):
+            for h in range(2):
+                start = (2 * k + h) * PART
+                wo_g[h, k * PART : (k + 1) * PART, cc] = product[start : start + PART]
         return carry
 
     def in_product(i, carry):
@@ -1207,32 +1213,39 @@
         kv_s[p] = (gw[p, c].astype(F32) + kv_rx[p].astype(F32)).astype(BF16)
         return carry
 
+    vec_rows_a, vec_rows_b = pl.ds(0, 16), pl.ds(16, 16)
     pool_range(0, 1)
     wait(own_q)
     arrive(q_core)
     halves(dot_nn(r_all[...], g_all[...]), 1)
-    pool_range(1, 2)
-    att_to_y.append(go(att.at[w, 1], att_y.at[1], y_dev))
-    arrive(out_x[1:])
-    out_fwd.append(go(a_fwd, a_all.at[:, lane(3)], core_dev))
-    pool_range(2, 4)
-    wait(own_out)
-    arrive(out_core + out_fwd)
-    lax.fori_loop(0, 4, out_product, 0)
-    pool_range(4, 5)
-    out_to_y = [go(wo_g.at[w], wo_y, y_dev)]
+    arrive(cot_z)
+    out_fwd = [go(c_all.at[slab(2 * t)], c_all.at[slab(2 * t + 1)], core_dev) for t in range(1, NZ)]
+    arrive(vec_a)
+    vs[0, 0:16, :] = (vecb_ref[16:32, :] + va_rx[...]).astype(BF16)
     arrive(in_x[1:])
     in_fwd.append(go(p_all.at[slab(2)], p_all.at[slab(3)], core_dev))
-    pool_range(5, PAIRS)
-    lax.fori_loop(0, triple, kv_sum, 0)
-    kv_copy(pair_at(PAIRS - 1)).start()
-    lax.fori_loop(triple, PAIRS - 1, kv_sum, 0)
+    pool_range(1, 2)
+    att_to_x.append(go(att.at[f, 1], att_xr.at[1], x_dev))
+    vec_a_y = [go(vs.at[0, vec_rows_a], vy_rx.at[vec_rows_a], y_dev)]
+    for t in range(1, NZ):
+        send_act(t)
+    pool_range(2, 3)
     wait(own_in)
     arrive(in_core + in_fwd)
     lax.fori_loop(0, 8, in_product, 0)
-    lax.fori_loop(PAIRS - 1, PAIRS, kv_sum, 0)
+    arrive(vec_a_y)
+    vs[1, 0:16, :] = (vs[0, 0:16, :].astype(F32) + vy_rx[0:16, :].astype(F32)).astype(BF16)
+    pool_range(3, 4)
+    in_to_y = [go(wi_g.at[w], wi_y, y_dev)]
+    vec_a_x = [go(vs.at[1, vec_rows_a], vx_rx.at[vec_rows_a], x_dev)]
+    pool_range(4, 5)
+    lax.fori_loop(0, triple, kv_sum, 0)
+    pool_range(5, PAIRS)
     kv_to_x = [go(kv_s.at[pl.ds(f * triple, triple)], kv_xr, x_dev)]
-    in_to_y = [go(wi_g.at[w], wi_y, y_dev)]
+    lax.fori_loop(triple, PAIRS - 1, kv_sum, 0)
+    kv_copy(pair_at(PAIRS - 1)).start()
+    arrive(vec_a_x)
+    vs[2, 0:16, :] = (vs[1, 0:16, :].astype(F32) + vx_rx[0:16, :].astype(F32)).astype(BF16)
 
     high_part = ghid[...].astype(BF16)
     low_part = (ghid[...] - high_part.astype(F32)).astype(BF16)
@@ -1276,61 +1289,63 @@
     for i in range(3):
         vecb_ref[i : i + 1, :] = sums[i]
 
-    arrive(att_to_y)
-    wide = D // 2
+    vec_b = [go(vecb_ref.at[pl.ds(0, 16)], vb_rx, core_dev)]
+    arrive(att_to_x)
     for g in range(2):
-        total = att[y, g].astype(F32) + att_y[g].astype(F32)
-        att_x[0, g] = total[:, :wide].astype(BF16)
-        att_x[1, g] = total[:, wide:].astype(BF16)
-    vec_core.append(go(vecb_ref.at[pl.ds(0, 16)], vb_rx, core_dev))
+        for k in range(2):
+            att_s[k, g] = (att[d, g, k].astype(F32) + att_xr[g, k].astype(F32)).astype(BF16)
+    arrive(act_z)
+    out_fwd += [go(a_fwd.at[t - 1], a_all.at[:, lane(2 * t + 1)], core_dev) for t in range(1, NZ)]
     attend(0)
-    att_to_x = [go(att_x.at[f], att_xr, x_dev)]
-    arrive(vec_core)
-    vs[0, 0:16, :] = (vecb_ref[16:32, :] + va_rx[...]).astype(BF16)
+    att_to_y = [go(att_s.at[w], att_yr, y_dev)]
+    vec_a_z = [go(vs.at[2, vec_rows_a], vz_rx.at[t, vec_rows_a], z_dev[t]) for t in range(NZ - 1)]
+    wait(own_out)
+    arrive(out_core + out_fwd)
+    lax.fori_loop(0, D // width, out_product, 0)
+    arrive(vec_b)
     vs[0, 16:32, :] = (vecb_ref[0:16, :] + vb_rx[...]).astype(BF16)
-    arrive(out_to_y)
+    arrive(in_to_y)
     for zz in range(NZ):
-        r = pl.ds(zz * PART, PART)
-        wo_z[zz] = (wo_g[y, r].astype(F32) + wo_y[r].astype(F32)).astype(BF16)
-    attend(1)
-    vec_to_y = [go(vs.at[0], vy_rx, y_dev)]
-    out_to_z = [go(wo_z.at[z_at[t]], wo_zr.at[t], z_dev[t]) for t in range(NZ - 1)]
+        r = pl.ds(zz * SH, SH)
+        wi_z[zz] = (wi_g[y, r].astype(F32) + wi_y[r].astype(F32)).astype(BF16)
+    lax.fori_loop(PAIRS - 1, PAIRS, kv_sum, 0)
     arrive(kv_to_x)
     for q in range(triple):
         total = kv_s[d * triple + q].astype(F32) + kv_xr[q].astype(F32)
         kv_t[0, q] = total[:rows].astype(BF16)
         kv_t[1, q] = total[rows:].astype(BF16)
-    attend(2)
+    attend(1)
     kv_to_y = [go(kv_t.at[w], kv_yr, y_dev)]
-    arrive(in_to_y)
-    for zz in range(NZ):
-        r = pl.ds(zz * SH, SH)
-        wi_z[zz] = (wi_g[y, r].astype(F32) + wi_y[r].astype(F32)).astype(BF16)
-    attend(3)
     in_to_z = [go(wi_z.at[z_at[t]], wi_zr.at[t], z_dev[t]) for t in range(NZ - 1)]
-    arrive(att_to_x)
+    out_to_x = [go(wo_g.at[f], wo_xr, x_dev)]
+    vec_b_y = [go(vs.at[0, vec_rows_b], vy_rx.at[vec_rows_b], y_dev)]
+    arrive(att_to_y)
     for zz in range(NZ):
         r = pl.ds(zz * SH, SH)
         for g in range(2):
-            att_z[zz, g] = (att_x[d, g, r].astype(F32) + att_xr[g, r].astype(F32)).astype(BF16)
-    residual()
+            att_z[zz, g] = (att_s[y, g, r].astype(F32) + att_yr[g, r].astype(F32)).astype(BF16)
+    attend(2)
     att_to_z = [go(att_z.at[z_at[t]], att_zr.at[t], z_dev[t]) for t in range(NZ - 1)]
-    arrive(vec_to_y)
-    vs[1] = (vs[0].astype(F32) + vy_rx[...].astype(F32)).astype(BF16)
-    feed(0, 1)
-    vec_to_x = [go(vs.at[1], vx_rx, x_dev)]
-    feed(1, 2)
+    arrive(vec_b_y)
+    vs[1, 16:32, :] = (vs[0, 16:32, :].astype(F32) + vy_rx[16:32, :].astype(F32)).astype(BF16)
+    attend(3)
+    vec_b_x = [go(vs.at[1, vec_rows_b], vx_rx.at[vec_rows_b], x_dev)]
     arrive(kv_to_y)
     for zz in range(NZ):
         r = pl.ds(zz * SH, SH)
         for q in range(triple):
             kv_z[zz, q] = (kv_t[y, q, r].astype(F32) + kv_yr[q, r].astype(F32)).astype(BF16)
-    feed(2, 3)
+    arrive(out_to_x)
+    for k in range(2):
+        r = pl.ds(k * PART, PART)
+        wo_s[k] = (wo_g[d, r].astype(F32) + wo_xr[r].astype(F32)).astype(BF16)
+    residual()
     kv_to_z = [go(kv_z.at[z_at[t]], kv_zr.at[t], z_dev[t]) for t in range(NZ - 1)]
-    arrive(vec_to_x)
-    vs[2] = (vs[1].astype(F32) + vx_rx[...].astype(F32)).astype(BF16)
-    feed(3, 4)
-    vec_to_z = [go(vs.at[2], vz_rx.at[t], z_dev[t]) for t in range(NZ - 1)]
+    out_to_y = [go(wo_s.at[w], wo_yr, y_dev)]
+    arrive(vec_b_x)
+    vs[2, 16:32, :] = (vs[1, 16:32, :].astype(F32) + vx_rx[16:32, :].astype(F32)).astype(BF16)
+    feed(0, 1)
+    vec_b_z = [go(vs.at[2, vec_rows_b], vz_rx.at[t, vec_rows_b], z_dev[t]) for t in range(NZ - 1)]
 
     def gathered(own, parts):
         total = own.astype(F32)
@@ -1343,24 +1358,26 @@
     def share(ref):
         last.append(go(ref.at[d], ref.at[d], x_dev))
 
-    arrive(out_to_z)
-    f_out[d] = gathered(wo_z[z], wo_zr).astype(BF16)
-    feed(4, 5)
+    feed(1, 3)
+    arrive(out_to_y)
+    f_out[d] = (wo_s[y].astype(F32) + wo_yr[...].astype(F32)).astype(BF16)
+    feed(3, 4)
     share(f_out)
     arrive(in_to_z)
     f_in[d] = gathered(wi_z[z], wi_zr).astype(BF16)
-    feed(5, 6)
+    feed(4, 5)
     share(f_in)
     arrive(att_to_z)
     f_oq[d] = gathered(att_z[z], att_zr).astype(BF16)
-    feed(6, 7)
+    feed(5, 6)
     share(f_oq)
     arrive(kv_to_z)
     f_kv[d] = gathered(kv_z[z], kv_zr).astype(BF16)
+    feed(6, 7)
+    share(f_kv)
     feed(7, 8)
-    share(f_kv)
     end()
-    arrive(vec_to_z)
+    arrive(vec_a_z + vec_b_z)
     f_vec[...] = gathered(vs[2], vz_rx)
     arrive(last)
     for copy in started:
@@ -1412,7 +1429,7 @@
         scratch_shapes=[
             b16(tok, D), b16(tok, D), b16(D, tok), b16(tok, D), b16(near_keys, 2 * D), b16(far_keys, 2 * D),
             b16(D, D), b16(D, D), b16(D, D), b16(D, D), b16(cap, D),
-            b16(2, 2, FF // 4, cap), b16(2, cap, FF // 2), b16(2, half, cap), b16(cap, D), b16(2, half, cap),
+            b16(2, NZ, 2 * SF, cap), b16(2, cap, FF // 2), b16(2, half, cap), b16(cap, D), b16(2, half, cap),
             b16(cap, D), b16(2, half, cap), b16(cap, D), b16(cap, D), b16(PAIRS, 2 * cap, near_keys),
             b16(PAIRS, 2 * cap, far_keys), f32(cap, D), b16(cap, D), f32(cap, near_keys), f32(cap, far_keys),
             b16(cap, D), f32(cap, D),
@@ -1420,16 +1437,16 @@
             b16(PAIRS, AFTER_ROWS, PAIR), b16(PAIRS, BEFORE_ROWS, PAIR),
             b16(PAIRS, tok, PAIR), b16(PAIRS, pooled + 16, PAIR), f32(tok + 16, 128), f32(tok + 16, 128),
             b16(tok, 2 * D), b16(cap, D),
-            b16(FF // 4, 4 * cap), b16(4 * cap, D), b16(half, 4 * cap), b16(4 * cap, FF // 2),
-            b16(FF // 4, cap), b16(half, cap),
+            b16(2 * SF, 2 * NZ * cap), b16(2 * NZ * cap, D), b16(half, 4 * cap), b16(4 * cap, FF // 2),
+            b16(NZ - 1, 2 * SF, cap), b16(half, cap),
             b16(half, 2 * cap), b16(2 * cap, D), b16(half, 2 * cap), b16(2 * cap, D),
             f32(16, D), f32(16, D), f32(32, D), b16(3, 32, D), b16(32, D), b16(32, D), b16(NZ - 1, 32, D),
             b16(PAIRS, 2, half, PAIR), b16(PAIRS, half, PAIR), b16(PAIRS, half, PAIR), b16(triple, half, PAIR),
             b16(2, triple, sums, PAIR), b16(triple, sums, PAIR), b16(NZ, triple, SH, PAIR),
             b16(NZ - 1, triple, SH, PAIR),
-            b16(2, 2, sums, D), b16(2, sums, D), b16(2, 2, sums, half), b16(2, sums, half),
+            b16(2, 2, 2, sums, half), b16(2, 2, sums, half), b16(2, 2, sums, half), b16(2, sums, half),
             b16(NZ, 2, SH, half), b16(NZ - 1, 2, SH, half),
-            b16(2, NZ * PART, D), b16(NZ * PART, D), b16(NZ, PART, D), b16(NZ - 1, PART, D),
+            b16(2, 2 * PART, D), b16(2 * PART, D), b16(2, PART, D), b16(PART, D),
             b16(2, sums, FF // 2), b16(sums, FF // 2), b16(NZ, SH, FF // 2), b16(NZ - 1, SH, FF // 2),
             dma((COPIES,)), dma((COPIES,)), dma((2 * PAIRS,)), dma((2 * PAIRS,)), dma((PAIRS,)), dma((PAIRS,)),
             dma((4,)), dma((4,)), dma((LOADS,)),

time: 126 us -> 107 us (0.85)
  Pallas kernels: 124 us -> 105 us
    pallas_call x1, Pallas kernels: 120 us -> 101 us  [layer(): pl.pallas_call(functools.partial(layer_kernel, count), out_shape=(struct(...]
where the time goes in v5:
time: 107 us; the launch traced here: 106 us
  Pallas kernels  105 us (98%)
    pallas_call x1, Pallas kernels, layer(): pl.pallas_call(functools.partial(layer_kernel, count), out_shape=(struct(...  101 us
    pallas_call x1, Pallas kernels, unpack(): pl.pallas_call(unpack_kernel, out_shape=(struct(output.shape, BF16), stru...  4.01 us

profile of v5, /device:TPU:8, one launch (start us, length us, event | category | flops | bytes accessed | tf_op | source)
XLA Modules:
  0.0 106.0 jit_solution(6565881971137321702)
XLA Ops:
  0.7 101.1 %layer.1 = (bf16[512,768]{1,0:T(8,128)(2,1)}, f32[512,768]{1,0:T(8,128)}, bf16[2,96,768]{2,1,0:T(8,128)(2,1)}, bf16[2,48,1536]{2,1,0:T(8,128)(2,1)}, bf16[2,2,48...) custom-call(bf16[512,768]{1,0:T(8,128)(2,1)} %bitcast.4, bf16[128,768]{1,0:T(8,128)(2,1)} %bitcast.5, ...), custom_call_target="tpu_custom_call" | custom-call | tf_op jit(solution)/shard_map/layer/pallas_call | solution.py:1416
  101.8 4.0 %unpack.1 = (bf16[512,768]{1,0:T(8,128)(2,1)}, f32[512,768]{1,0:T(8,128)}, f32[48]{0:T(128)}, f32[48]{0:T(128)}, f32[48,768]{1,0:T(8,128)}, /*index=5*/f32[48]{0...) custom-call(bf16[512,768]{1,0:T(8,128)(2,1)} %get-tuple-element.45.o, ...), custom_call_target="tpu_custom_call" | custom-call | tf_op jit(solution)/shard_map/unpack/pallas_call | solution.py:1491

commit v6 on v5

--- a/solution.py
+++ b/solution.py
@@ -351,6 +351,7 @@
 
 
 FF_TILE = 384
+DENSE_TILE = 256
 
 
 def masked_kernel(
@@ -656,7 +657,7 @@
             mix_ref[rows, c] = merge_pair(out).astype(BF16)
             return carry
 
-        lax.fori_loop(0, PAIRS, pair, 0)
+        lax.fori_loop(0, PAIRS, pair, 0, unroll=2)
 
     def residual():
         def one(b, carry):
@@ -672,19 +673,18 @@
             copy.wait()
 
     def feed(first, last):
-        high_rows = 256
-        halves = tok // high_rows
-
-        def one(i, carry):
-            t, b = i // halves, i % halves
-            c = cols(t, FF_TILE)
-            rows = rows_at(b * high_rows, high_rows, high_rows)
-            pre = dot_nn(n2_ref[rows, :], win_ref[:, c]) + bin_row[:, c]
-            act = (pre * (0.5 * (1.0 + lax.erf(pre * SQRT_HALF)))).astype(BF16)
-            acc_ref[rows, :] += dot_nn(act, wout_ref[rows_at(t * FF_TILE, FF_TILE, FF_TILE), :])
+        halves = [pl.ds(b, 256) for b in range(0, tok, 256)]
+
+        def one(t, carry):
+            c = cols(t, DENSE_TILE)
+            out_rows = rows_at(t * DENSE_TILE, DENSE_TILE, DENSE_TILE)
+            pres = [dot_nn(n2_ref[rows, :], win_ref[:, c]) + bin_row[:, c] for rows in halves]
+            for rows, pre in zip(halves, pres):
+                act = (pre * (0.5 * (1.0 + lax.erf(pre * SQRT_HALF)))).astype(BF16)
+                acc_ref[rows, :] += dot_nn(act, wout_ref[out_rows, :])
             return carry
 
-        lax.fori_loop(first * halves, last * halves, one, 0)
+        lax.fori_loop(first, last, one, 0)
 
     def end():
         out_ref[...] = acc_ref[...].astype(BF16)
@@ -698,7 +698,7 @@
     for b in range(blocks):
         attend(b)
     residual()
-    feed(0, FF // FF_TILE)
+    feed(0, FF // DENSE_TILE)
     end()
 
 
@@ -748,7 +748,7 @@
             ref[core, at : at + SH, :] = values[start : start + SH]
 
 
-COPIES = 80
+COPIES = 96
 LOADS = 16
 LAYER_VMEM = 65472 * 1024
 
@@ -843,14 +843,6 @@
     grads[0:8, :] = zero_rows
     vecb_ref[...] = jnp.zeros_like(vecb_ref)
 
-    @pl.when(has_far)
-    def _():
-        pl.semaphore_wait(barrier, len(peers) + 1)
-
-    @pl.when(jnp.logical_not(has_far))
-    def _():
-        pl.semaphore_wait(barrier, len(peers))
-
     wait(x_load)
     n_one, _ = norm_stats(x_ref[...].astype(F32))
     nrm_ref[...] = (n_one * row_of(g1_ref) + row_of(s1_ref)).astype(BF16)
@@ -902,6 +894,15 @@
 
     wo_load = [load(wo_hbm, wo_ref)]
     ff_load = [load(win_hbm, win_ref), load(wout_hbm, wout_ref)]
+
+    @pl.when(has_far)
+    def _():
+        pl.semaphore_wait(barrier, len(peers) + 1)
+
+    @pl.when(jnp.logical_not(has_far))
+    def _():
+        pl.semaphore_wait(barrier, len(peers))
+
     start_edges(near_edge)
     out_core = [go(cot, c_all.at[slab(1)], core_dev)]
     own_out = [load(cot, c_all.at[slab(0)])]
@@ -953,6 +954,13 @@
     q_core = [go(nrmt.at[e], r_all.at[:, lane(1)], core_dev)]
     own_q = [load(nrmt.at[c], r_all.at[:, lane(0)])]
     begin()
+    wait(ff_load)
+
+    def grad_act_rows(t, carry):
+        acc_ref[rows_at(t * cap, cap, cap), :] = dot_nt(cot[...], wout_ref[rows_at(t * D, D, D), :])
+        return carry
+
+    lax.fori_loop(0, NZ, grad_act_rows, 0)
     wait_edges(near_edge)
     wait_edges(far_edge)
     tap_rows = jnp.concatenate([pk_ref[...].astype(F32), pv_ref[...].astype(F32)], axis=1)
@@ -1004,28 +1012,24 @@
     o_core = [go(mixt.at[e], m_all.at[:, lane(1)], core_dev)]
     own_o = [load(mixt.at[c], m_all.at[:, lane(0)])]
     accm[...] = jnp.zeros_like(accm)
-    wait(ff_load)
     in_x = [go(n2t.at[e], n_fwd, x_dev), go(n2t.at[c], n_all.at[:, lane(2)], x_dev)]
     in_core = [go(n2t.at[e], n_all.at[:, lane(1)], core_dev)]
     own_in = [load(n2t.at[c], n_all.at[:, lane(0)])]
-    tiles = FF // FF_TILE
-    half_tiles = tiles // 2
 
     def feed_rows(i, carry):
-        zt = (z + 1 + i // 2) % NZ
-        yt = i % 2
-        t = zt * 2 + yt
-        cc = cols(t, FF_TILE)
+        zt = (2 * f + i) % NZ
+        cc = cols(zt, D)
         pre = dot_nn(n2m[...], win_ref[:, cc]) + bin_row[:, cc]
         cdf = 0.5 * (1.0 + lax.erf(pre * SQRT_HALF))
         act_t = jnp.transpose(pre * cdf).astype(BF16)
-        for core in range(2):
-            actt[core, zt, rows_at(yt * SF, SF, SF), :] = act_t[core * SF : (core + 1) * SF]
+        for yt in range(2):
+            for core in range(2):
+                start = (2 * yt + core) * SF
+                actt[core, zt, yt * SF : (yt + 1) * SF, :] = act_t[start : start + SF]
         slope = cdf + pre * (INV_SQRT_2PI * jnp.exp(-0.5 * pre * pre))
-        grad_act = dot_nt(cot[...], wout_ref[rows_at(t * FF_TILE, FF_TILE, FF_TILE), :])
-        grad_pre = (grad_act * slope).astype(BF16)
-        gpre[t // half_tiles, :, cols(t % half_tiles, FF_TILE)] = grad_pre
-        vecb_ref[pl.ds(24 + t // 2, 1), cols(t % 2, FF_TILE)] = col_sum(grad_pre.astype(F32))
+        grad_pre = (acc_ref[rows_at(zt * cap, cap, cap), :] * slope).astype(BF16)
+        gpre[zt // 2, :, cols(zt % 2, D)] = grad_pre
+        vecb_ref[pl.ds(24 + zt, 1), :] = col_sum(grad_pre.astype(F32))
         accm[...] += dot_nt(grad_pre, win_ref[:, cc])
         return carry
 
@@ -1035,13 +1039,19 @@
         act_z.append(go(actt.at[e, z_at[t - 1]], a_fwd.at[t - 1], z_dev[t - 1]))
         act_z.append(go(actt.at[c, z_at[t - 1]], a_all.at[:, lane(2 * t)], z_dev[t - 1]))
 
-    lax.fori_loop(0, NZ, feed_rows, 0)
+    def send_gpre(q):
+        cc = pl.ds(q * D, D)
+        in_x.append(go(gpre.at[f, :, cc], p_all.at[slab(2), cc], x_dev))
+
+    lax.fori_loop(0, 2, feed_rows, 0)
+    send_gpre(0)
     send_cot(3)
-    lax.fori_loop(NZ, tiles, feed_rows, 0)
+    lax.fori_loop(2, 3, feed_rows, 0)
+    send_gpre(1)
+    lax.fori_loop(3, NZ, feed_rows, 0)
     cot_f = cot[...].astype(F32)
     grad_n2 = accm[...]
     grad_hidden = cot_f + norm_back(n_two, inv_two, gain_two, grad_n2)
-    in_x.append(go(gpre.at[f], p_all.at[slab(2)], x_dev))
     out_core.append(go(actt.at[e, z], a_all.at[:, lane(1)], core_dev))
     own_out.append(load(actt.at[c, z], a_all.at[:, lane(0)]))
     in_core.append(go(gpre.at[d], p_all.at[slab(1)], core_dev))
@@ -1116,15 +1126,23 @@
             for k in range(2):
                 att[h, g, k] = values[k * rows : (k + 1) * rows, h * wide : (h + 1) * wide].astype(BF16)
 
+    def forward_gpre(q):
+        cc = pl.ds(q * D, D)
+        arrive(in_x[2 + q : 3 + q])
+        in_fwd.append(go(p_all.at[slab(2), cc], p_all.at[slab(3), cc], core_dev))
+
     lax.fori_loop(0, 2, attend_back, 0)
     arrive(in_x[:1])
     in_fwd = [go(n_fwd, n_all.at[:, lane(3)], core_dev)]
+    lax.fori_loop(2, 4, attend_back, 0)
     wait(own_o)
     arrive(o_core)
     halves(dot_nn(m_all[...], b_all[...]), 0)
-    lax.fori_loop(2, 3, attend_back, 0)
+    forward_gpre(0)
+    lax.fori_loop(4, PAIRS, attend_back, 0)
+    arrive(in_x[1:2])
+    forward_gpre(1)
     att_to_x = [go(att.at[f, 0], att_xr.at[0], x_dev)]
-    lax.fori_loop(3, PAIRS, attend_back, 0)
     g_all[slab(0), :] = gq_ref[...]
     vecb_ref[13:14, :] = col_sum(gq_ref[...].astype(F32))
     send_halo(pair_at(PAIRS - 1))
@@ -1199,12 +1217,34 @@
                 wo_g[h, k * PART : (k + 1) * PART, cc] = product[start : start + PART]
         return carry
 
-    def in_product(i, carry):
-        r = rows_at((i // 4) * rows, rows, rows)
-        cc = cols(i % 4, FF // 8)
-        wi_g[i // 4, :, cc] = dot_nn(n_all[r, :], p_all[:, cc]).astype(BF16)
-        return carry
-
+    def in_product(k, h):
+        r = rows_at(k * rows, rows, rows)
+
+        def one(i, carry):
+            cc = cols(3 * h + i, width)
+            wi_g[k, :, cc] = dot_nn(n_all[r, :], p_all[:, cc]).astype(BF16)
+            return carry
+
+        lax.fori_loop(0, 3, one, 0)
+
+    def send_in(h):
+        cc = pl.ds(h * D, D)
+        in_to_y.append(go(wi_g.at[w, :, cc], wi_y.at[:, cc], y_dev))
+
+    def sum_in(h):
+        cc = pl.ds(h * D, D)
+        arrive(in_to_y[h : h + 1])
+        for zz in range(NZ):
+            r = pl.ds(zz * SH, SH)
+            wi_z[zz, :, cc] = (wi_g[y, r, cc].astype(F32) + wi_y[r, cc].astype(F32)).astype(BF16)
+
+    def in_over_z(h):
+        cc = pl.ds(h * D, D)
+        in_to_z.append(
+            [go(wi_z.at[z_at[t], :, cc], wi_zr.at[t, :, cc], z_dev[t]) for t in range(NZ - 1)]
+        )
+
+    in_to_y, in_to_z = [], []
     triple = PAIRS // 2
 
     def kv_sum(i, carry):
@@ -1214,38 +1254,39 @@
         return carry
 
     vec_rows_a, vec_rows_b = pl.ds(0, 16), pl.ds(16, 16)
+    arrive(vec_a)
+    vs[0, 0:16, :] = (vecb_ref[16:32, :] + va_rx[...]).astype(BF16)
     pool_range(0, 1)
+    vec_a_y = [go(vs.at[0, vec_rows_a], vy_rx.at[vec_rows_a], y_dev)]
+    wait(own_in)
+    arrive(in_core + in_fwd)
+    in_product(w, 0)
+    in_product(w, 1)
+    pool_range(1, 2)
+    send_in(0)
+    send_in(1)
     wait(own_q)
     arrive(q_core)
     halves(dot_nn(r_all[...], g_all[...]), 1)
     arrive(cot_z)
     out_fwd = [go(c_all.at[slab(2 * t)], c_all.at[slab(2 * t + 1)], core_dev) for t in range(1, NZ)]
-    arrive(vec_a)
-    vs[0, 0:16, :] = (vecb_ref[16:32, :] + va_rx[...]).astype(BF16)
-    arrive(in_x[1:])
-    in_fwd.append(go(p_all.at[slab(2)], p_all.at[slab(3)], core_dev))
-    pool_range(1, 2)
-    att_to_x.append(go(att.at[f, 1], att_xr.at[1], x_dev))
-    vec_a_y = [go(vs.at[0, vec_rows_a], vy_rx.at[vec_rows_a], y_dev)]
     for t in range(1, NZ):
         send_act(t)
     pool_range(2, 3)
-    wait(own_in)
-    arrive(in_core + in_fwd)
-    lax.fori_loop(0, 8, in_product, 0)
+    att_to_x.append(go(att.at[f, 1], att_xr.at[1], x_dev))
+    pool_range(3, 5)
+    lax.fori_loop(0, triple, kv_sum, 0)
     arrive(vec_a_y)
     vs[1, 0:16, :] = (vs[0, 0:16, :].astype(F32) + vy_rx[0:16, :].astype(F32)).astype(BF16)
-    pool_range(3, 4)
-    in_to_y = [go(wi_g.at[w], wi_y, y_dev)]
+    pool_range(5, PAIRS)
     vec_a_x = [go(vs.at[1, vec_rows_a], vx_rx.at[vec_rows_a], x_dev)]
-    pool_range(4, 5)
-    lax.fori_loop(0, triple, kv_sum, 0)
-    pool_range(5, PAIRS)
     kv_to_x = [go(kv_s.at[pl.ds(f * triple, triple)], kv_xr, x_dev)]
+    in_product(y, 0)
+    in_product(y, 1)
     lax.fori_loop(triple, PAIRS - 1, kv_sum, 0)
     kv_copy(pair_at(PAIRS - 1)).start()
-    arrive(vec_a_x)
-    vs[2, 0:16, :] = (vs[1, 0:16, :].astype(F32) + vx_rx[0:16, :].astype(F32)).astype(BF16)
+    attend(0)
+    sum_in(0)
 
     high_part = ghid[...].astype(BF16)
     low_part = (ghid[...] - high_part.astype(F32)).astype(BF16)
@@ -1268,6 +1309,11 @@
         return carry
 
     lax.fori_loop(0, D // width, back, 0)
+    in_over_z(0)
+    arrive(att_to_x)
+    for g in range(2):
+        for k in range(2):
+            att_s[k, g] = (att[d, g, k].astype(F32) + att_xr[g, k].astype(F32)).astype(BF16)
     block = 128
     gain = row_of(g1_ref)
 
@@ -1289,64 +1335,52 @@
     for i in range(3):
         vecb_ref[i : i + 1, :] = sums[i]
 
+    att_to_y = [go(att_s.at[w], att_yr, y_dev)]
     vec_b = [go(vecb_ref.at[pl.ds(0, 16)], vb_rx, core_dev)]
-    arrive(att_to_x)
-    for g in range(2):
-        for k in range(2):
-            att_s[k, g] = (att[d, g, k].astype(F32) + att_xr[g, k].astype(F32)).astype(BF16)
-    arrive(act_z)
-    out_fwd += [go(a_fwd.at[t - 1], a_all.at[:, lane(2 * t + 1)], core_dev) for t in range(1, NZ)]
-    attend(0)
-    att_to_y = [go(att_s.at[w], att_yr, y_dev)]
+    lax.fori_loop(PAIRS - 1, PAIRS, kv_sum, 0)
+    sum_in(1)
+    arrive(vec_a_x)
+    vs[2, 0:16, :] = (vs[1, 0:16, :].astype(F32) + vx_rx[0:16, :].astype(F32)).astype(BF16)
+    attend(1)
+    in_over_z(1)
     vec_a_z = [go(vs.at[2, vec_rows_a], vz_rx.at[t, vec_rows_a], z_dev[t]) for t in range(NZ - 1)]
-    wait(own_out)
-    arrive(out_core + out_fwd)
-    lax.fori_loop(0, D // width, out_product, 0)
-    arrive(vec_b)
-    vs[0, 16:32, :] = (vecb_ref[0:16, :] + vb_rx[...]).astype(BF16)
-    arrive(in_to_y)
-    for zz in range(NZ):
-        r = pl.ds(zz * SH, SH)
-        wi_z[zz] = (wi_g[y, r].astype(F32) + wi_y[r].astype(F32)).astype(BF16)
-    lax.fori_loop(PAIRS - 1, PAIRS, kv_sum, 0)
     arrive(kv_to_x)
     for q in range(triple):
         total = kv_s[d * triple + q].astype(F32) + kv_xr[q].astype(F32)
         kv_t[0, q] = total[:rows].astype(BF16)
         kv_t[1, q] = total[rows:].astype(BF16)
-    attend(1)
-    kv_to_y = [go(kv_t.at[w], kv_yr, y_dev)]
-    in_to_z = [go(wi_z.at[z_at[t]], wi_zr.at[t], z_dev[t]) for t in range(NZ - 1)]
-    out_to_x = [go(wo_g.at[f], wo_xr, x_dev)]
-    vec_b_y = [go(vs.at[0, vec_rows_b], vy_rx.at[vec_rows_b], y_dev)]
+    arrive(act_z)
+    out_fwd += [go(a_fwd.at[t - 1], a_all.at[:, lane(2 * t + 1)], core_dev) for t in range(1, NZ)]
+    arrive(vec_b)
+    vs[0, 16:32, :] = (vecb_ref[0:16, :] + vb_rx[...]).astype(BF16)
     arrive(att_to_y)
     for zz in range(NZ):
         r = pl.ds(zz * SH, SH)
         for g in range(2):
             att_z[zz, g] = (att_s[y, g, r].astype(F32) + att_yr[g, r].astype(F32)).astype(BF16)
+    kv_to_y = [go(kv_t.at[w], kv_yr, y_dev)]
+    vec_b_y = [go(vs.at[0, vec_rows_b], vy_rx.at[vec_rows_b], y_dev)]
+    wait(own_out)
+    arrive(out_core + out_fwd)
+    lax.fori_loop(0, D // width, out_product, 0)
     attend(2)
+    out_to_x = [go(wo_g.at[f], wo_xr, x_dev)]
     att_to_z = [go(att_z.at[z_at[t]], att_zr.at[t], z_dev[t]) for t in range(NZ - 1)]
-    arrive(vec_b_y)
-    vs[1, 16:32, :] = (vs[0, 16:32, :].astype(F32) + vy_rx[16:32, :].astype(F32)).astype(BF16)
     attend(3)
-    vec_b_x = [go(vs.at[1, vec_rows_b], vx_rx.at[vec_rows_b], x_dev)]
     arrive(kv_to_y)
     for zz in range(NZ):
         r = pl.ds(zz * SH, SH)
         for q in range(triple):
             kv_z[zz, q] = (kv_t[y, q, r].astype(F32) + kv_yr[q, r].astype(F32)).astype(BF16)
+    arrive(vec_b_y)
+    vs[1, 16:32, :] = (vs[0, 16:32, :].astype(F32) + vy_rx[16:32, :].astype(F32)).astype(BF16)
+    residual()
+    kv_to_z = [go(kv_z.at[z_at[t]], kv_zr.at[t], z_dev[t]) for t in range(NZ - 1)]
+    vec_b_x = [go(vs.at[1, vec_rows_b], vx_rx.at[vec_rows_b], x_dev)]
     arrive(out_to_x)
     for k in range(2):
         r = pl.ds(k * PART, PART)
         wo_s[k] = (wo_g[d, r].astype(F32) + wo_xr[r].astype(F32)).astype(BF16)
-    residual()
-    kv_to_z = [go(kv_z.at[z_at[t]], kv_zr.at[t], z_dev[t]) for t in range(NZ - 1)]
-    out_to_y = [go(wo_s.at[w], wo_yr, y_dev)]
-    arrive(vec_b_x)
-    vs[2, 16:32, :] = (vs[1, 16:32, :].astype(F32) + vx_rx[16:32, :].astype(F32)).astype(BF16)
-    feed(0, 1)
-    vec_b_z = [go(vs.at[2, vec_rows_b], vz_rx.at[t, vec_rows_b], z_dev[t]) for t in range(NZ - 1)]
-
     def gathered(own, parts):
         total = own.astype(F32)
         for t in range(NZ - 1):
@@ -1358,24 +1392,30 @@
     def share(ref):
         last.append(go(ref.at[d], ref.at[d], x_dev))
 
-    feed(1, 3)
-    arrive(out_to_y)
-    f_out[d] = (wo_s[y].astype(F32) + wo_yr[...].astype(F32)).astype(BF16)
-    feed(3, 4)
-    share(f_out)
-    arrive(in_to_z)
+    feed(0, 2)
+    out_to_y = [go(wo_s.at[w], wo_yr, y_dev)]
+    for h in range(2):
+        arrive(in_to_z[h])
     f_in[d] = gathered(wi_z[z], wi_zr).astype(BF16)
-    feed(4, 5)
+    feed(2, 3)
     share(f_in)
+    arrive(vec_b_x)
+    vs[2, 16:32, :] = (vs[1, 16:32, :].astype(F32) + vx_rx[16:32, :].astype(F32)).astype(BF16)
+    feed(3, 5)
+    vec_b_z = [go(vs.at[2, vec_rows_b], vz_rx.at[t, vec_rows_b], z_dev[t]) for t in range(NZ - 1)]
     arrive(att_to_z)
     f_oq[d] = gathered(att_z[z], att_zr).astype(BF16)
     feed(5, 6)
     share(f_oq)
+    arrive(out_to_y)
+    f_out[d] = (wo_s[y].astype(F32) + wo_yr[...].astype(F32)).astype(BF16)
+    feed(6, 8)
+    share(f_out)
     arrive(kv_to_z)
     f_kv[d] = gathered(kv_z[z], kv_zr).astype(BF16)
-    feed(6, 7)
+    feed(8, 9)
     share(f_kv)
-    feed(7, 8)
+    feed(9, 12)
     end()
     arrive(vec_a_z + vec_b_z)
     f_vec[...] = gathered(vs[2], vz_rx)
@@ -1461,10 +1501,20 @@
 def unpack_kernel(
     out_hbm, gin_hbm, f_out, f_in, f_oq, f_kv, f_vec,
     out_ref, gin_ref, g1, s1, wq, bq, wk, wv, bv, wo, bo, pk, pv, g2, s2, wi, bi, wu, bu,
+    out_rows, gin_rows, sems,
 ):
     s = lax.axis_index("seq")
-    out_ref[...] = out_hbm[...]
-    gin_ref[...] = gin_hbm[...]
+    loads = [
+        pltpu.make_async_copy(gin_hbm, gin_rows, sems.at[0]), pltpu.make_async_copy(out_hbm, out_rows, sems.at[1]),
+    ]
+    stores = [
+        pltpu.make_async_copy(gin_rows, gin_ref, sems.at[2]), pltpu.make_async_copy(out_rows, out_ref, sems.at[3]),
+    ]
+    for copy in loads:
+        copy.start()
+    for copy, store in zip(loads, stores):
+        copy.wait()
+        store.start()
     wu[0:PART, :] = f_out[0].astype(F32)
     wu[PART : 2 * PART, :] = f_out[1].astype(F32)
     for h in range(2):
@@ -1484,6 +1534,8 @@
     part = jnp.sum(jnp.where(rows == s // 4, f_vec[8:12, :], 0.0), axis=0, keepdims=True)
     part = jnp.broadcast_to(part, (8, D))
     bi[...] = pltpu.roll(part, lax.rem(D - SF * (s % 4), D), 1)[0, :SF]
+    for store in stores:
+        store.wait()
 
 
 def unpack(output, grad_input, *finals):
@@ -1495,8 +1547,11 @@
             one, one, square, one, square, square, one, square, one, taps, taps, one, one,
             struct((SH, FF), F32), struct((SF,), F32), struct((SF, D), F32), one,
         ),
-        in_specs=[VMEM] * 7,
-        out_specs=(VMEM,) * 19,
+        in_specs=[ANY] * 2 + [VMEM] * 5,
+        out_specs=(ANY,) * 2 + (VMEM,) * 17,
+        scratch_shapes=[
+            pltpu.VMEM(output.shape, BF16), pltpu.VMEM(grad_input.shape, F32), pltpu.SemaphoreType.DMA((4,)),
+        ],
         compiler_params=pltpu.CompilerParams(vmem_limit_bytes=VMEM_LIMIT),
         name="unpack",
     )(output, grad_input, *finals)

time: 107 us -> 103 us (0.963)
  Pallas kernels: 105 us -> 102 us
    pallas_call x1, Pallas kernels: 101 us -> 96.4 us  [layer(): pl.pallas_call(functools.partial(layer_kernel, count), out_shape=(struct(...]
    pallas_call x1, Pallas kernels: 4.01 us -> 5.27 us  [unpack(): pl.pallas_call(unpack_kernel, out_shape=(struct(output.shape, BF16), stru...]
where the time goes in v6:
time: 103 us
  Pallas kernels  102 us (99%)
    pallas_call x1, Pallas kernels, layer(): pl.pallas_call(functools.partial(layer_kernel, count), out_shape=(struct(...  96.4 us
    pallas_call x1, Pallas kernels, unpack(): pl.pallas_call(unpack_kernel, out_shape=(struct(output.shape, BF16), stru...  5.27 us

profile of v6, /device:TPU:8, one launch (start us, length us, event | category | flops | bytes accessed | tf_op | source)
XLA Modules:
  0.0 102.5 jit_solution(2968255801573375797)
XLA Ops:
  0.7 96.4 %layer.1 = (bf16[512,768]{1,0:T(8,128)(2,1)}, f32[512,768]{1,0:T(8,128)}, bf16[2,96,768]{2,1,0:T(8,128)(2,1)}, bf16[2,48,1536]{2,1,0:T(8,128)(2,1)}, bf16[2,2,48...) custom-call(bf16[512,768]{1,0:T(8,128)(2,1)} %bitcast.4, bf16[128,768]{1,0:T(8,128)(2,1)} %bitcast.5, ...), custom_call_target="tpu_custom_call" | custom-call | tf_op jit(solution)/shard_map/layer/pallas_call | solution.py:1456
  97.1 5.3 %unpack.1 = (bf16[512,768]{1,0:T(8,128)(2,1)}, f32[512,768]{1,0:T(8,128)}, f32[48]{0:T(128)}, f32[48]{0:T(128)}, f32[48,768]{1,0:T(8,128)}, /*index=5*/f32[48]{0...) custom-call(bf16[512,768]{1,0:T(8,128)(2,1)} %get-tuple-element.45.o, ...), custom_call_target="tpu_custom_call" | custom-call | tf_op jit(solution)/shard_map/unpack/pallas_call | solution.py:1543

commit v7 on v6

--- a/solution.py
+++ b/solution.py
@@ -95,6 +95,11 @@
 def softmax_rows(scores):
     exp_scores = jnp.exp(scores - jnp.max(scores, axis=-1, keepdims=True))
     return exp_scores * (1.0 / jnp.sum(exp_scores, axis=-1, keepdims=True))
+
+
+def exp_rows(scores):
+    exp_scores = jnp.exp(scores - jnp.max(scores, axis=-1, keepdims=True))
+    return exp_scores.astype(BF16), 1.0 / jnp.sum(exp_scores, axis=-1, keepdims=True)
 
 
 def project_kernel(
@@ -651,9 +656,9 @@
             c, cv = cols(p), cols(p + PAIRS)
             qs = stack_pair(q_ref[rows, c] * jnp.asarray(HD**-0.5, BF16), low, high)
             nb, fb = nbias_ref[b], fbias_ref[b]
-            near_w = softmax_rows(dot_nt(qs, kvx_ref[near, c]) + jnp.concatenate([nb, nb], axis=0))
-            far_w = softmax_rows(dot_nt(qs, pkvx_ref[far, c]) + jnp.concatenate([fb, fb], axis=0))
-            out = dot_nn(near_w.astype(BF16), kvx_ref[near, cv]) + dot_nn(far_w.astype(BF16), pkvx_ref[far, cv])
+            near_e, near_s = exp_rows(dot_nt(qs, kvx_ref[near, c]) + jnp.concatenate([nb, nb], axis=0))
+            far_e, far_s = exp_rows(dot_nt(qs, pkvx_ref[far, c]) + jnp.concatenate([fb, fb], axis=0))
+            out = dot_nn(near_e, kvx_ref[near, cv]) * near_s + dot_nn(far_e, pkvx_ref[far, cv]) * far_s
             mix_ref[rows, c] = merge_pair(out).astype(BF16)
             return carry
 
@@ -999,7 +1004,7 @@
         mixm[:, cc] = merge_pair(mixed_pair).astype(BF16)
         return carry
 
-    lax.fori_loop(0, PAIRS, attend_rows, 0)
+    lax.fori_loop(0, PAIRS, attend_rows, 0, unroll=2)
     wait(wo_load)
     mixed = mixm[...]
     store_rows(mixt, jnp.transpose(mixed.astype(F32)).astype(BF16))
@@ -1254,24 +1259,24 @@
         return carry
 
     vec_rows_a, vec_rows_b = pl.ds(0, 16), pl.ds(16, 16)
+    for t in range(1, NZ):
+        send_act(t)
     arrive(vec_a)
     vs[0, 0:16, :] = (vecb_ref[16:32, :] + va_rx[...]).astype(BF16)
     pool_range(0, 1)
     vec_a_y = [go(vs.at[0, vec_rows_a], vy_rx.at[vec_rows_a], y_dev)]
+    pool_range(1, 2)
     wait(own_in)
     arrive(in_core + in_fwd)
     in_product(w, 0)
     in_product(w, 1)
-    pool_range(1, 2)
-    send_in(0)
-    send_in(1)
     wait(own_q)
     arrive(q_core)
     halves(dot_nn(r_all[...], g_all[...]), 1)
+    send_in(0)
+    send_in(1)
     arrive(cot_z)
     out_fwd = [go(c_all.at[slab(2 * t)], c_all.at[slab(2 * t + 1)], core_dev) for t in range(1, NZ)]
-    for t in range(1, NZ):
-        send_act(t)
     pool_range(2, 3)
     att_to_x.append(go(att.at[f, 1], att_xr.at[1], x_dev))
     pool_range(3, 5)

time: 103 us -> 101 us (0.981)
  Pallas kernels: 102 us -> 99.8 us
    pallas_call x1, Pallas kernels: 96.4 us -> 94.6 us  [layer(): pl.pallas_call(functools.partial(layer_kernel, count), out_shape=(struct(...]
where the time goes in v7:
time: 101 us
  Pallas kernels  99.8 us (99%)
    pallas_call x1, Pallas kernels, layer(): pl.pallas_call(functools.partial(layer_kernel, count), out_shape=(struct(...  94.6 us
    pallas_call x1, Pallas kernels, unpack(): pl.pallas_call(unpack_kernel, out_shape=(struct(output.shape, BF16), stru...  5.27 us

profile of v7, /device:TPU:8, one launch (start us, length us, event | category | flops | bytes accessed | tf_op | source)
XLA Modules:
  0.0 100.7 jit_solution(13129641975017372033)
XLA Ops:
  0.7 94.6 %layer.1 = (bf16[512,768]{1,0:T(8,128)(2,1)}, f32[512,768]{1,0:T(8,128)}, bf16[2,96,768]{2,1,0:T(8,128)(2,1)}, bf16[2,48,1536]{2,1,0:T(8,128)(2,1)}, bf16[2,2,48...) custom-call(bf16[512,768]{1,0:T(8,128)(2,1)} %bitcast.4, bf16[128,768]{1,0:T(8,128)(2,1)} %bitcast.5, ...), custom_call_target="tpu_custom_call" | custom-call | tf_op jit(solution)/shard_map/layer/pallas_call | solution.py:1461
  95.2 5.3 %unpack.1 = (bf16[512,768]{1,0:T(8,128)(2,1)}, f32[512,768]{1,0:T(8,128)}, f32[48]{0:T(128)}, f32[48]{0:T(128)}, f32[48,768]{1,0:T(8,128)}, /*index=5*/f32[48]{0...) custom-call(bf16[512,768]{1,0:T(8,128)(2,1)} %get-tuple-element.45.o, ...), custom_call_target="tpu_custom_call" | custom-call | tf_op jit(solution)/shard_map/unpack/pallas_call | solution.py:1548
